TPU v7x, 32 devices: a whole 2x2x4 slice. The times are simulated.
32 devices in a mesh: clus: 8 (over z, core), node: 4 (over y, x).
Axes of the slice: x: 2, y: 2, z: 4, core: 2. Of those that a mesh axis runs over, the one named last changes fastest.
Arguments:
- node_feats: bfloat16 [8, 512, 1024], P('clus', 'node'), may hold values from -6 to 6
- cotangent: bfloat16 [8, 512, 1024], P('clus', 'node'), may hold values from -6 to 6
- w_query: bfloat16 [1024, 1024], replicated, may hold values from -0.1875 to 0.1875
- w_key: bfloat16 [1024, 1024], replicated, may hold values from -0.1875 to 0.1875
- w_value: bfloat16 [1024, 1024], replicated, may hold values from -0.1875 to 0.1875
- w_out: bfloat16 [1024, 1024], replicated, may hold values from -0.1875 to 0.1875
- eigvec: bfloat16 [8, 64, 512], P('clus'), may hold values from -3.5 to 3.5
- eig_weight: float32 [16, 64], P('node'), may hold values from 0.1 to 1
- block_mask: int32 [8, 16, 4, 4], P('clus', 'node'), may hold values from 0 to 1, as said below
Outputs:
- grad_nodes: bfloat16 [8, 512, 1024], P('clus', 'node')
- grad_eigvec: float32 [8, 64, 512], P('clus', None, 'node')
- grad_weight: float32 [16, 64], P('node')
- grad_proj: float32 [4, 1024, 1024], P(None, 'clus', 'node')
Inputs may be any that keep to these rules, and one draw needn't show every extreme that they name: `block_mask`: each entry is 0 or 1; every diagonal tile is 1; the share of present tiles differs between clusters and heads.
All inputs are finite; a program needn't handle non-finite values.
Results may differ from a plain program's by a relative error of at most 0.012.
The roundings to bfloat16 on the way count: a program that leaves them out, or rounds other values in their place, can miss the bound.
Values may be sent and summed in bfloat16 or wider, within the bound.
No kernel may reach another device: no remote copies, remote signals or barrier semaphores. Data moves between devices by JAX's collectives and lax.ppermute only.
A program may use at most 128 MiB of HBM per device.

v0:
```python
import functools
import math

import jax
import jax.numpy as jnp
from jax import lax
from jax.experimental import pallas as pl
from jax.experimental.pallas import tpu as pltpu
from jax.sharding import PartitionSpec as P


BF16 = jnp.bfloat16
F32 = jnp.float32
LIMIT = pltpu.CompilerParams(vmem_limit_bytes=32 * 2**20)


def mm(a, b):
    return jnp.dot(a, b, preferred_element_type=F32)


def take(value, axis, step, size):
    if size & (size - 1) == 0:
        pairs = [(i, i ^ step) for i in range(size)]
    else:
        pairs = [((i + step) % size, i) for i in range(size)]
    return lax.ppermute(value, axis, pairs)


def give(value, axis, step, size):
    if size & (size - 1) == 0:
        return take(value, axis, step, size)
    return lax.ppermute(value, axis, [(i, (i + step) % size) for i in range(size)])


def whole(shape):
    return pl.BlockSpec(shape, lambda *_: (0,) * len(shape))


def column_blocks(weight, width):
    model = weight.shape[0]
    if width % 128 == 0:
        return weight, lambda at: pl.BlockSpec((model, width), lambda *g: (0, at(*g)))
    parts = weight.reshape(model, -1, width).transpose(1, 0, 2)
    return parts, lambda at: pl.BlockSpec((None, model, width), lambda *g: (at(*g), 0, 0))


def out_grad_kernel(count, ids_ref, rows_ref, w_ref, *out_refs):
    step = pl.program_id(0)
    value = mm(rows_ref[...], w_ref[...]).astype(BF16)
    for s in range(count):

        @pl.when(step == s)
        def _(s=s):
            out_refs[s][...] = value


def attention_kernel(scale, heads, head_size, blocks, ids_ref, mask_ref, *refs):
    row_refs, d_refs = refs[:blocks], refs[blocks : 2 * blocks]
    refs = refs[2 * blocks :]
    wq_ref, wk_ref, wv_ref, eig_ref, lam_ref, lam_t_ref = refs[:6]
    grads_ref, eig_out, gw_ref = refs[6:9]
    ret_refs = refs[9 : 9 + blocks]
    (kw, qe, qn, kt, vn, vt, dn, dt, eig_t, acc_k, acc_v, eig_acc) = refs[9 + blocks :]
    head, block = pl.program_id(0), pl.program_id(1)
    last_head, last_block = pl.num_programs(0) - 1, pl.num_programs(1) - 1
    eig_count, nodes = eig_ref.shape
    width = heads * head_size
    size = nodes // blocks
    cols = qe.shape[3]
    tile_count = mask_ref.shape[1]
    tile = nodes // tile_count
    per = tile_count // blocks

    @pl.when((head == 0) & (block == 0))
    def _():
        parts = []
        for s in range(blocks):
            at = pl.multiple_of(ids_ref[s] * size, size)
            parts.append(eig_ref[:, pl.ds(at, size)])
        eig = jnp.concatenate(parts, axis=1)
        turned = eig.T
        eig_t[...] = turned
        rows = jnp.concatenate([r[...] for r in row_refs], axis=0)
        query = mm(rows, wq_ref[...]).astype(BF16)
        query_t = (query.astype(F32) * scale).astype(BF16).T
        keys = mm(rows, wk_ref[...]).astype(BF16)
        keys_t = keys.T
        values = mm(rows, wv_ref[...]).astype(BF16)
        values_t = values.T
        d_att = jnp.concatenate([r[...] for r in d_refs], axis=0)
        d_att_t = d_att.T
        for h in range(heads):
            part = slice(h * head_size, (h + 1) * head_size)
            weighted_t = (turned.astype(F32) * lam_ref[h : h + 1, :]).astype(BF16)
            kw[h] = jnp.concatenate([keys[:, part], weighted_t], axis=1)
            qn[h] = jnp.concatenate([query[:, part], turned], axis=1)
            kt[h] = jnp.concatenate([keys_t[part], eig], axis=0)
            vn[h] = values[:, part]
            vt[h] = values_t[part]
            dn[h] = d_att[:, part]
            for b in range(nodes // cols):
                here = slice(b * cols, (b + 1) * cols)
                qe[h, b] = jnp.concatenate([query_t[part, here], eig[:, here]], axis=0)
                dt[h, b] = d_att_t[part, here]
        eig_acc[...] = jnp.zeros_like(eig_acc)

    lane = lax.broadcasted_iota(jnp.int32, (eig_count, heads), 1)
    lam = jnp.sum(jnp.where(lane == head, lam_t_ref[...], 0.0), axis=1, keepdims=True)
    at = pl.multiple_of(block * cols, cols)
    here = pl.ds(at, cols)
    scores = mm(kw[head], qe[head, block])
    tiles_here = cols // tile
    columns = []
    for i in range(tiles_here):
        i_tile = block * tiles_here + i
        i_at = ids_ref[i_tile // per] * per + i_tile % per
        rows = []
        for j in range(tile_count):
            j_at = ids_ref[j // per] * per + j % per
            part = scores[j * tile : (j + 1) * tile, i * tile : (i + 1) * tile]
            rows.append(jnp.where(mask_ref[head, i_at, j_at] > 0, part, -jnp.inf))
        columns.append(jnp.concatenate(rows, axis=0))
    masked = jnp.concatenate(columns, axis=1)
    top = jnp.max(masked, axis=0, keepdims=True)
    raised = jnp.exp(masked - top)
    total = jnp.sum(raised, axis=0, keepdims=True)
    prob = raised * (1.0 / total)
    half = prob.astype(BF16)
    first = pl.multiple_of(head * head_size, head_size)
    grads_ref[pl.ds(3 * width + first, head_size), here] = mm(vt[head], half).astype(BF16)
    dprob = mm(vn[head], dt[head, block])
    delta = jnp.sum(prob * dprob, axis=0, keepdims=True)
    dscore = (prob * (dprob - delta)).astype(BF16)
    left = mm(kt[head], dscore)
    grads_ref[pl.ds(first, head_size), here] = (left[:head_size] * scale).astype(BF16)
    eig_acc[:, here] += lam * left[head_size:]
    right = mm(dscore, qn[head, here, :])
    value = mm(half, dn[head, here, :])

    @pl.when(block == 0)
    def _():
        acc_k[...] = right
        acc_v[...] = value

    @pl.when(block > 0)
    def _():
        acc_k[...] += right
        acc_v[...] += value

    @pl.when(block == last_block)
    def _():
        full = acc_k[...]
        flat = full.T
        grads_ref[pl.ds(width + first, head_size), :] = (flat[:head_size] * scale).astype(BF16)
        eig_acc[...] += lam * flat[head_size:]
        gw_ref[pl.ds(head, 1), :] = jnp.sum(
            eig_t[...].astype(F32) * full[:, head_size:], axis=0, keepdims=True
        )
        grads_ref[pl.ds(2 * width + first, head_size), :] = acc_v[...].T.astype(BF16)

    @pl.when((block == last_block) & (head == last_head))
    def _():
        eig_out[...] = eig_acc[:, :size]
        for b in range(blocks):
            part = slice(b * size, (b + 1) * size)
            ret_refs[b][: 3 * width] = grads_ref[: 3 * width, part]
            ret_refs[b][3 * width :] = eig_acc[:, part].astype(BF16)


def terms_kernel(base, nodes_blocks, target, ids_ref, *refs):
    row_refs, cot_refs = refs[:nodes_blocks], refs[nodes_blocks : 2 * nodes_blocks]
    grads_ref, out_ref = refs[2 * nodes_blocks :]
    count, _, width, _ = out_ref.shape

    def columns(ref, index):
        if target % 128 == 0:
            return ref[:, pl.ds(pl.multiple_of(index * target, target), target)]
        fit = 128 // target
        both = ref[:, pl.ds(pl.multiple_of(index // fit * 128, 128), 128)]
        found = both[:, :target]
        for part in range(1, fit):
            here = both[:, part * target : (part + 1) * target]
            found = jnp.where(index % fit == part, here, found)
        return found

    def right_of(pieces, at):
        return jnp.concatenate(
            [jnp.concatenate([columns(ref, a) for ref in pieces], axis=0) for a in at], axis=1
        )

    group = 2 if count % 2 == 0 else 1
    for start in range(0, count, group):
        at = [ids_ref[base + start + i] for i in range(group)]
        first = mm(grads_ref[: 3 * width], right_of(row_refs, at)).astype(BF16)
        second = mm(grads_ref[3 * width :], right_of(cot_refs, at)).astype(BF16)
        for i in range(group):
            lanes = slice(i * target, (i + 1) * target)
            for a in range(3):
                out_ref[start + i, a] = first[a * width : (a + 1) * width, lanes]
            out_ref[start + i, 3] = second[:, lanes]


def pair_kernel(count, keep_ref, got_ref, gw_ref, gw_got_ref, own_ref, gw_out, *piece_refs):
    _, terms, width, target = keep_ref.shape
    sums = gw_ref[...] + gw_got_ref[...]
    high = sums.astype(BF16)
    low = (sums - high.astype(F32)).astype(BF16)
    rows, lanes = sums.shape
    base = terms * width
    gw_out[...] = sums
    own_ref[...] = keep_ref[0].astype(F32) + got_ref[0].astype(F32)
    for s in range(1, count):
        ref = piece_refs[s - 1]
        total = keep_ref[s].astype(F32) + got_ref[s].astype(F32)
        for a in range(terms):
            ref[a * width : (a + 1) * width] = total[a].astype(BF16)
        ref[base:] = jnp.zeros((ref.shape[0] - base, target), BF16)
        ref[base : base + rows, :lanes] = high
        ref[base + 8 : base + 8 + rows, :lanes] = low


def final_kernel(count, own_ref, gw_ref, *refs):
    piece_refs = refs[: count - 1]
    out_ref, gw_out = refs[count - 1 :]
    terms, width, _ = own_ref.shape
    for a in range(terms):
        total = own_ref[a]
        for r in piece_refs:
            total += r[a * width : (a + 1) * width].astype(F32)
        out_ref[a] = total.T
    sums = gw_ref[...]
    rows, lanes = sums.shape
    base = terms * width
    for r in piece_refs:
        sums += r[base : base + rows, :lanes].astype(F32)
        sums += r[base + 8 : base + 8 + rows, :lanes].astype(F32)
    gw_out[...] = sums


def nodes_kernel(blocks, width, ids_ref, eig_ref, *refs):
    ret_refs = refs[:blocks]
    w_refs = refs[blocks : blocks + 3]
    out_ref, eig_out, joined = refs[blocks + 3 :]

    @pl.when(pl.program_id(0) == 0)
    def _():
        total = eig_ref[...]
        for s in range(blocks):
            at = pl.multiple_of(ids_ref[s] * width, width)
            for a in range(3):
                joined[a, pl.ds(at, width)] = ret_refs[s][a * width : (a + 1) * width]
            if s > 0:
                total += ret_refs[s][3 * width :].astype(F32)
        eig_out[...] = total

    total = mm(w_refs[0][...], joined[0])
    total += mm(w_refs[1][...], joined[1])
    total += mm(w_refs[2][...], joined[2])
    out_ref[...] = total.T.astype(BF16)


def body(node_feats, cotangent, w_query, w_key, w_value, w_out, eigvec, eig_weight, block_mask):
    node_size = lax.axis_size("node")
    clus_size = lax.axis_size("clus")
    node_me = lax.axis_index("node")
    clus_me = lax.axis_index("clus")
    own_rows, own_cot = node_feats[0], cotangent[0]
    size, model = own_rows.shape
    heads, eig_count = eig_weight.shape
    nodes = size * node_size
    width = model // node_size
    head_size = width // heads
    scale = head_size ** (-0.5)
    assert math.frexp(scale)[0] == 0.5
    assert clus_size & (clus_size - 1) == 0
    block = nodes
    while block * nodes > 512 * 512 and block > 128:
        block //= 2
    far_first = [s for s in range(node_size - 1, 0, -1)]

    rest = clus_size // 2
    order = jnp.arange(node_size, dtype=jnp.int32)
    order = order ^ node_me if node_size & (node_size - 1) == 0 else (order + node_me) % node_size
    slots = jnp.arange(clus_size, dtype=jnp.int32)
    slots = (2 * (slots % rest) + jnp.where(slots < rest, 1, 0)) ^ clus_me
    ids = jnp.concatenate([order, slots])

    rows = [own_rows] + [None] * (node_size - 1)
    for s in far_first:
        rows[s] = take(own_rows, "node", s, node_size)

    weight, spec = column_blocks(w_out, width)
    d_parts = pl.pallas_call(
        functools.partial(out_grad_kernel, node_size),
        grid_spec=pltpu.PrefetchScalarGridSpec(
            num_scalar_prefetch=1,
            grid=(node_size,),
            in_specs=[whole((size, model)), spec(lambda s, ids: ids[s])],
            out_specs=[whole((size, width))] * node_size,
        ),
        out_shape=[jax.ShapeDtypeStruct((size, width), BF16)] * node_size,
        cost_estimate=pl.CostEstimate(flops=3 * 10**8, bytes_accessed=3 * 2**20, transcendentals=0),
        compiler_params=LIMIT,
        name="out_grad",
    )(ids, own_cot, weight)
    d_att = [d_parts[0]] + [None] * (node_size - 1)
    for s in far_first:
        d_att[s] = give(d_parts[s], "node", s, node_size)
    cots = [own_cot] + [None] * (node_size - 1)
    for s in far_first:
        cots[s] = take(own_cot, "node", s, node_size)

    steps = nodes // block
    both = head_size + eig_count
    weights = [column_blocks(w, width) for w in (w_query, w_key, w_value)]
    results = pl.pallas_call(
        functools.partial(attention_kernel, scale, heads, head_size, node_size),
        grid_spec=pltpu.PrefetchScalarGridSpec(
            num_scalar_prefetch=2,
            grid=(heads, steps),
            in_specs=[whole((size, model))] * node_size
            + [whole((size, width))] * node_size
            + [w[1](lambda h, b, ids, mask: ids[0]) for w in weights]
            + [
                whole((eig_count, nodes)),
                whole((heads, eig_count)),
                whole((eig_count, heads)),
            ],
            out_specs=[
                whole((4 * width, nodes)),
                whole((eig_count, size)),
                whole((heads, eig_count)),
            ]
            + [whole((3 * width + eig_count, size))] * node_size,
            scratch_shapes=[
                pltpu.VMEM((heads, nodes, both), BF16),
                pltpu.VMEM((heads, steps, both, block), BF16),
                pltpu.VMEM((heads, nodes, both), BF16),
                pltpu.VMEM((heads, both, nodes), BF16),
                pltpu.VMEM((heads, nodes, head_size), BF16),
                pltpu.VMEM((heads, head_size, nodes), BF16),
                pltpu.VMEM((heads, nodes, head_size), BF16),
                pltpu.VMEM((heads, steps, head_size, block), BF16),
                pltpu.VMEM((nodes, eig_count), BF16),
                pltpu.VMEM((nodes, both), F32),
                pltpu.VMEM((nodes, head_size), F32),
                pltpu.VMEM((eig_count, nodes), F32),
            ],
        ),
        out_shape=[
            jax.ShapeDtypeStruct((4 * width, nodes), BF16),
            jax.ShapeDtypeStruct((eig_count, size), F32),
            jax.ShapeDtypeStruct((heads, eig_count), F32),
        ]
        + [jax.ShapeDtypeStruct((3 * width + eig_count, size), BF16)] * node_size,
        cost_estimate=pl.CostEstimate(
            flops=8 * 10**9, bytes_accessed=8 * 2**20, transcendentals=10**6
        ),
        compiler_params=LIMIT,
        name="attention",
    )(
        ids,
        block_mask[0],
        *rows,
        *d_att,
        *[w[0] for w in weights],
        eigvec[0],
        eig_weight,
        eig_weight.T,
    )
    grads_t, eig_own, gw_own = results[:3]
    parts = results[3:]

    target = model // clus_size
    smem, vmem = pl.BlockSpec(memory_space=pltpu.SMEM), pl.BlockSpec(memory_space=pltpu.VMEM)

    def terms(base):
        return pl.pallas_call(
            functools.partial(terms_kernel, node_size + base, node_size, target),
            in_specs=[smem] + [vmem] * (2 * node_size + 1),
            out_specs=vmem,
            out_shape=jax.ShapeDtypeStruct((rest, 4, width, target), BF16),
            cost_estimate=pl.CostEstimate(
                flops=2 * 10**9, bytes_accessed=2 * 2**20, transcendentals=0
            ),
            compiler_params=LIMIT,
        )(ids, *rows, *cots, grads_t)

    give_half = terms(0)
    gw_got = give(gw_own, "clus", 1, clus_size)
    got_half = give(give_half, "clus", 1, clus_size)
    keep_half = terms(rest)

    piece_rows = 4 * width + 16
    paired = pl.pallas_call(
        functools.partial(pair_kernel, rest),
        in_specs=[vmem] * 4,
        out_specs=[vmem] * (rest + 1),
        out_shape=[
            jax.ShapeDtypeStruct((4, width, target), F32),
            jax.ShapeDtypeStruct(eig_weight.shape, F32),
        ]
        + [jax.ShapeDtypeStruct((piece_rows, target), BF16)] * (rest - 1),
        cost_estimate=pl.CostEstimate(flops=10**6, bytes_accessed=4 * 2**20, transcendentals=0),
        compiler_params=LIMIT,
        name="pair",
    )(keep_half, got_half, gw_own, gw_got)
    own_sum, gw_pair = paired[:2]
    pieces = [None] * (rest - 1)
    for s in range(rest - 1, 0, -1):
        pieces[s - 1] = give(paired[1 + s], "clus", 2 * s, clus_size)

    returned = [parts[0]] + [None] * (node_size - 1)
    for s in far_first:
        returned[s] = give(parts[s], "node", s, node_size)

    chunk = min(256, model)
    grad_rows, grad_eig = pl.pallas_call(
        functools.partial(nodes_kernel, node_size, width),
        grid_spec=pltpu.PrefetchScalarGridSpec(
            num_scalar_prefetch=1,
            grid=(model // chunk,),
            in_specs=[whole((eig_count, size))]
            + [whole((3 * width + eig_count, size))] * node_size
            + [pl.BlockSpec((chunk, model), lambda g, *_: (g, 0))] * 3,
            out_specs=[
                pl.BlockSpec((size, chunk), lambda g, *_: (0, g)),
                whole((eig_count, size)),
            ],
            scratch_shapes=[pltpu.VMEM((3, model, size), BF16)],
        ),
        out_shape=[
            jax.ShapeDtypeStruct((size, model), BF16),
            jax.ShapeDtypeStruct((eig_count, size), F32),
        ],
        cost_estimate=pl.CostEstimate(flops=10**9, bytes_accessed=7 * 2**20, transcendentals=0),
        compiler_params=LIMIT,
        name="nodes",
    )(ids, eig_own, *returned, w_query, w_key, w_value)

    grad_proj, grad_weight = pl.pallas_call(
        functools.partial(final_kernel, rest),
        in_specs=[vmem] * (rest + 1),
        out_specs=[vmem] * 2,
        out_shape=[
            jax.ShapeDtypeStruct((4, target, width), F32),
            jax.ShapeDtypeStruct(eig_weight.shape, F32),
        ],
        cost_estimate=pl.CostEstimate(flops=10**6, bytes_accessed=2 * 2**20, transcendentals=0),
        compiler_params=LIMIT,
        name="final",
    )(own_sum, gw_pair, *pieces)
    return (grad_rows[None], grad_eig[None], grad_weight, grad_proj)


def solution(mesh):
    placed = (
        P("clus", "node", None),
        P("clus", "node", None),
        P(),
        P(),
        P(),
        P(),
        P("clus", None, None),
        P("node", None),
        P("clus", "node", None, None),
    )
    return jax.shard_map(
        body,
        mesh=mesh,
        in_specs=placed,
        out_specs=(
            P("clus", "node", None),
            P("clus", None, "node"),
            P("node", None),
            P(None, "clus", "node"),
        ),
        check_vma=False,
    )
```

profile of v0, /device:TPU:20, one launch (start us, length us, event | category | flops | bytes accessed | tf_op | source)
XLA Modules:
  0.0 73.8 jit_solution(12471239511167753921)
XLA Ops:
  0.6 0.0 copy-start
  0.6 1.6 %collective-permute-start = (bf16[128,1024]{1,0:T(8,128)(2,1)}, bf16[128,1024]{1,0:T(8,128)(2,1)S(1)}, u32[]{:S(2)}, u32[]{:S(2)}) collective-permute-start(bf16[128,1024]{1,0:T(8,128)(2,1)} %bitcast.14), channel_id=1, source_target_pairs={{0,1},{1,0},{2,3},{3,2},{4,5},{5,4},{6,7},{7,6},{8,9},{9,8},{10,11... | collective-permute-start | bytes 786440 | tf_op jit(solution)/shard_map/ppermute | solution.py:26
  2.2 0.5 collective-permute-start.1
  2.7 1.5 %collective-permute-start.2 = (bf16[128,1024]{1,0:T(8,128)(2,1)}, bf16[128,1024]{1,0:T(8,128)(2,1)S(1)}, u32[]{:S(2)}, u32[]{:S(2)}) collective-permute-start(bf16[128,1024]{1,0:T(8,128)(2,1)} %bitcast.16), channel_id=1, source_target_pairs={{0,3},{1,2},{2,1},{3,0},{4,7},{5,6},{6,5},{7,4},{8,11},{9,10},{10,... | collective-permute-start | bytes 786440 | tf_op jit(solution)/shard_map/ppermute | solution.py:26
  4.2 0.1 pad_add_fusion.ids_ref
  4.3 0.0 copy-start.5
  4.3 1.6 %copy-done.5 = bf16[1024,1024]{1,0:T(8,128)(2,1)S(1)} copy-done((bf16[1024,1024]{1,0:T(8,128)(2,1)S(1)}, bf16[1024,1024]{1,0:T(8,128)(2,1)}, u32[]{:S(2)}) %copy-start.5) | copy-done | bytes 2097176
  5.9 0.0 copy-start.6
  5.9 0.9 %copy-done.6 = bf16[1,128,1024]{2,1,0:T(8,128)(2,1)S(1)} copy-done((bf16[1,128,1024]{2,1,0:T(8,128)(2,1)S(1)}, bf16[1,128,1024]{2,1,0:T(8,128)(2,1)}, u32[]{:S(2)}) %copy-start.6) | copy-done | bytes 262168
  6.8 0.0 copy-start.8
  6.8 0.0 copy-start.7
  6.8 0.0 copy-start.10
  6.8 2.5 %out_grad.1 = (bf16[128,256]{1,0:T(8,128)(2,1)S(1)}, bf16[128,256]{1,0:T(8,128)(2,1)S(1)}, bf16[128,256]{1,0:T(8,128)(2,1)}, bf16[128,256]{1,0:T(8,128)(2,1)}) custom-call(s32[12]{0:T(128)S(1)} %pad_add_fusion.ids_ref, bf16[128,1024]{1,0:T(8,128)(2,1)S(1)} %bitcast.7, bf16[1024,1024]{1,0:T(8,128)(2,1)S(1)} %copy-done.5), custom_call_target="tpu_custom_call" | custom-call | flops 300000000 | bytes 3145728 | tf_op jit(solution)/shard_map/out_grad/pallas_call | solution.py:293
  9.4 1.5 %collective-permute-start.3 = (bf16[128,256]{1,0:T(8,128)(2,1)S(1)}, bf16[128,256]{1,0:T(8,128)(2,1)S(1)}, u32[]{:S(2)}, u32[]{:S(2)}) collective-permute-start(bf16[128,256]{1,0:T(8,128)(2,1)S(1)} %get-tuple-element.25), channel_id=1, source_target_pairs={{0,1},{1,0},{2,3},{3,2},{4,5},{5,4},{6,7},{7,6},{8,9},{9,8},{10,11... | collective-permute-start | bytes 196616 | tf_op jit(solution)/shard_map/ppermute | solution.py:26
  10.8 0.5 collective-permute-start.4
  11.4 4.7 %collective-permute-done.3.refs_5_ = bf16[128,256]{1,0:T(8,128)(2,1)S(1)} collective-permute-done((bf16[128,256]{1,0:T(8,128)(2,1)S(1)}, bf16[128,256]{1,0:T(8,128)(2,1)S(1)}, u32[]{:S(2)}, u32[]{:S(2)}) %collective-permute-start.3) | collective-permute-done | bytes 65568 | tf_op jit(solution)/shard_map/ppermute | solution.py:26
  16.0 1.4 %collective-permute-start.5 = (bf16[128,256]{1,0:T(8,128)(2,1)}, bf16[128,256]{1,0:T(8,128)(2,1)S(1)}, u32[]{:S(2)}, u32[]{:S(2)}) collective-permute-start(bf16[128,256]{1,0:T(8,128)(2,1)} %get-tuple-element.27), channel_id=1, source_target_pairs={{0,3},{1,2},{2,1},{3,0},{4,7},{5,6},{6,5},{7,4},{8,11},{9,10},{10,... | collective-permute-start | bytes 196616 | tf_op jit(solution)/shard_map/ppermute | solution.py:26
  17.5 0.0 copy-done.8
  17.5 0.1 copy.13
  17.6 0.0 collective-permute-done.4.refs_6_
  17.6 0.0 copy-done.7
  17.6 0.6 collective-permute-start.9
  18.2 3.9 %collective-permute-done.5.refs_7_ = bf16[128,256]{1,0:T(8,128)(2,1)S(1)} collective-permute-done((bf16[128,256]{1,0:T(8,128)(2,1)}, bf16[128,256]{1,0:T(8,128)(2,1)S(1)}, u32[]{:S(2)}, u32[]{:S(2)}) %collective-permute-start.5) | collective-permute-done | bytes 65568 | tf_op jit(solution)/shard_map/ppermute | solution.py:26
  22.1 0.5 collective-permute-start.10
  22.6 0.0 collective-permute-done.refs_1_
  22.6 2.4 %collective-permute-start.11 = (bf16[128,1024]{1,0:T(8,128)(2,1)S(1)}, bf16[128,1024]{1,0:T(8,128)(2,1)S(1)}, u32[]{:S(2)}, u32[]{:S(2)}) collective-permute-start(bf16[128,1024]{1,0:T(8,128)(2,1)S(1)} %bitcast.10), channel_id=1, source_target_pairs={{0,3},{1,2},{2,1},{3,0},{4,7},{5,6},{6,5},{7,4},{8,11},{9,10},{10,... | collective-permute-start | bytes 786440 | tf_op jit(solution)/shard_map/ppermute | solution.py:26
  25.1 0.0 collective-permute-done.1.refs_2_
  25.1 0.0 collective-permute-done.2.refs_3_
  25.1 0.0 copy-done
  25.1 0.0 copy-done.10
  25.1 0.0 copy-start.1
  25.1 1.6 %copy-done.1 = bf16[1024,1024]{1,0:T(8,128)(2,1)S(1)} copy-done((bf16[1024,1024]{1,0:T(8,128)(2,1)S(1)}, bf16[1024,1024]{1,0:T(8,128)(2,1)}, u32[]{:S(2)}) %copy-start.1) | copy-done | bytes 2097176
  26.7 0.0 copy-start.3
  26.7 1.6 %copy-done.3 = bf16[1024,1024]{1,0:T(8,128)(2,1)S(1)} copy-done((bf16[1024,1024]{1,0:T(8,128)(2,1)S(1)}, bf16[1024,1024]{1,0:T(8,128)(2,1)}, u32[]{:S(2)}) %copy-start.3) | copy-done | bytes 2097176
  28.3 0.9 %copy-done.9 = bf16[1,128,1024]{2,1,0:T(8,128)(2,1)S(1)} copy-done((bf16[1,128,1024]{2,1,0:T(8,128)(2,1)S(1)}, bf16[1,128,1024]{2,1,0:T(8,128)(2,1)}, u32[]{:S(2)}) %copy-start.9) | copy-done | bytes 262168
  29.2 0.7 copy-done.11
  29.9 9.0 %attention.1 = (bf16[1024,512]{1,0:T(8,128)(2,1)S(1)}, f32[64,128]{1,0:T(8,128)S(1)}, f32[4,64]{1,0:T(4,128)S(1)}, bf16[832,128]{1,0:T(8,128)(2,1)S(1)}, bf16[83...) custom-call(s32[12]{0:T(128)S(1)} %pad_add_fusion.ids_ref, ...), custom_call_target="tpu_custom_call" | custom-call | flops 8000000000 | bytes 8388608 | tf_op jit(solution)/shard_map/attention/pallas_call | solution.py:316
  38.9 0.0 collective-permute-done.9.refs_5_
  39.0 0.0 collective-permute-done.10.refs_6_
  39.0 0.0 collective-permute-done.11.refs_7_
  39.0 1.3 %shard_map.121 = bf16[4,4,256,128]{3,2,1,0:T(8,128)(2,1)S(1)} custom-call(s32[12]{0:T(128)S(1)} %pad_add_fusion.ids_ref, bf16[128,1024]{1,0:T(8,128)(2,1)S(1)} %bitcast.18, bf16[128,1024]{1,0:T(8,128)(2,1)S(1)} %collective-permute-done.refs_1_, bf16[128,1024]{1,0:T(8,128)(2,1)S(1)} %collective-permute-done.1.refs_2_, ...), custom_call_target="tpu_custom_call" | custom-call | flops 2000000000 | bytes 2097152 | tf_op jit(solution)/shard_map/pallas_call | solution.py:378
  40.3 0.1 collective-permute-start.12
  40.4 0.6 collective-permute-start.6
  41.0 0.5 collective-permute-start.7
  41.5 2.4 %collective-permute-start.8 = (bf16[832,128]{1,0:T(8,128)(2,1)S(1)}, bf16[832,128]{1,0:T(8,128)(2,1)S(1)}, u32[]{:S(2)}, u32[]{:S(2)}) collective-permute-start(bf16[832,128]{1,0:T(8,128)(2,1)S(1)} %get-tuple-element.32), channel_id=1, source_target_pairs={{0,3},{1,2},{2,1},{3,0},{4,7},{5,6},{6,5},{7,4},{8,11},{9,10},{10,... | collective-permute-start | bytes 638984 | tf_op jit(solution)/shard_map/ppermute | solution.py:26
  44.0 0.0 collective-permute-start.13
  44.0 1.3 %shard_map.120.keep_ref = bf16[4,4,256,128]{3,2,1,0:T(8,128)(2,1)S(1)} custom-call(s32[12]{0:T(128)S(1)} %pad_add_fusion.ids_ref, bf16[128,1024]{1,0:T(8,128)(2,1)S(1)} %bitcast.19, bf16[128,1024]{1,0:T(8,128)(2,1)S(1)} %collective-permute-done.refs_1_, bf16[128,1024]{1,0:T(8,128)(2,1)S(1)} %collective-permute-done.1.refs_2_, ...), custom_call_target="tpu_custom_call" | custom-call | flops 2000000000 | bytes 2097152 | tf_op jit(solution)/shard_map/pallas_call | solution.py:378
  45.3 0.0 copy-start.2
  45.3 0.0 collective-permute-done.13.gw_got_ref
  45.3 0.0 collective-permute-done.12.got_ref
  45.3 0.2 pair.1
  45.5 1.6 %collective-permute-start.14 = (bf16[1040,128]{1,0:T(8,128)(2,1)S(1)}, bf16[1040,128]{1,0:T(8,128)(2,1)S(1)}, u32[]{:S(2)}, u32[]{:S(2)}) collective-permute-start(bf16[1040,128]{1,0:T(8,128)(2,1)S(1)} %get-tuple-element.39), channel_id=1, source_target_pairs={{0,8},{4,12},{8,0},{12,4},{16,24},{20,28},{24,16},{28,20},{1,9},{5... | collective-permute-start | bytes 798728 | tf_op jit(solution)/shard_map/ppermute | solution.py:26
  47.2 0.3 collective-permute-start.15
  47.5 1.1 %collective-permute-done.6.refs_1_ = bf16[832,128]{1,0:T(8,128)(2,1)S(1)} collective-permute-done((bf16[832,128]{1,0:T(8,128)(2,1)S(1)}, bf16[832,128]{1,0:T(8,128)(2,1)S(1)}, u32[]{:S(2)}, u32[]{:S(2)}) %collective-permute-start.6) | collective-permute-done | bytes 213024 | tf_op jit(solution)/shard_map/ppermute | solution.py:26
  48.6 0.5 collective-permute-start.16
  49.1 3.8 %collective-permute-done.7.refs_2_ = bf16[832,128]{1,0:T(8,128)(2,1)S(1)} collective-permute-done((bf16[832,128]{1,0:T(8,128)(2,1)S(1)}, bf16[832,128]{1,0:T(8,128)(2,1)S(1)}, u32[]{:S(2)}, u32[]{:S(2)}) %collective-permute-start.7) | collective-permute-done | bytes 213024 | tf_op jit(solution)/shard_map/ppermute | solution.py:26
  52.9 0.0 collective-permute-done.8.refs_3_
  52.9 0.0 copy-done.4
  52.9 0.0 copy-done.2
  52.9 3.9 %nodes.1 = (bf16[128,1024]{1,0:T(8,128)(2,1)}, f32[64,128]{1,0:T(8,128)}) custom-call(s32[12]{0:T(128)S(1)} %pad_add_fusion.ids_ref, f32[64,128]{1,0:T(8,128)S(1)} %get-tuple-element.28.eig_ref, bf16[832,128]{1,0:T(8,128)(2,1)S(1)} %get-tuple-element.29.refs_0_, bf16[832,128]{1,0:T(8,128)(2,1)S(1)} %collective-permute-done.6.refs_1_, ...), custom_call_target="tpu_custom_call" | custom-call | flops 1000000000 | bytes 7340032 | tf_op jit(solution)/shard_map/nodes/pallas_call | solution.py:418
  56.8 1.2 %collective-permute-done.14.refs_0_ = bf16[1040,128]{1,0:T(8,128)(2,1)S(1)} collective-permute-done((bf16[1040,128]{1,0:T(8,128)(2,1)S(1)}, bf16[1040,128]{1,0:T(8,128)(2,1)S(1)}, u32[]{:S(2)}, u32[]{:S(2)}) %collective-permute-start.14) | collective-permute-done | bytes 266272 | tf_op jit(solution)/shard_map/ppermute | solution.py:26
  58.0 7.8 %collective-permute-done.15.refs_1_ = bf16[1040,128]{1,0:T(8,128)(2,1)S(1)} collective-permute-done((bf16[1040,128]{1,0:T(8,128)(2,1)S(1)}, bf16[1040,128]{1,0:T(8,128)(2,1)S(1)}, u32[]{:S(2)}, u32[]{:S(2)}) %collective-permute-start.15) | collective-permute-done | bytes 266272 | tf_op jit(solution)/shard_map/ppermute | solution.py:26
  65.8 7.0 %collective-permute-done.16.refs_2_ = bf16[1040,128]{1,0:T(8,128)(2,1)S(1)} collective-permute-done((bf16[1040,128]{1,0:T(8,128)(2,1)S(1)}, bf16[1040,128]{1,0:T(8,128)(2,1)S(1)}, u32[]{:S(2)}, u32[]{:S(2)}) %collective-permute-start.16) | collective-permute-done | bytes 266272 | tf_op jit(solution)/shard_map/ppermute | solution.py:26
  72.8 1.0 %final.1 = (f32[4,128,256]{2,1,0:T(8,128)}, f32[4,64]{1,0:T(4,128)}) custom-call(f32[4,256,128]{2,1,0:T(8,128)S(1)} %get-tuple-element.37.own_ref, f32[4,64]{1,0:T(4,128)S(1)} %get-tuple-element.38.gw_ref, bf16[1040,128]{1,0:T(8,128)(2,1)S(1)} %collective-permute-done.14.refs_0_, bf16[1040,128]{1,0:T(8,128)(2,1)S(1)} %collective-permute-done.15.refs_1_, ...), custom_call_target="tpu_custom_call" | custom-call | flops 1000000 | bytes 2097152 | tf_op jit(solution)/shard_map/final/pallas_call | solution.py:441
  (5 shorter events, 0.0 us)
Async XLA Ops:
  0.6 24.4 %copy-start = (bf16[1024,1024]{1,0:T(8,128)(2,1)S(1)}, bf16[1024,1024]{1,0:T(8,128)(2,1)}, u32[]{:S(2)}) copy-start(bf16[1024,1024]{1,0:T(8,128)(2,1)} %refs_4_.1) | copy-start | bytes 6291460
  0.6 22.0 %collective-permute-start = (bf16[128,1024]{1,0:T(8,128)(2,1)}, bf16[128,1024]{1,0:T(8,128)(2,1)S(1)}, u32[]{:S(2)}, u32[]{:S(2)}) collective-permute-start(bf16[128,1024]{1,0:T(8,128)(2,1)} %bitcast.14), channel_id=1, source_target_pairs={{0,1},{1,0},{2,3},{3,2},{4,5},{5,4},{6,7},{7,6},{8,9},{9,8},{10,11... | collective-permute-start | bytes 786440 | tf_op jit(solution)/shard_map/ppermute | solution.py:26
  2.2 22.9 %collective-permute-start.1 = (bf16[128,1024]{1,0:T(8,128)(2,1)}, bf16[128,1024]{1,0:T(8,128)(2,1)S(1)}, u32[]{:S(2)}, u32[]{:S(2)}) collective-permute-start(bf16[128,1024]{1,0:T(8,128)(2,1)} %bitcast.15), channel_id=1, source_target_pairs={{0,2},{1,3},{2,0},{3,1},{4,6},{5,7},{6,4},{7,5},{8,10},{9,11},{10,... | collective-permute-start | bytes 786440 | tf_op jit(solution)/shard_map/ppermute | solution.py:26
  2.7 22.4 %collective-permute-start.2 = (bf16[128,1024]{1,0:T(8,128)(2,1)}, bf16[128,1024]{1,0:T(8,128)(2,1)S(1)}, u32[]{:S(2)}, u32[]{:S(2)}) collective-permute-start(bf16[128,1024]{1,0:T(8,128)(2,1)} %bitcast.16), channel_id=1, source_target_pairs={{0,3},{1,2},{2,1},{3,0},{4,7},{5,6},{6,5},{7,4},{8,11},{9,10},{10,... | collective-permute-start | bytes 786440 | tf_op jit(solution)/shard_map/ppermute | solution.py:26
  4.3 1.6 %copy-start.5 = (bf16[1024,1024]{1,0:T(8,128)(2,1)S(1)}, bf16[1024,1024]{1,0:T(8,128)(2,1)}, u32[]{:S(2)}) copy-start(bf16[1024,1024]{1,0:T(8,128)(2,1)} %w_ref.1) | copy-start | bytes 6291460
  5.9 0.9 %copy-start.6 = (bf16[1,128,1024]{2,1,0:T(8,128)(2,1)S(1)}, bf16[1,128,1024]{2,1,0:T(8,128)(2,1)}, u32[]{:S(2)}) copy-start(bf16[1,128,1024]{2,1,0:T(8,128)(2,1)} %param.10) | copy-start | bytes 786436
  6.8 10.6 %copy-start.8 = (f32[4,64]{1,0:T(4,128)S(1)}, f32[4,64]{1,0:T(4,128)}, u32[]{:S(2)}) copy-start(f32[4,64]{1,0:T(4,128)} %refs_12_.1) | copy-start | bytes 3076
  6.8 10.7 %copy-start.7 = (bf16[1,128,1024]{2,1,0:T(8,128)(2,1)S(1)}, bf16[1,128,1024]{2,1,0:T(8,128)(2,1)}, u32[]{:S(2)}) copy-start(bf16[1,128,1024]{2,1,0:T(8,128)(2,1)} %param.10) | copy-start | bytes 786436
  6.8 18.2 %copy-start.10 = (bf16[1,64,512]{2,1,0:T(8,128)(2,1)S(1)}, bf16[1,64,512]{2,1,0:T(8,128)(2,1)}, u32[]{:S(2)}) copy-start(bf16[1,64,512]{2,1,0:T(8,128)(2,1)} %param.15) | copy-start | bytes 196612
  9.4 6.7 %collective-permute-start.3 = (bf16[128,256]{1,0:T(8,128)(2,1)S(1)}, bf16[128,256]{1,0:T(8,128)(2,1)S(1)}, u32[]{:S(2)}, u32[]{:S(2)}) collective-permute-start(bf16[128,256]{1,0:T(8,128)(2,1)S(1)} %get-tuple-element.25), channel_id=1, source_target_pairs={{0,1},{1,0},{2,3},{3,2},{4,5},{5,4},{6,7},{7,6},{8,9},{9,8},{10,11... | collective-permute-start | bytes 196616 | tf_op jit(solution)/shard_map/ppermute | solution.py:26
  10.8 6.7 %collective-permute-start.4 = (bf16[128,256]{1,0:T(8,128)(2,1)}, bf16[128,256]{1,0:T(8,128)(2,1)S(1)}, u32[]{:S(2)}, u32[]{:S(2)}) collective-permute-start(bf16[128,256]{1,0:T(8,128)(2,1)} %get-tuple-element.26), channel_id=1, source_target_pairs={{0,2},{1,3},{2,0},{3,1},{4,6},{5,7},{6,4},{7,5},{8,10},{9,11},{10,... | collective-permute-start | bytes 196616 | tf_op jit(solution)/shard_map/ppermute | solution.py:26
  16.0 6.1 %collective-permute-start.5 = (bf16[128,256]{1,0:T(8,128)(2,1)}, bf16[128,256]{1,0:T(8,128)(2,1)S(1)}, u32[]{:S(2)}, u32[]{:S(2)}) collective-permute-start(bf16[128,256]{1,0:T(8,128)(2,1)} %get-tuple-element.27), channel_id=1, source_target_pairs={{0,3},{1,2},{2,1},{3,0},{4,7},{5,6},{6,5},{7,4},{8,11},{9,10},{10,... | collective-permute-start | bytes 196616 | tf_op jit(solution)/shard_map/ppermute | solution.py:26
  17.6 21.4 %collective-permute-start.9 = (bf16[128,1024]{1,0:T(8,128)(2,1)S(1)}, bf16[128,1024]{1,0:T(8,128)(2,1)S(1)}, u32[]{:S(2)}, u32[]{:S(2)}) collective-permute-start(bf16[128,1024]{1,0:T(8,128)(2,1)S(1)} %bitcast.8), channel_id=1, source_target_pairs={{0,1},{1,0},{2,3},{3,2},{4,5},{5,4},{6,7},{7,6},{8,9},{9,8},{10,11... | collective-permute-start | bytes 786440 | tf_op jit(solution)/shard_map/ppermute | solution.py:26
  22.1 16.9 %collective-permute-start.10 = (bf16[128,1024]{1,0:T(8,128)(2,1)S(1)}, bf16[128,1024]{1,0:T(8,128)(2,1)S(1)}, u32[]{:S(2)}, u32[]{:S(2)}) collective-permute-start(bf16[128,1024]{1,0:T(8,128)(2,1)S(1)} %bitcast.9), channel_id=1, source_target_pairs={{0,2},{1,3},{2,0},{3,1},{4,6},{5,7},{6,4},{7,5},{8,10},{9,11},{10,... | collective-permute-start | bytes 786440 | tf_op jit(solution)/shard_map/ppermute | solution.py:26
  22.6 16.4 %collective-permute-start.11 = (bf16[128,1024]{1,0:T(8,128)(2,1)S(1)}, bf16[128,1024]{1,0:T(8,128)(2,1)S(1)}, u32[]{:S(2)}, u32[]{:S(2)}) collective-permute-start(bf16[128,1024]{1,0:T(8,128)(2,1)S(1)} %bitcast.10), channel_id=1, source_target_pairs={{0,3},{1,2},{2,1},{3,0},{4,7},{5,6},{6,5},{7,4},{8,11},{9,10},{10,... | collective-permute-start | bytes 786440 | tf_op jit(solution)/shard_map/ppermute | solution.py:26
  25.1 1.6 %copy-start.1 = (bf16[1024,1024]{1,0:T(8,128)(2,1)S(1)}, bf16[1024,1024]{1,0:T(8,128)(2,1)}, u32[]{:S(2)}) copy-start(bf16[1024,1024]{1,0:T(8,128)(2,1)} %refs_5_.1) | copy-start | bytes 6291460
  26.7 1.6 %copy-start.3 = (bf16[1024,1024]{1,0:T(8,128)(2,1)S(1)}, bf16[1024,1024]{1,0:T(8,128)(2,1)}, u32[]{:S(2)}) copy-start(bf16[1024,1024]{1,0:T(8,128)(2,1)} %refs_6_.1) | copy-start | bytes 6291460
  28.3 0.9 %copy-start.9 = (bf16[1,128,1024]{2,1,0:T(8,128)(2,1)S(1)}, bf16[1,128,1024]{2,1,0:T(8,128)(2,1)}, u32[]{:S(2)}) copy-start(bf16[1,128,1024]{2,1,0:T(8,128)(2,1)} %param.9) | copy-start | bytes 786436
  29.2 0.7 copy-start.11
  40.3 5.0 %collective-permute-start.12 = (bf16[4,4,256,128]{3,2,1,0:T(8,128)(2,1)S(1)}, bf16[4,4,256,128]{3,2,1,0:T(8,128)(2,1)S(1)}, u32[]{:S(2)}, u32[]{:S(2)}) collective-permute-start(bf16[4,4,256,128]{3,2,1,0:T(8,128)(2,1)S(1)} %shard_map.121), channel_id=1, source_target_pairs={{0,4},{4,0},{8,12},{12,8},{16,20},{20,16},{24,28},{28,24},{1,5},{5... | collective-permute-start | bytes 3145736 | tf_op jit(solution)/shard_map/ppermute | solution.py:26
  40.4 8.2 %collective-permute-start.6 = (bf16[832,128]{1,0:T(8,128)(2,1)S(1)}, bf16[832,128]{1,0:T(8,128)(2,1)S(1)}, u32[]{:S(2)}, u32[]{:S(2)}) collective-permute-start(bf16[832,128]{1,0:T(8,128)(2,1)S(1)} %get-tuple-element.30), channel_id=1, source_target_pairs={{0,1},{1,0},{2,3},{3,2},{4,5},{5,4},{6,7},{7,6},{8,9},{9,8},{10,11... | collective-permute-start | bytes 638984 | tf_op jit(solution)/shard_map/ppermute | solution.py:26
  41.0 11.9 %collective-permute-start.7 = (bf16[832,128]{1,0:T(8,128)(2,1)S(1)}, bf16[832,128]{1,0:T(8,128)(2,1)S(1)}, u32[]{:S(2)}, u32[]{:S(2)}) collective-permute-start(bf16[832,128]{1,0:T(8,128)(2,1)S(1)} %get-tuple-element.31), channel_id=1, source_target_pairs={{0,2},{1,3},{2,0},{3,1},{4,6},{5,7},{6,4},{7,5},{8,10},{9,11},{10,... | collective-permute-start | bytes 638984 | tf_op jit(solution)/shard_map/ppermute | solution.py:26
  41.5 11.4 %collective-permute-start.8 = (bf16[832,128]{1,0:T(8,128)(2,1)S(1)}, bf16[832,128]{1,0:T(8,128)(2,1)S(1)}, u32[]{:S(2)}, u32[]{:S(2)}) collective-permute-start(bf16[832,128]{1,0:T(8,128)(2,1)S(1)} %get-tuple-element.32), channel_id=1, source_target_pairs={{0,3},{1,2},{2,1},{3,0},{4,7},{5,6},{6,5},{7,4},{8,11},{9,10},{10,... | collective-permute-start | bytes 638984 | tf_op jit(solution)/shard_map/ppermute | solution.py:26
  44.0 1.3 %collective-permute-start.13 = (f32[4,64]{1,0:T(4,128)S(1)}, f32[4,64]{1,0:T(4,128)S(1)}, u32[]{:S(2)}, u32[]{:S(2)}) collective-permute-start(f32[4,64]{1,0:T(4,128)S(1)} %get-tuple-element.36.gw_ref), channel_id=1, source_target_pairs={{0,4},{4,0},{8,12},{12,8},{16,20},{20,16},{24,28},{28,24},{1,5},{5... | collective-permute-start | bytes 3080 | tf_op jit(solution)/shard_map/ppermute | solution.py:26
  44.0 8.9 %copy-start.4 = (bf16[1024,1024]{1,0:T(8,128)(2,1)S(1)}, bf16[1024,1024]{1,0:T(8,128)(2,1)}, u32[]{:S(2)}) copy-start(bf16[1024,1024]{1,0:T(8,128)(2,1)} %refs_6_.1) | copy-start | bytes 6291460
  45.3 7.6 %copy-start.2 = (bf16[1024,1024]{1,0:T(8,128)(2,1)S(1)}, bf16[1024,1024]{1,0:T(8,128)(2,1)}, u32[]{:S(2)}) copy-start(bf16[1024,1024]{1,0:T(8,128)(2,1)} %refs_5_.1) | copy-start | bytes 6291460
  45.5 12.4 %collective-permute-start.14 = (bf16[1040,128]{1,0:T(8,128)(2,1)S(1)}, bf16[1040,128]{1,0:T(8,128)(2,1)S(1)}, u32[]{:S(2)}, u32[]{:S(2)}) collective-permute-start(bf16[1040,128]{1,0:T(8,128)(2,1)S(1)} %get-tuple-element.39), channel_id=1, source_target_pairs={{0,8},{4,12},{8,0},{12,4},{16,24},{20,28},{24,16},{28,20},{1,9},{5... | collective-permute-start | bytes 798728 | tf_op jit(solution)/shard_map/ppermute | solution.py:26
  47.2 18.6 %collective-permute-start.15 = (bf16[1040,128]{1,0:T(8,128)(2,1)S(1)}, bf16[1040,128]{1,0:T(8,128)(2,1)S(1)}, u32[]{:S(2)}, u32[]{:S(2)}) collective-permute-start(bf16[1040,128]{1,0:T(8,128)(2,1)S(1)} %get-tuple-element.40), channel_id=1, source_target_pairs={{0,16},{4,20},{8,24},{12,28},{16,0},{20,4},{24,8},{28,12},{1,17},{... | collective-permute-start | bytes 798728 | tf_op jit(solution)/shard_map/ppermute | solution.py:26
  48.6 24.2 %collective-permute-start.16 = (bf16[1040,128]{1,0:T(8,128)(2,1)S(1)}, bf16[1040,128]{1,0:T(8,128)(2,1)S(1)}, u32[]{:S(2)}, u32[]{:S(2)}) collective-permute-start(bf16[1040,128]{1,0:T(8,128)(2,1)S(1)} %get-tuple-element.41), channel_id=1, source_target_pairs={{0,24},{4,28},{8,16},{12,20},{16,8},{20,12},{24,0},{28,4},{1,25},{... | collective-permute-start | bytes 798728 | tf_op jit(solution)/shard_map/ppermute | solution.py:26
where the time goes:
time: 74.1 us; the launch traced here: 73.8 us
  waiting for transfers between devices  29.5 us (40%)
  Pallas kernels  19.3 us (26%)
  starting transfers between devices  16.6 us (22%)
  local copies, waits for them, and re-layouts  7.48 us (10%)
  between operations  0.78 us (1%)
    ppermute x17, waiting for transfers between devices, take(): return lax.ppermute(value, axis, pairs)  29.5 us
    ppermute x17, starting transfers between devices, take(): return lax.ppermute(value, axis, pairs)  16.6 us
    pallas_call x1, Pallas kernels, body(): pl.pallas_call(functools.partial(attention_kernel, scale, heads, head_siz...  9.02 us
    unnamed x25, local copies, waits for them, and re-layouts  7.48 us
    pallas_call x1, Pallas kernels, body(): pl.pallas_call(functools.partial(nodes_kernel, node_size, width), grid_sp...  3.89 us
    pallas_call x2, Pallas kernels, terms(): pl.pallas_call(functools.partial(terms_kernel, node_size + base, node_siz...  2.64 us
    pallas_call x1, Pallas kernels, body(): pl.pallas_call(functools.partial(out_grad_kernel, node_size), grid_spec=p...  2.52 us
  transfers between devices with their start and end apart: 17, of which 7 were waited for; matrix products, arithmetic and copies ran while one was open for 0% of the time, Pallas kernels for 23%

commit v1 on v0

v1 whole, which is shorter than its diff:
```python
import functools
import math

import jax
import jax.numpy as jnp
from jax import lax
from jax.experimental import pallas as pl
from jax.experimental.pallas import tpu as pltpu
from jax.sharding import PartitionSpec as P


BF16 = jnp.bfloat16
F32 = jnp.float32
LIMIT = pltpu.CompilerParams(vmem_limit_bytes=32 * 2**20)


def mm(a, b):
    return jnp.dot(a, b, preferred_element_type=F32)


def take(value, axis, step, size):
    if size & (size - 1) == 0:
        pairs = [(i, i ^ step) for i in range(size)]
    else:
        pairs = [((i + step) % size, i) for i in range(size)]
    return lax.ppermute(value, axis, pairs)


def give(value, axis, step, size):
    if size & (size - 1) == 0:
        return take(value, axis, step, size)
    return lax.ppermute(value, axis, [(i, (i + step) % size) for i in range(size)])


def column_blocks(weight, width):
    if width % 128 == 0:
        return weight
    return weight.reshape(weight.shape[0], -1, width).transpose(1, 0, 2)


def column_copy(ref, at, width, target, sem):
    if len(ref.shape) == 3:
        return pltpu.make_async_copy(ref.at[at], target, sem)
    at = pl.multiple_of(at * width, width)
    return pltpu.make_async_copy(ref.at[:, pl.ds(at, width)], target, sem)


def out_grad_kernel(count, width, ids_ref, rows_ref, w_ref, *refs):
    out_refs, (held, sems) = refs[:count], refs[count:]
    order = list(range(count - 1, -1, -1))
    copies = {s: column_copy(w_ref, ids_ref[s], width, held.at[s], sems.at[s]) for s in order}
    for s in order:
        copies[s].start()
    for s in order:
        copies[s].wait()
        out_refs[s][...] = mm(rows_ref[...], held[s]).astype(BF16)


def weights_kernel(width, ids_ref, *refs):
    sources, targets, sems = refs[:3], refs[3:6], refs[6]
    copies = [
        column_copy(sources[a], ids_ref[0], width, targets[a], sems.at[a]) for a in range(3)
    ]
    for c in copies:
        c.start()
    for c in copies:
        c.wait()


def attention_kernel(scale, heads, head_size, blocks, ids_ref, mask_ref, *refs):
    row_refs, d_refs = refs[:blocks], refs[blocks : 2 * blocks]
    refs = refs[2 * blocks :]
    wq_ref, wk_ref, wv_ref, eig_ref, lam_ref, lam_t_ref = refs[:6]
    grads_ref, eig_out, gw_ref = refs[6:9]
    ret_refs = refs[9 : 9 + blocks]
    (kw, qe, qn, kt, vn, vt, dn, dt, eig_t, eig_acc) = refs[9 + blocks :]
    eig_count, nodes = eig_ref.shape
    width = heads * head_size
    size = nodes // blocks
    steps, cols = qe.shape[1], qe.shape[3]
    tile_count = mask_ref.shape[1]
    tile = nodes // tile_count
    per = tile_count // blocks

    parts = []
    for s in range(blocks):
        parts.append(eig_ref[:, pl.ds(pl.multiple_of(ids_ref[s] * size, size), size)])
    eig = jnp.concatenate(parts, axis=1)
    turned = eig.T
    eig_t[...] = turned
    rows = jnp.concatenate([r[...] for r in row_refs], axis=0)
    query = mm(rows, wq_ref[...]).astype(BF16)
    query_t = (query.astype(F32) * scale).astype(BF16).T
    keys = mm(rows, wk_ref[...]).astype(BF16)
    keys_t = keys.T
    values = mm(rows, wv_ref[...]).astype(BF16)
    values_t = values.T
    d_att = jnp.concatenate([r[...] for r in d_refs], axis=0)
    d_att_t = d_att.T
    for h in range(heads):
        part = slice(h * head_size, (h + 1) * head_size)
        weighted_t = (turned.astype(F32) * lam_ref[h : h + 1, :]).astype(BF16)
        kw[h] = jnp.concatenate([keys[:, part], weighted_t], axis=1)
        qn[h] = jnp.concatenate([query[:, part], turned], axis=1)
        kt[h] = jnp.concatenate([keys_t[part], eig], axis=0)
        vn[h] = values[:, part]
        vt[h] = values_t[part]
        dn[h] = d_att[:, part]
        for b in range(steps):
            here = slice(b * cols, (b + 1) * cols)
            qe[h, b] = jnp.concatenate([query_t[part, here], eig[:, here]], axis=0)
            dt[h, b] = d_att_t[part, here]
    eig_acc[...] = jnp.zeros_like(eig_acc)
    lane = lax.broadcasted_iota(jnp.int32, (eig_count, heads), 1)

    def one_block(head, lam, first, block, totals):
        here = pl.ds(pl.multiple_of(block * cols, cols), cols)
        scores = mm(kw[head], qe[head, block])
        tiles_here = cols // tile
        columns = []
        for i in range(tiles_here):
            i_tile = block * tiles_here + i
            i_at = ids_ref[i_tile // per] * per + i_tile % per
            found = []
            for j in range(tile_count):
                j_at = ids_ref[j // per] * per + j % per
                part = scores[j * tile : (j + 1) * tile, i * tile : (i + 1) * tile]
                found.append(jnp.where(mask_ref[head, i_at, j_at] > 0, part, -jnp.inf))
            columns.append(jnp.concatenate(found, axis=0))
        masked = jnp.concatenate(columns, axis=1)
        top = jnp.max(masked, axis=0, keepdims=True)
        raised = jnp.exp(masked - top)
        total = jnp.sum(raised, axis=0, keepdims=True)
        prob = raised * (1.0 / total)
        half = prob.astype(BF16)
        grads_ref[pl.ds(3 * width + first, head_size), here] = mm(vt[head], half).astype(BF16)
        dprob = mm(vn[head], dt[head, block])
        delta = jnp.sum(prob * dprob, axis=0, keepdims=True)
        dscore = (prob * (dprob - delta)).astype(BF16)
        left = mm(kt[head], dscore)
        grads_ref[pl.ds(first, head_size), here] = (left[:head_size] * scale).astype(BF16)
        eig_acc[:, here] += lam * left[head_size:]
        right = mm(dscore, qn[head, here, :])
        value = mm(half, dn[head, here, :])
        if totals is None:
            return right, value
        return totals[0] + right, totals[1] + value

    def one_head(head, _):
        lam = jnp.sum(jnp.where(lane == head, lam_t_ref[...], 0.0), axis=1, keepdims=True)
        first = pl.multiple_of(head * head_size, head_size)
        totals = one_block(head, lam, first, 0, None)
        if steps > 1:
            totals = lax.fori_loop(
                1, steps, lambda b, t: one_block(head, lam, first, b, t), totals
            )
        full, value = totals
        flat = full.T
        grads_ref[pl.ds(width + first, head_size), :] = (flat[:head_size] * scale).astype(BF16)
        eig_acc[...] += lam * flat[head_size:]
        gw_ref[pl.ds(head, 1), :] = jnp.sum(
            eig_t[...].astype(F32) * full[:, head_size:], axis=0, keepdims=True
        )
        grads_ref[pl.ds(2 * width + first, head_size), :] = value.T.astype(BF16)
        return 0

    lax.fori_loop(0, heads, one_head, 0)
    eig_out[...] = eig_acc[:, :size]
    for b in range(blocks):
        part = slice(b * size, (b + 1) * size)
        ret_refs[b][: 3 * width] = grads_ref[: 3 * width, part]
        ret_refs[b][3 * width :] = eig_acc[:, part].astype(BF16)


def terms_kernel(base, nodes_blocks, target, ids_ref, *refs):
    row_refs, cot_refs = refs[:nodes_blocks], refs[nodes_blocks : 2 * nodes_blocks]
    grads_ref, out_ref = refs[2 * nodes_blocks :]
    count, _, width, _ = out_ref.shape

    def columns(ref, index):
        if target % 128 == 0:
            return ref[:, pl.ds(pl.multiple_of(index * target, target), target)]
        fit = 128 // target
        both = ref[:, pl.ds(pl.multiple_of(index // fit * 128, 128), 128)]
        found = both[:, :target]
        for part in range(1, fit):
            here = both[:, part * target : (part + 1) * target]
            found = jnp.where(index % fit == part, here, found)
        return found

    def right_of(pieces, at):
        return jnp.concatenate(
            [jnp.concatenate([columns(ref, a) for ref in pieces], axis=0) for a in at], axis=1
        )

    group = 2 if count % 2 == 0 else 1
    for start in range(0, count, group):
        at = [ids_ref[base + start + i] for i in range(group)]
        first = mm(grads_ref[: 3 * width], right_of(row_refs, at)).astype(BF16)
        second = mm(grads_ref[3 * width :], right_of(cot_refs, at)).astype(BF16)
        for i in range(group):
            lanes = slice(i * target, (i + 1) * target)
            for a in range(3):
                out_ref[start + i, a] = first[a * width : (a + 1) * width, lanes]
            out_ref[start + i, 3] = second[:, lanes]


def pair_kernel(count, near, keep_ref, got_ref, gw_ref, gw_got_ref, *refs):
    near_give, near_keep, own_ref, gw_out = refs[:4]
    piece_refs = refs[4:]
    _, terms, width, target = keep_ref.shape
    sums = gw_ref[...] + gw_got_ref[...]
    high = sums.astype(BF16)
    low = (sums - high.astype(F32)).astype(BF16)
    rows, lanes = sums.shape
    base = (terms - near) * width
    gw_out[...] = sums
    for s in range(count):
        total = keep_ref[s].astype(F32) + got_ref[s].astype(F32)
        if s % 2 == 0:
            near_keep[s // 2] = total[:near]
        else:
            near_give[s // 2] = total[:near].astype(BF16)
        if s == 0:
            own_ref[...] = total[near:]
            continue
        ref = piece_refs[s - 1]
        for a in range(terms - near):
            ref[a * width : (a + 1) * width] = total[near + a].astype(BF16)
        ref[base:] = jnp.zeros((ref.shape[0] - base, target), BF16)
        ref[base : base + rows, :lanes] = high
        ref[base + 8 : base + 8 + rows, :lanes] = low


def near_kernel(keep_ref, got_ref, own_ref, *piece_refs):
    own_ref[...] = keep_ref[0] + got_ref[0].astype(F32)
    for s, ref in enumerate(piece_refs):
        ref[...] = (keep_ref[s + 1] + got_ref[s + 1].astype(F32)).astype(BF16)


def final_kernel(near_count, near_own, own_ref, gw_ref, *refs):
    near_refs, piece_refs, (out_ref, gw_out) = refs[:near_count], refs[near_count:-2], refs[-2:]
    near, width, _ = near_own.shape
    terms = own_ref.shape[0]
    for a in range(near):
        total = near_own[a]
        for r in near_refs:
            total += r[a].astype(F32)
        out_ref[a] = total.T
    for a in range(terms):
        total = own_ref[a]
        for r in piece_refs:
            total += r[a * width : (a + 1) * width].astype(F32)
        out_ref[near + a] = total.T
    sums = gw_ref[...]
    rows, lanes = sums.shape
    base = terms * width
    for r in piece_refs:
        sums += r[base : base + rows, :lanes].astype(F32)
        sums += r[base + 8 : base + 8 + rows, :lanes].astype(F32)
    gw_out[...] = sums


def nodes_kernel(blocks, width, ids_ref, eig_ref, *refs):
    ret_refs = refs[:blocks]
    w_refs = refs[blocks : blocks + 3]
    out_ref, eig_out, joined = refs[blocks + 3 :]
    total = eig_ref[...]
    for s in range(blocks):
        at = pl.multiple_of(ids_ref[s] * width, width)
        for a in range(3):
            joined[a, pl.ds(at, width)] = ret_refs[s][a * width : (a + 1) * width]
        if s > 0:
            total += ret_refs[s][3 * width :].astype(F32)
    eig_out[...] = total
    chunk = min(256, out_ref.shape[1])
    for c in range(0, out_ref.shape[1], chunk):
        part = slice(c, c + chunk)
        total = mm(w_refs[0][part], joined[0])
        total += mm(w_refs[1][part], joined[1])
        total += mm(w_refs[2][part], joined[2])
        out_ref[:, part] = total.T.astype(BF16)


def body(node_feats, cotangent, w_query, w_key, w_value, w_out, eigvec, eig_weight, block_mask):
    node_size = lax.axis_size("node")
    clus_size = lax.axis_size("clus")
    node_me = lax.axis_index("node")
    clus_me = lax.axis_index("clus")
    own_rows, own_cot = node_feats[0], cotangent[0]
    size, model = own_rows.shape
    heads, eig_count = eig_weight.shape
    nodes = size * node_size
    width = model // node_size
    head_size = width // heads
    scale = head_size ** (-0.5)
    assert math.frexp(scale)[0] == 0.5
    assert clus_size & (clus_size - 1) == 0
    block = nodes
    while block * nodes > 512 * 512 and block > 128:
        block //= 2
    far_first = [s for s in range(node_size - 1, 0, -1)]

    rest = clus_size // 2
    order = jnp.arange(node_size, dtype=jnp.int32)
    order = order ^ node_me if node_size & (node_size - 1) == 0 else (order + node_me) % node_size
    slots = jnp.arange(clus_size, dtype=jnp.int32)
    slots = (2 * (slots % rest) + jnp.where(slots < rest, 1, 0)) ^ clus_me
    ids = jnp.concatenate([order, slots])

    rows = [own_rows] + [None] * (node_size - 1)
    for s in far_first:
        rows[s] = take(own_rows, "node", s, node_size)

    smem, vmem = pl.BlockSpec(memory_space=pltpu.SMEM), pl.BlockSpec(memory_space=pltpu.VMEM)
    hbm = pl.BlockSpec(memory_space=pltpu.HBM)

    def call(kernel, in_specs, out_shapes, operands, flops, moved, scratch=()):
        return pl.pallas_call(
            kernel,
            in_specs=in_specs,
            out_specs=[vmem] * len(out_shapes),
            out_shape=[jax.ShapeDtypeStruct(*o) for o in out_shapes],
            scratch_shapes=scratch,
            cost_estimate=pl.CostEstimate(flops=flops, bytes_accessed=moved, transcendentals=0),
            compiler_params=LIMIT,
        )(*operands)

    d_parts = call(
        functools.partial(out_grad_kernel, node_size, width),
        [smem, vmem, hbm],
        [((size, width), BF16)] * node_size,
        (ids, own_cot, pltpu.with_memory_space_constraint(column_blocks(w_out, width), pltpu.HBM)),
        3 * 10**8,
        3 * 2**20,
        [pltpu.VMEM((node_size, model, width), BF16), pltpu.SemaphoreType.DMA((node_size,))],
    )
    d_att = [d_parts[0]] + [None] * (node_size - 1)
    for s in far_first:
        d_att[s] = give(d_parts[s], "node", s, node_size)
    cots = [own_cot] + [None] * (node_size - 1)
    for s in far_first:
        cots[s] = take(own_cot, "node", s, node_size)

    weights = call(
        functools.partial(weights_kernel, width),
        [smem] + [hbm] * 3,
        [((model, width), BF16)] * 3,
        (ids, *[pltpu.with_memory_space_constraint(column_blocks(w, width), pltpu.HBM) for w in (w_query, w_key, w_value)]),
        0,
        3 * 2**20,
        [pltpu.SemaphoreType.DMA((3,))],
    )

    steps = nodes // block
    both = head_size + eig_count
    results = call(
        functools.partial(attention_kernel, scale, heads, head_size, node_size),
        [smem, smem] + [vmem] * (2 * node_size + 6),
        [((4 * width, nodes), BF16), ((eig_count, size), F32), ((heads, eig_count), F32)]
        + [((3 * width + eig_count, size), BF16)] * node_size,
        (ids, block_mask[0], *rows, *d_att, *weights, eigvec[0], eig_weight, eig_weight.T),
        8 * 10**9,
        8 * 2**20,
        [
            pltpu.VMEM((heads, nodes, both), BF16),
            pltpu.VMEM((heads, steps, both, block), BF16),
            pltpu.VMEM((heads, nodes, both), BF16),
            pltpu.VMEM((heads, both, nodes), BF16),
            pltpu.VMEM((heads, nodes, head_size), BF16),
            pltpu.VMEM((heads, head_size, nodes), BF16),
            pltpu.VMEM((heads, nodes, head_size), BF16),
            pltpu.VMEM((heads, steps, head_size, block), BF16),
            pltpu.VMEM((nodes, eig_count), BF16),
            pltpu.VMEM((eig_count, nodes), F32),
        ],
    )
    grads_t, eig_own, gw_own = results[:3]
    parts = results[3:]

    target = model // clus_size

    def terms(base):
        return call(
            functools.partial(terms_kernel, node_size + base, node_size, target),
            [smem] + [vmem] * (2 * node_size + 1),
            [((rest, 4, width, target), BF16)],
            (ids, *rows, *cots, grads_t),
            2 * 10**9,
            2 * 2**20,
        )[0]

    give_half = terms(0)
    gw_got = give(gw_own, "clus", 1, clus_size)
    got_half = give(give_half, "clus", 1, clus_size)
    keep_half = terms(rest)

    near, pairs = 2, rest // 2
    piece_rows = (4 - near) * width + 16
    near_give, near_keep, own_sum, gw_pair, *straight = call(
        functools.partial(pair_kernel, rest, near),
        [vmem] * 4,
        [
            ((pairs, near, width, target), BF16),
            ((pairs, near, width, target), F32),
            ((4 - near, width, target), F32),
            (eig_weight.shape, F32),
        ]
        + [((piece_rows, target), BF16)] * (rest - 1),
        (keep_half, got_half, gw_own, gw_got),
        10**6,
        4 * 2**20,
    )
    near_got = give(near_give, "clus", 2, clus_size)
    pieces = [None] * (rest - 1)
    for s in range(rest - 1, 0, -1):
        pieces[s - 1] = give(straight[s - 1], "clus", 2 * s, clus_size)
    near_own, *near_parts = call(
        near_kernel,
        [vmem] * 2,
        [((near, width, target), F32)] + [((near, width, target), BF16)] * (pairs - 1),
        (near_keep, near_got),
        10**6,
        2**20,
    )
    near_pieces = [None] * (pairs - 1)
    for s in range(pairs - 1, 0, -1):
        near_pieces[s - 1] = give(near_parts[s - 1], "clus", 4 * s, clus_size)

    returned = [parts[0]] + [None] * (node_size - 1)
    for s in far_first:
        returned[s] = give(parts[s], "node", s, node_size)

    grad_rows, grad_eig = call(
        functools.partial(nodes_kernel, node_size, width),
        [smem] + [vmem] * (node_size + 4),
        [((size, model), BF16), ((eig_count, size), F32)],
        (ids, eig_own, *returned, w_query, w_key, w_value),
        10**9,
        7 * 2**20,
        [pltpu.VMEM((3, model, size), BF16)],
    )

    grad_proj, grad_weight = call(
        functools.partial(final_kernel, pairs - 1),
        [vmem] * (3 + pairs - 1 + rest - 1),
        [((4, target, width), F32), (eig_weight.shape, F32)],
        (near_own, own_sum, gw_pair, *near_pieces, *pieces),
        10**6,
        2 * 2**20,
    )
    return (grad_rows[None], grad_eig[None], grad_weight, grad_proj)


def solution(mesh):
    placed = (
        P("clus", "node", None),
        P("clus", "node", None),
        P(),
        P(),
        P(),
        P(),
        P("clus", None, None),
        P("node", None),
        P("clus", "node", None, None),
    )
    return jax.shard_map(
        body,
        mesh=mesh,
        in_specs=placed,
        out_specs=(
            P("clus", "node", None),
            P("clus", None, "node"),
            P("node", None),
            P(None, "clus", "node"),
        ),
        check_vma=False,
    )
```

time: 74.1 us -> 68.8 us (0.928)
  the two profiles are of different devices: /device:TPU:20 before, /device:TPU:0 now
where the time goes in v1:
time: 68.8 us; the launch traced here: 68.6 us
  starting transfers between devices  26.3 us (38%)
  Pallas kernels  20.5 us (30%)
  waiting for transfers between devices  19.8 us (29%)
  local copies, waits for them, and re-layouts  1.08 us (2%)
  between operations  0.8 us (1%)
    ppermute x19, starting transfers between devices, take(): return lax.ppermute(value, axis, pairs)  26.3 us
    pallas_call x9, Pallas kernels, call(): pl.pallas_call(kernel, in_specs=in_specs, out_specs=[vmem] * len(out_shap...  20.5 us
    ppermute x19, waiting for transfers between devices, take(): return lax.ppermute(value, axis, pairs)  19.8 us
  transfers between devices with their start and end apart: 19, of which 7 were waited for; matrix products, arithmetic and copies ran while one was open for 0% of the time, Pallas kernels for 26%

profile of v1, /device:TPU:0, one launch (start us, length us, event | category | flops | bytes accessed | tf_op | source)
XLA Modules:
  0.0 68.6 jit_solution(15891474498612853144)
XLA Ops:
  0.6 0.0 copy-start.5
  0.6 3.0 %collective-permute-start = (bf16[128,1024]{1,0:T(8,128)(2,1)}, bf16[128,1024]{1,0:T(8,128)(2,1)S(1)}, u32[]{:S(2)}, u32[]{:S(2)}) collective-permute-start(bf16[128,1024]{1,0:T(8,128)(2,1)} %bitcast.14), channel_id=1, source_target_pairs={{0,1},{1,0},{2,3},{3,2},{4,5},{5,4},{6,7},{7,6},{8,9},{9,8},{10,11... | collective-permute-start | bytes 786440 | tf_op jit(solution)/shard_map/ppermute | solution.py:26
  3.7 1.5 %collective-permute-start.1 = (bf16[128,1024]{1,0:T(8,128)(2,1)}, bf16[128,1024]{1,0:T(8,128)(2,1)S(1)}, u32[]{:S(2)}, u32[]{:S(2)}) collective-permute-start(bf16[128,1024]{1,0:T(8,128)(2,1)} %bitcast.15), channel_id=1, source_target_pairs={{0,2},{1,3},{2,0},{3,1},{4,6},{5,7},{6,4},{7,5},{8,10},{9,11},{10,... | collective-permute-start | bytes 786440 | tf_op jit(solution)/shard_map/ppermute | solution.py:26
  5.2 0.0 collective-permute-start.2
  5.2 0.1 pad_add_fusion.ids_ref
  5.3 0.0 copy-start.3
  5.3 0.9 %copy-done.3 = bf16[1,128,1024]{2,1,0:T(8,128)(2,1)S(1)} copy-done((bf16[1,128,1024]{2,1,0:T(8,128)(2,1)S(1)}, bf16[1,128,1024]{2,1,0:T(8,128)(2,1)}, u32[]{:S(2)}) %copy-start.3) | copy-done | bytes 262168
  6.3 2.8 %shard_map.120 = (bf16[128,256]{1,0:T(8,128)(2,1)S(1)}, bf16[128,256]{1,0:T(8,128)(2,1)S(1)}, bf16[128,256]{1,0:T(8,128)(2,1)S(1)}, bf16[128,256]{1,0:T(8,128)(2,1)S(1)}) custom-call(s32[12]{0:T(128)S(1)} %pad_add_fusion.ids_ref, bf16[128,1024]{1,0:T(8,128)(2,1)S(1)} %bitcast.7, bf16[1024,1024]{1,0:T(8,128)(2,1)} %w_ref.1), custom_call_target="tpu_custom_call" | custom-call | flops 300000000 | bytes 3145728 | tf_op jit(solution)/shard_map/pallas_call | solution.py:319
  9.0 2.0 %collective-permute-start.3 = (bf16[128,256]{1,0:T(8,128)(2,1)S(1)}, bf16[128,256]{1,0:T(8,128)(2,1)S(1)}, u32[]{:S(2)}, u32[]{:S(2)}) collective-permute-start(bf16[128,256]{1,0:T(8,128)(2,1)S(1)} %get-tuple-element.32), channel_id=1, source_target_pairs={{0,1},{1,0},{2,3},{3,2},{4,5},{5,4},{6,7},{7,6},{8,9},{9,8},{10,11... | collective-permute-start | bytes 196616 | tf_op jit(solution)/shard_map/ppermute | solution.py:26
  11.0 1.5 %collective-permute-start.4 = (bf16[128,256]{1,0:T(8,128)(2,1)S(1)}, bf16[128,256]{1,0:T(8,128)(2,1)S(1)}, u32[]{:S(2)}, u32[]{:S(2)}) collective-permute-start(bf16[128,256]{1,0:T(8,128)(2,1)S(1)} %get-tuple-element.33), channel_id=1, source_target_pairs={{0,2},{1,3},{2,0},{3,1},{4,6},{5,7},{6,4},{7,5},{8,10},{9,11},{10,... | collective-permute-start | bytes 196616 | tf_op jit(solution)/shard_map/ppermute | solution.py:26
  12.6 4.7 %collective-permute-done.3.refs_5_ = bf16[128,256]{1,0:T(8,128)(2,1)S(1)} collective-permute-done((bf16[128,256]{1,0:T(8,128)(2,1)S(1)}, bf16[128,256]{1,0:T(8,128)(2,1)S(1)}, u32[]{:S(2)}, u32[]{:S(2)}) %collective-permute-start.3) | collective-permute-done | bytes 65568 | tf_op jit(solution)/shard_map/ppermute | solution.py:26
  17.3 2.7 %collective-permute-start.5 = (bf16[128,256]{1,0:T(8,128)(2,1)S(1)}, bf16[128,256]{1,0:T(8,128)(2,1)S(1)}, u32[]{:S(2)}, u32[]{:S(2)}) collective-permute-start(bf16[128,256]{1,0:T(8,128)(2,1)S(1)} %get-tuple-element.34), channel_id=1, source_target_pairs={{0,3},{1,2},{2,1},{3,0},{4,7},{5,6},{6,5},{7,4},{8,11},{9,10},{10,... | collective-permute-start | bytes 196616 | tf_op jit(solution)/shard_map/ppermute | solution.py:26
  20.0 0.0 copy-done.5
  20.0 0.1 copy.13
  20.1 0.0 copy-start.4
  20.1 0.0 copy-start.7
  20.1 0.0 copy-start.8
  20.1 1.9 %shard_map.121 = (bf16[1024,256]{1,0:T(8,128)(2,1)S(1)}, bf16[1024,256]{1,0:T(8,128)(2,1)S(1)}, bf16[1024,256]{1,0:T(8,128)(2,1)S(1)}) custom-call(s32[12]{0:T(128)S(1)} %pad_add_fusion.ids_ref, bf16[1024,1024]{1,0:T(8,128)(2,1)} %refs_4_.1, bf16[1024,1024]{1,0:T(8,128)(2,1)} %refs_5_.1, bf16[1024,1024]{1,0:T(8,128)(2,1)} %refs_6_.1), custom_call_target="tpu_custom_call" | custom-call | bytes 3145728 | tf_op jit(solution)/shard_map/pallas_call | solution.py:319
  22.0 0.0 collective-permute-done.4.refs_6_
  22.1 0.0 copy-done.4
  22.1 0.6 collective-permute-start.9
  22.7 0.0 collective-permute-done.5.refs_7_
  22.7 1.5 %collective-permute-start.10 = (bf16[128,1024]{1,0:T(8,128)(2,1)S(1)}, bf16[128,1024]{1,0:T(8,128)(2,1)S(1)}, u32[]{:S(2)}, u32[]{:S(2)}) collective-permute-start(bf16[128,1024]{1,0:T(8,128)(2,1)S(1)} %bitcast.9), channel_id=1, source_target_pairs={{0,2},{1,3},{2,0},{3,1},{4,6},{5,7},{6,4},{7,5},{8,10},{9,11},{10,... | collective-permute-start | bytes 786440 | tf_op jit(solution)/shard_map/ppermute | solution.py:26
  24.2 0.0 collective-permute-done.refs_1_
  24.2 1.6 %collective-permute-start.11 = (bf16[128,1024]{1,0:T(8,128)(2,1)S(1)}, bf16[128,1024]{1,0:T(8,128)(2,1)S(1)}, u32[]{:S(2)}, u32[]{:S(2)}) collective-permute-start(bf16[128,1024]{1,0:T(8,128)(2,1)S(1)} %bitcast.10), channel_id=1, source_target_pairs={{0,3},{1,2},{2,1},{3,0},{4,7},{5,6},{6,5},{7,4},{8,11},{9,10},{10,... | collective-permute-start | bytes 786440 | tf_op jit(solution)/shard_map/ppermute | solution.py:26
  25.8 0.0 collective-permute-done.1.refs_2_
  25.8 0.0 collective-permute-done.2.refs_3_
  25.8 0.0 copy-done.6
  25.8 0.0 copy-done.7
  25.8 0.0 copy-done.8
  25.8 8.7 %shard_map.122 = (bf16[1024,512]{1,0:T(8,128)(2,1)S(1)}, f32[64,128]{1,0:T(8,128)S(1)}, f32[4,64]{1,0:T(4,128)S(1)}, bf16[832,128]{1,0:T(8,128)(2,1)S(1)}, bf16[...) custom-call(s32[12]{0:T(128)S(1)} %pad_add_fusion.ids_ref, ...), custom_call_target="tpu_custom_call" | custom-call | flops 8000000000 | bytes 8388608 | tf_op jit(solution)/shard_map/pallas_call | solution.py:319
  34.5 0.0 collective-permute-done.9.refs_5_
  34.5 0.4 collective-permute-done.10.refs_6_
  34.9 0.0 collective-permute-done.11.refs_7_
  34.9 1.3 %shard_map.125 = bf16[4,4,256,128]{3,2,1,0:T(8,128)(2,1)S(1)} custom-call(s32[12]{0:T(128)S(1)} %pad_add_fusion.ids_ref, bf16[128,1024]{1,0:T(8,128)(2,1)S(1)} %bitcast.18, bf16[128,1024]{1,0:T(8,128)(2,1)S(1)} %collective-permute-done.refs_1_, bf16[128,1024]{1,0:T(8,128)(2,1)S(1)} %collective-permute-done.1.refs_2_, ...), custom_call_target="tpu_custom_call" | custom-call | flops 2000000000 | bytes 2097152 | tf_op jit(solution)/shard_map/pallas_call | solution.py:319
  36.3 0.1 collective-permute-start.12
  36.3 0.5 collective-permute-start.13
  36.8 1.3 %shard_map.124.keep_ref = bf16[4,4,256,128]{3,2,1,0:T(8,128)(2,1)S(1)} custom-call(s32[12]{0:T(128)S(1)} %pad_add_fusion.ids_ref, bf16[128,1024]{1,0:T(8,128)(2,1)S(1)} %bitcast.19, bf16[128,1024]{1,0:T(8,128)(2,1)S(1)} %collective-permute-done.refs_1_, bf16[128,1024]{1,0:T(8,128)(2,1)S(1)} %collective-permute-done.1.refs_2_, ...), custom_call_target="tpu_custom_call" | custom-call | flops 2000000000 | bytes 2097152 | tf_op jit(solution)/shard_map/pallas_call | solution.py:319
  38.2 0.0 copy-start
  38.2 0.8 %collective-permute-done.13.gw_got_ref = f32[4,64]{1,0:T(4,128)S(1)} collective-permute-done((f32[4,64]{1,0:T(4,128)S(1)}, f32[4,64]{1,0:T(4,128)S(1)}, u32[]{:S(2)}, u32[]{:S(2)}) %collective-permute-start.13) | collective-permute-done | bytes 1056 | tf_op jit(solution)/shard_map/ppermute | solution.py:26
  39.0 0.0 collective-permute-done.12.got_ref
  39.0 0.2 shard_map.126
  39.2 1.6 %collective-permute-start.14 = (bf16[2,2,256,128]{3,2,1,0:T(8,128)(2,1)S(1)}, bf16[2,2,256,128]{3,2,1,0:T(8,128)(2,1)S(1)}, u32[]{:S(2)}, u32[]{:S(2)}) collective-permute-start(bf16[2,2,256,128]{3,2,1,0:T(8,128)(2,1)S(1)} %get-tuple-element.48), channel_id=1, source_target_pairs={{0,8},{4,12},{8,0},{12,4},{16,24},{20,28},{24,16},{28,20},{1,9},{5... | collective-permute-start | bytes 786440 | tf_op jit(solution)/shard_map/ppermute | solution.py:26
  40.9 1.5 %collective-permute-start.6 = (bf16[832,128]{1,0:T(8,128)(2,1)S(1)}, bf16[832,128]{1,0:T(8,128)(2,1)S(1)}, u32[]{:S(2)}, u32[]{:S(2)}) collective-permute-start(bf16[832,128]{1,0:T(8,128)(2,1)S(1)} %get-tuple-element.40), channel_id=1, source_target_pairs={{0,1},{1,0},{2,3},{3,2},{4,5},{5,4},{6,7},{7,6},{8,9},{9,8},{10,11... | collective-permute-start | bytes 638984 | tf_op jit(solution)/shard_map/ppermute | solution.py:26
  42.4 1.4 %collective-permute-start.7 = (bf16[832,128]{1,0:T(8,128)(2,1)S(1)}, bf16[832,128]{1,0:T(8,128)(2,1)S(1)}, u32[]{:S(2)}, u32[]{:S(2)}) collective-permute-start(bf16[832,128]{1,0:T(8,128)(2,1)S(1)} %get-tuple-element.41), channel_id=1, source_target_pairs={{0,2},{1,3},{2,0},{3,1},{4,6},{5,7},{6,4},{7,5},{8,10},{9,11},{10,... | collective-permute-start | bytes 638984 | tf_op jit(solution)/shard_map/ppermute | solution.py:26
  43.8 0.6 collective-permute-start.8
  44.4 0.5 collective-permute-start.16
  44.8 4.2 %collective-permute-done.6.refs_1_ = bf16[832,128]{1,0:T(8,128)(2,1)S(1)} collective-permute-done((bf16[832,128]{1,0:T(8,128)(2,1)S(1)}, bf16[832,128]{1,0:T(8,128)(2,1)S(1)}, u32[]{:S(2)}, u32[]{:S(2)}) %collective-permute-start.6) | collective-permute-done | bytes 213024 | tf_op jit(solution)/shard_map/ppermute | solution.py:26
  49.0 2.6 %collective-permute-start.17 = (bf16[528,128]{1,0:T(8,128)(2,1)S(1)}, bf16[528,128]{1,0:T(8,128)(2,1)S(1)}, u32[]{:S(2)}, u32[]{:S(2)}) collective-permute-start(bf16[528,128]{1,0:T(8,128)(2,1)S(1)} %get-tuple-element.54), channel_id=1, source_target_pairs={{0,16},{4,20},{8,24},{12,28},{16,0},{20,4},{24,8},{28,12},{1,17},{... | collective-permute-start | bytes 405512 | tf_op jit(solution)/shard_map/ppermute | solution.py:26
  51.6 0.0 collective-permute-done.14.got_ref
  51.6 0.5 collective-permute-start.18
  52.1 0.1 shard_map.127
  52.1 1.5 %collective-permute-done.7.refs_2_ = bf16[832,128]{1,0:T(8,128)(2,1)S(1)} collective-permute-done((bf16[832,128]{1,0:T(8,128)(2,1)S(1)}, bf16[832,128]{1,0:T(8,128)(2,1)S(1)}, u32[]{:S(2)}, u32[]{:S(2)}) %collective-permute-start.7) | collective-permute-done | bytes 213024 | tf_op jit(solution)/shard_map/ppermute | solution.py:26
  53.7 2.6 %collective-permute-start.15 = (bf16[2,256,128]{2,1,0:T(8,128)(2,1)S(1)}, bf16[2,256,128]{2,1,0:T(8,128)(2,1)S(1)}, u32[]{:S(2)}, u32[]{:S(2)}) collective-permute-start(bf16[2,256,128]{2,1,0:T(8,128)(2,1)S(1)} %get-tuple-element.52), channel_id=1, source_target_pairs={{0,16},{4,20},{8,24},{12,28},{16,0},{20,4},{24,8},{28,12},{1,17},{... | collective-permute-start | bytes 393224 | tf_op jit(solution)/shard_map/ppermute | solution.py:26
  56.2 0.0 collective-permute-done.8.refs_3_
  56.2 0.0 copy-done.1
  56.2 0.0 copy-done.2
  56.3 0.0 copy-done
  56.3 3.2 %shard_map.123 = (bf16[128,1024]{1,0:T(8,128)(2,1)}, f32[64,128]{1,0:T(8,128)}) custom-call(s32[12]{0:T(128)S(1)} %pad_add_fusion.ids_ref, f32[64,128]{1,0:T(8,128)S(1)} %get-tuple-element.38.eig_ref, bf16[832,128]{1,0:T(8,128)(2,1)S(1)} %get-tuple-element.39.refs_0_, bf16[832,128]{1,0:T(8,128)(2,1)S(1)} %collective-permute-done.6.refs_1_, ...), custom_call_target="tpu_custom_call" | custom-call | flops 1000000000 | bytes 7340032 | tf_op jit(solution)/shard_map/pallas_call | solution.py:319
  59.5 0.0 collective-permute-done.16.refs_1_
  59.5 4.6 %collective-permute-done.17.refs_2_ = bf16[528,128]{1,0:T(8,128)(2,1)S(1)} collective-permute-done((bf16[528,128]{1,0:T(8,128)(2,1)S(1)}, bf16[528,128]{1,0:T(8,128)(2,1)S(1)}, u32[]{:S(2)}, u32[]{:S(2)}) %collective-permute-start.17) | collective-permute-done | bytes 135200 | tf_op jit(solution)/shard_map/ppermute | solution.py:26
  64.1 0.0 collective-permute-done.18.refs_3_
  64.1 3.5 %collective-permute-done.15.refs_0_ = bf16[2,256,128]{2,1,0:T(8,128)(2,1)S(1)} collective-permute-done((bf16[2,256,128]{2,1,0:T(8,128)(2,1)S(1)}, bf16[2,256,128]{2,1,0:T(8,128)(2,1)S(1)}, u32[]{:S(2)}, u32[]{:S(2)}) %collective-permute-start.15) | collective-permute-done | bytes 131104 | tf_op jit(solution)/shard_map/ppermute | solution.py:26
  67.6 1.0 %shard_map.128 = (f32[4,128,256]{2,1,0:T(8,128)}, f32[4,64]{1,0:T(4,128)}) custom-call(f32[2,256,128]{2,1,0:T(8,128)S(1)} %get-tuple-element.49.near_own, f32[2,256,128]{2,1,0:T(8,128)S(1)} %get-tuple-element.50.own_ref, f32[4,64]{1,0:T(4,128)S(1)} %get-tuple-element.51.gw_ref, bf16[2,256,128]{2,1,0:T(8,128)(2,1)S(1)} %collective-permute-done.15.refs_0_, ...), custom_call_target="tpu_custom_call" | custom-call | flops 1000000 | bytes 2097152 | tf_op jit(solution)/shard_map/pallas_call | solution.py:319
  (5 shorter events, 0.0 us)
Async XLA Ops:
  0.6 19.3 %copy-start.5 = (f32[4,64]{1,0:T(4,128)S(1)}, f32[4,64]{1,0:T(4,128)}, u32[]{:S(2)}) copy-start(f32[4,64]{1,0:T(4,128)} %refs_12_.1) | copy-start | bytes 3076
  0.6 23.6 %collective-permute-start = (bf16[128,1024]{1,0:T(8,128)(2,1)}, bf16[128,1024]{1,0:T(8,128)(2,1)S(1)}, u32[]{:S(2)}, u32[]{:S(2)}) collective-permute-start(bf16[128,1024]{1,0:T(8,128)(2,1)} %bitcast.14), channel_id=1, source_target_pairs={{0,1},{1,0},{2,3},{3,2},{4,5},{5,4},{6,7},{7,6},{8,9},{9,8},{10,11... | collective-permute-start | bytes 786440 | tf_op jit(solution)/shard_map/ppermute | solution.py:26
  3.7 22.1 %collective-permute-start.1 = (bf16[128,1024]{1,0:T(8,128)(2,1)}, bf16[128,1024]{1,0:T(8,128)(2,1)S(1)}, u32[]{:S(2)}, u32[]{:S(2)}) collective-permute-start(bf16[128,1024]{1,0:T(8,128)(2,1)} %bitcast.15), channel_id=1, source_target_pairs={{0,2},{1,3},{2,0},{3,1},{4,6},{5,7},{6,4},{7,5},{8,10},{9,11},{10,... | collective-permute-start | bytes 786440 | tf_op jit(solution)/shard_map/ppermute | solution.py:26
  5.2 20.6 %collective-permute-start.2 = (bf16[128,1024]{1,0:T(8,128)(2,1)}, bf16[128,1024]{1,0:T(8,128)(2,1)S(1)}, u32[]{:S(2)}, u32[]{:S(2)}) collective-permute-start(bf16[128,1024]{1,0:T(8,128)(2,1)} %bitcast.16), channel_id=1, source_target_pairs={{0,3},{1,2},{2,1},{3,0},{4,7},{5,6},{6,5},{7,4},{8,11},{9,10},{10,... | collective-permute-start | bytes 786440 | tf_op jit(solution)/shard_map/ppermute | solution.py:26
  5.3 0.9 %copy-start.3 = (bf16[1,128,1024]{2,1,0:T(8,128)(2,1)S(1)}, bf16[1,128,1024]{2,1,0:T(8,128)(2,1)}, u32[]{:S(2)}) copy-start(bf16[1,128,1024]{2,1,0:T(8,128)(2,1)} %param.10) | copy-start | bytes 786436
  9.0 8.2 %collective-permute-start.3 = (bf16[128,256]{1,0:T(8,128)(2,1)S(1)}, bf16[128,256]{1,0:T(8,128)(2,1)S(1)}, u32[]{:S(2)}, u32[]{:S(2)}) collective-permute-start(bf16[128,256]{1,0:T(8,128)(2,1)S(1)} %get-tuple-element.32), channel_id=1, source_target_pairs={{0,1},{1,0},{2,3},{3,2},{4,5},{5,4},{6,7},{7,6},{8,9},{9,8},{10,11... | collective-permute-start | bytes 196616 | tf_op jit(solution)/shard_map/ppermute | solution.py:26
  11.0 11.0 %collective-permute-start.4 = (bf16[128,256]{1,0:T(8,128)(2,1)S(1)}, bf16[128,256]{1,0:T(8,128)(2,1)S(1)}, u32[]{:S(2)}, u32[]{:S(2)}) collective-permute-start(bf16[128,256]{1,0:T(8,128)(2,1)S(1)} %get-tuple-element.33), channel_id=1, source_target_pairs={{0,2},{1,3},{2,0},{3,1},{4,6},{5,7},{6,4},{7,5},{8,10},{9,11},{10,... | collective-permute-start | bytes 196616 | tf_op jit(solution)/shard_map/ppermute | solution.py:26
  17.3 5.4 %collective-permute-start.5 = (bf16[128,256]{1,0:T(8,128)(2,1)S(1)}, bf16[128,256]{1,0:T(8,128)(2,1)S(1)}, u32[]{:S(2)}, u32[]{:S(2)}) collective-permute-start(bf16[128,256]{1,0:T(8,128)(2,1)S(1)} %get-tuple-element.34), channel_id=1, source_target_pairs={{0,3},{1,2},{2,1},{3,0},{4,7},{5,6},{6,5},{7,4},{8,11},{9,10},{10,... | collective-permute-start | bytes 196616 | tf_op jit(solution)/shard_map/ppermute | solution.py:26
  20.1 2.0 %copy-start.4 = (bf16[1,128,1024]{2,1,0:T(8,128)(2,1)S(1)}, bf16[1,128,1024]{2,1,0:T(8,128)(2,1)}, u32[]{:S(2)}) copy-start(bf16[1,128,1024]{2,1,0:T(8,128)(2,1)} %param.10) | copy-start | bytes 786436
  20.1 5.8 %copy-start.6 = (bf16[1,128,1024]{2,1,0:T(8,128)(2,1)S(1)}, bf16[1,128,1024]{2,1,0:T(8,128)(2,1)}, u32[]{:S(2)}) copy-start(bf16[1,128,1024]{2,1,0:T(8,128)(2,1)} %param.9) | copy-start | bytes 786436
  20.1 5.8 %copy-start.7 = (bf16[1,64,512]{2,1,0:T(8,128)(2,1)S(1)}, bf16[1,64,512]{2,1,0:T(8,128)(2,1)}, u32[]{:S(2)}) copy-start(bf16[1,64,512]{2,1,0:T(8,128)(2,1)} %param.15) | copy-start | bytes 196612
  20.1 5.8 %copy-start.8 = (s32[1,4,4,4]{3,2,1,0:T(4,128)S(1)}, s32[1,4,4,4]{3,2,1,0:T(4,128)}, u32[]{:S(2)}) copy-start(s32[1,4,4,4]{3,2,1,0:T(4,128)} %param.17) | copy-start | bytes 772
  22.1 12.5 %collective-permute-start.9 = (bf16[128,1024]{1,0:T(8,128)(2,1)S(1)}, bf16[128,1024]{1,0:T(8,128)(2,1)S(1)}, u32[]{:S(2)}, u32[]{:S(2)}) collective-permute-start(bf16[128,1024]{1,0:T(8,128)(2,1)S(1)} %bitcast.8), channel_id=1, source_target_pairs={{0,1},{1,0},{2,3},{3,2},{4,5},{5,4},{6,7},{7,6},{8,9},{9,8},{10,11... | collective-permute-start | bytes 786440 | tf_op jit(solution)/shard_map/ppermute | solution.py:26
  22.7 12.2 %collective-permute-start.10 = (bf16[128,1024]{1,0:T(8,128)(2,1)S(1)}, bf16[128,1024]{1,0:T(8,128)(2,1)S(1)}, u32[]{:S(2)}, u32[]{:S(2)}) collective-permute-start(bf16[128,1024]{1,0:T(8,128)(2,1)S(1)} %bitcast.9), channel_id=1, source_target_pairs={{0,2},{1,3},{2,0},{3,1},{4,6},{5,7},{6,4},{7,5},{8,10},{9,11},{10,... | collective-permute-start | bytes 786440 | tf_op jit(solution)/shard_map/ppermute | solution.py:26
  24.2 10.7 %collective-permute-start.11 = (bf16[128,1024]{1,0:T(8,128)(2,1)S(1)}, bf16[128,1024]{1,0:T(8,128)(2,1)S(1)}, u32[]{:S(2)}, u32[]{:S(2)}) collective-permute-start(bf16[128,1024]{1,0:T(8,128)(2,1)S(1)} %bitcast.10), channel_id=1, source_target_pairs={{0,3},{1,2},{2,1},{3,0},{4,7},{5,6},{6,5},{7,4},{8,11},{9,10},{10,... | collective-permute-start | bytes 786440 | tf_op jit(solution)/shard_map/ppermute | solution.py:26
  36.3 2.7 %collective-permute-start.12 = (bf16[4,4,256,128]{3,2,1,0:T(8,128)(2,1)S(1)}, bf16[4,4,256,128]{3,2,1,0:T(8,128)(2,1)S(1)}, u32[]{:S(2)}, u32[]{:S(2)}) collective-permute-start(bf16[4,4,256,128]{3,2,1,0:T(8,128)(2,1)S(1)} %shard_map.125), channel_id=1, source_target_pairs={{0,4},{4,0},{8,12},{12,8},{16,20},{20,16},{24,28},{28,24},{1,5},{5... | collective-permute-start | bytes 3145736 | tf_op jit(solution)/shard_map/ppermute | solution.py:26
  36.3 2.6 %collective-permute-start.13 = (f32[4,64]{1,0:T(4,128)S(1)}, f32[4,64]{1,0:T(4,128)S(1)}, u32[]{:S(2)}, u32[]{:S(2)}) collective-permute-start(f32[4,64]{1,0:T(4,128)S(1)} %get-tuple-element.46.gw_ref), channel_id=1, source_target_pairs={{0,4},{4,0},{8,12},{12,8},{16,20},{20,16},{24,28},{28,24},{1,5},{5... | collective-permute-start | bytes 3080 | tf_op jit(solution)/shard_map/ppermute | solution.py:26
  36.8 19.4 %copy-start.1 = (bf16[1024,1024]{1,0:T(8,128)(2,1)S(1)}, bf16[1024,1024]{1,0:T(8,128)(2,1)}, u32[]{:S(2)}) copy-start(bf16[1024,1024]{1,0:T(8,128)(2,1)} %refs_5_.1) | copy-start | bytes 6291460
  36.8 19.4 %copy-start.2 = (bf16[1024,1024]{1,0:T(8,128)(2,1)S(1)}, bf16[1024,1024]{1,0:T(8,128)(2,1)}, u32[]{:S(2)}) copy-start(bf16[1024,1024]{1,0:T(8,128)(2,1)} %refs_6_.1) | copy-start | bytes 6291460
  38.2 18.1 %copy-start = (bf16[1024,1024]{1,0:T(8,128)(2,1)S(1)}, bf16[1024,1024]{1,0:T(8,128)(2,1)}, u32[]{:S(2)}) copy-start(bf16[1024,1024]{1,0:T(8,128)(2,1)} %refs_4_.1) | copy-start | bytes 6291460
  39.2 12.4 %collective-permute-start.14 = (bf16[2,2,256,128]{3,2,1,0:T(8,128)(2,1)S(1)}, bf16[2,2,256,128]{3,2,1,0:T(8,128)(2,1)S(1)}, u32[]{:S(2)}, u32[]{:S(2)}) collective-permute-start(bf16[2,2,256,128]{3,2,1,0:T(8,128)(2,1)S(1)} %get-tuple-element.48), channel_id=1, source_target_pairs={{0,8},{4,12},{8,0},{12,4},{16,24},{20,28},{24,16},{28,20},{1,9},{5... | collective-permute-start | bytes 786440 | tf_op jit(solution)/shard_map/ppermute | solution.py:26
  40.9 8.1 %collective-permute-start.6 = (bf16[832,128]{1,0:T(8,128)(2,1)S(1)}, bf16[832,128]{1,0:T(8,128)(2,1)S(1)}, u32[]{:S(2)}, u32[]{:S(2)}) collective-permute-start(bf16[832,128]{1,0:T(8,128)(2,1)S(1)} %get-tuple-element.40), channel_id=1, source_target_pairs={{0,1},{1,0},{2,3},{3,2},{4,5},{5,4},{6,7},{7,6},{8,9},{9,8},{10,11... | collective-permute-start | bytes 638984 | tf_op jit(solution)/shard_map/ppermute | solution.py:26
  42.4 11.3 %collective-permute-start.7 = (bf16[832,128]{1,0:T(8,128)(2,1)S(1)}, bf16[832,128]{1,0:T(8,128)(2,1)S(1)}, u32[]{:S(2)}, u32[]{:S(2)}) collective-permute-start(bf16[832,128]{1,0:T(8,128)(2,1)S(1)} %get-tuple-element.41), channel_id=1, source_target_pairs={{0,2},{1,3},{2,0},{3,1},{4,6},{5,7},{6,4},{7,5},{8,10},{9,11},{10,... | collective-permute-start | bytes 638984 | tf_op jit(solution)/shard_map/ppermute | solution.py:26
  43.8 12.5 %collective-permute-start.8 = (bf16[832,128]{1,0:T(8,128)(2,1)S(1)}, bf16[832,128]{1,0:T(8,128)(2,1)S(1)}, u32[]{:S(2)}, u32[]{:S(2)}) collective-permute-start(bf16[832,128]{1,0:T(8,128)(2,1)S(1)} %get-tuple-element.42), channel_id=1, source_target_pairs={{0,3},{1,2},{2,1},{3,0},{4,7},{5,6},{6,5},{7,4},{8,11},{9,10},{10,... | collective-permute-start | bytes 638984 | tf_op jit(solution)/shard_map/ppermute | solution.py:26
  44.4 15.1 %collective-permute-start.16 = (bf16[528,128]{1,0:T(8,128)(2,1)S(1)}, bf16[528,128]{1,0:T(8,128)(2,1)S(1)}, u32[]{:S(2)}, u32[]{:S(2)}) collective-permute-start(bf16[528,128]{1,0:T(8,128)(2,1)S(1)} %get-tuple-element.53), channel_id=1, source_target_pairs={{0,8},{4,12},{8,0},{12,4},{16,24},{20,28},{24,16},{28,20},{1,9},{5... | collective-permute-start | bytes 405512 | tf_op jit(solution)/shard_map/ppermute | solution.py:26
  49.0 15.1 %collective-permute-start.17 = (bf16[528,128]{1,0:T(8,128)(2,1)S(1)}, bf16[528,128]{1,0:T(8,128)(2,1)S(1)}, u32[]{:S(2)}, u32[]{:S(2)}) collective-permute-start(bf16[528,128]{1,0:T(8,128)(2,1)S(1)} %get-tuple-element.54), channel_id=1, source_target_pairs={{0,16},{4,20},{8,24},{12,28},{16,0},{20,4},{24,8},{28,12},{1,17},{... | collective-permute-start | bytes 405512 | tf_op jit(solution)/shard_map/ppermute | solution.py:26
  51.6 12.5 %collective-permute-start.18 = (bf16[528,128]{1,0:T(8,128)(2,1)S(1)}, bf16[528,128]{1,0:T(8,128)(2,1)S(1)}, u32[]{:S(2)}, u32[]{:S(2)}) collective-permute-start(bf16[528,128]{1,0:T(8,128)(2,1)S(1)} %get-tuple-element.55), channel_id=1, source_target_pairs={{0,24},{4,28},{8,16},{12,20},{16,8},{20,12},{24,0},{28,4},{1,25},{... | collective-permute-start | bytes 405512 | tf_op jit(solution)/shard_map/ppermute | solution.py:26
  53.7 14.0 %collective-permute-start.15 = (bf16[2,256,128]{2,1,0:T(8,128)(2,1)S(1)}, bf16[2,256,128]{2,1,0:T(8,128)(2,1)S(1)}, u32[]{:S(2)}, u32[]{:S(2)}) collective-permute-start(bf16[2,256,128]{2,1,0:T(8,128)(2,1)S(1)} %get-tuple-element.52), channel_id=1, source_target_pairs={{0,16},{4,20},{8,24},{12,28},{16,0},{20,4},{24,8},{28,12},{1,17},{... | collective-permute-start | bytes 393224 | tf_op jit(solution)/shard_map/ppermute | solution.py:26

commit v2 on v1

v2 whole, which is shorter than its diff:
```python
import functools
import math

import jax
import jax.numpy as jnp
from jax import lax
from jax.experimental import pallas as pl
from jax.experimental.pallas import tpu as pltpu
from jax.sharding import PartitionSpec as P


BF16 = jnp.bfloat16
SPAN = 512
F32 = jnp.float32
LIMIT = pltpu.CompilerParams(vmem_limit_bytes=32 * 2**20)


def mm(a, b):
    return jnp.dot(a, b, preferred_element_type=F32)


def take(value, axis, step, size):
    if size & (size - 1) == 0:
        pairs = [(i, i ^ step) for i in range(size)]
    else:
        pairs = [((i + step) % size, i) for i in range(size)]
    return lax.ppermute(value, axis, pairs)


def give(value, axis, step, size):
    if size & (size - 1) == 0:
        return take(value, axis, step, size)
    return lax.ppermute(value, axis, [(i, (i + step) % size) for i in range(size)])


def column_blocks(weight, width):
    if width % 128 == 0:
        return weight
    return weight.reshape(weight.shape[0], -1, width).transpose(1, 0, 2)


def column_copy(ref, at, width, target, sem):
    if len(ref.shape) == 3:
        return pltpu.make_async_copy(ref.at[at], target, sem)
    at = pl.multiple_of(at * width, width)
    return pltpu.make_async_copy(ref.at[:, pl.ds(at, width)], target, sem)


def out_grad_kernel(count, width, ids_ref, rows_ref, w_ref, *refs):
    out_refs, (held, sems) = refs[:count], refs[count:]
    order = list(range(count - 1, -1, -1))
    copies = {s: column_copy(w_ref, ids_ref[s], width, held.at[s], sems.at[s]) for s in order}
    for s in order:
        copies[s].start()
    for s in order:
        copies[s].wait()
        out_refs[s][...] = mm(rows_ref[...], held[s]).astype(BF16)


def split_kernel(first_ref, second_ref, top_ref, bottom_ref):
    half = top_ref.shape[0]
    top_ref[...] = second_ref[:half]
    bottom_ref[...] = first_ref[half:]


def weights_kernel(width, calls, ids_ref, *refs):
    sources, targets, sems = refs[:3], refs[3:-1], refs[-1]
    copies = []
    for c in range(calls):
        for a in range(3):
            at = 3 * c + a
            if calls == 1:
                copies.append(column_copy(sources[a], ids_ref[0], width, targets[at], sems.at[at]))
            else:
                copies.append(
                    column_copy(
                        sources[a],
                        ids_ref[0] * calls + c,
                        width // calls,
                        targets[at],
                        sems.at[at],
                    )
                )
    for c in copies:
        c.start()
    for c in copies:
        c.wait()


def attention_kernel(scale, heads, head_size, blocks, pieces, base, last, ids_ref, mask_ref, *refs):
    row_refs, d_refs = refs[:pieces], refs[pieces : pieces + blocks]
    refs = refs[pieces + blocks :]
    wq_ref, wk_ref, wv_ref, eig_ref, lam_ref, lam_t_ref = refs[:6]
    earlier = base // heads
    prior_refs, refs = refs[6 : 6 + 2 * earlier], refs[6 + 2 * earlier :]
    grads_ref, out_ref, gw_ref = refs[:3]
    result_refs = refs[3:-5]
    qe, qn, dt, dn, left_acc = refs[-5:]
    eig_count, nodes = eig_ref.shape
    width = heads * head_size
    size = nodes // blocks
    steps, cols = qe.shape[1], qe.shape[3]
    tile_count = mask_ref.shape[1]
    tile = nodes // tile_count
    per = tile_count // blocks
    both = 2 * head_size
    assert eig_count == head_size
    groups = -(-heads // 2)

    def fit(array):
        extra = groups * both - array.shape[1]
        if extra == 0:
            return array
        return jnp.concatenate([array, jnp.zeros((array.shape[0], extra), array.dtype)], axis=1)

    parts = []
    for s in range(blocks):
        parts.append(eig_ref[:, pl.ds(pl.multiple_of(ids_ref[s] * size, size), size)])
    eig = jnp.concatenate(parts, axis=1)
    turned = jnp.concatenate([eig, eig], axis=0).T
    wide = turned.astype(F32)
    rows = jnp.concatenate([r[...] for r in row_refs], axis=0)
    query = fit(mm(rows, wq_ref[...]).astype(BF16))
    keys = fit(mm(rows, wk_ref[...]).astype(BF16))
    values = fit(mm(rows, wv_ref[...]).astype(BF16))
    first_column = base * head_size
    d_att = fit(
        jnp.concatenate([r[:, first_column : first_column + width] for r in d_refs], axis=0)
    )
    query_t = (query.astype(F32) * scale).astype(BF16).T
    keys_t = keys.T
    values_t = values.T
    d_att_t = d_att.T
    first_half = lax.broadcasted_iota(jnp.int32, (nodes, both), 1) < head_size
    first_row = lax.broadcasted_iota(jnp.int32, (1, both), 1) < head_size

    def pick(even, first, second):
        return jnp.where(first_half, first, second) if even else jnp.where(first_half, second, first)

    def stack(even, first, second):
        return jnp.concatenate([first, second] if even else [second, first], axis=0)

    for g in range(groups):
        group = slice(g * both, (g + 1) * both)
        dn[g] = d_att[:, group]
        for b in range(steps):
            here = slice(b * cols, (b + 1) * cols)
            dt[g, b] = d_att_t[group, here]
        for h in range(2 * g, min(2 * g + 2, heads)):
            even = h % 2 == 0
            part = slice(h * head_size, (h + 1) * head_size)
            qn[h] = pick(even, query[:, group], turned)
            for b in range(steps):
                here = slice(b * cols, (b + 1) * cols)
                qe[h, b] = stack(even, query_t[part, here], eig[:, here])

    def before(head, block, kw, vn):
        return mm(kw, qe[head, block]), mm(vn, dt[head // 2, block])

    def one_block(head, block, kt, vt, scores, dprob, totals):
        at = block * cols
        here = pl.ds(at if isinstance(block, int) else pl.multiple_of(at, cols), cols)
        tiles_here = cols // tile
        columns = []
        for i in range(tiles_here):
            i_tile = block * tiles_here + i
            i_at = ids_ref[i_tile // per] * per + i_tile % per
            found = []
            for j in range(tile_count):
                j_at = ids_ref[j // per] * per + j % per
                part = scores[j * tile : (j + 1) * tile, i * tile : (i + 1) * tile]
                found.append(jnp.where(mask_ref[base + head, i_at, j_at] > 0, part, -jnp.inf))
            columns.append(jnp.concatenate(found, axis=0))
        masked = jnp.concatenate(columns, axis=1)
        top = jnp.max(masked, axis=0, keepdims=True)
        raised = jnp.exp(masked - top)
        total = jnp.sum(raised, axis=0, keepdims=True)
        prob = raised * (1.0 / total)
        half = prob.astype(BF16)
        first = head * head_size
        out_ref[first : first + head_size, here] = mm(vt, half).astype(BF16)
        value = mm(half, dn[head // 2, here, :])
        delta = jnp.sum(prob * dprob, axis=0, keepdims=True)
        dscore = (prob * (dprob - delta)).astype(BF16)
        left = mm(kt, dscore)
        grads_ref[first : first + head_size, here] = (left[:head_size] * scale).astype(BF16)
        weighted = lam_t_ref[:, base + head : base + head + 1] * left[head_size:]
        if head == 0:
            left_acc[:, here] = weighted
        else:
            left_acc[:, here] += weighted
        right = mm(dscore, qn[head, here, :])
        if totals is None:
            return right, value
        return totals[0] + right, totals[1] + value

    def operands(h):
        even, g = h % 2 == 0, h // 2
        group = slice(g * both, (g + 1) * both)
        part = slice(h * head_size, (h + 1) * head_size)
        lam_row = jnp.concatenate([lam_ref[base + h : base + h + 1, :]] * 2, axis=1)
        kw = pick(even, keys[:, group], (wide * lam_row).astype(BF16))
        kt = jnp.concatenate([keys_t[part], eig], axis=0)
        vn = pick(even, values[:, group], jnp.zeros((nodes, both), BF16))
        return lam_row, kw, kt, values_t[part], vn

    unrolled = [(h, b) for h in range(heads) for b in range(steps)] if steps <= 4 else []
    ready = {}

    def prepare(at):
        if at < len(unrolled):
            h, b = unrolled[at]
            if b == 0:
                ready[h] = operands(h)
            ready[h, b] = before(h, b, ready[h][1], ready[h][4])

    def all_blocks(h):
        if unrolled:
            totals = None
            for b in range(steps):
                prepare(h * steps + b + 1)
                _, _, kt, vt, _ = ready[h]
                totals = one_block(h, b, kt, vt, *ready.pop((h, b)), totals)
            return ready[h][0], totals
        lam_row, kw, kt, vt, vn = operands(h)
        return lam_row, lax.fori_loop(
            1,
            steps,
            lambda b, t: one_block(h, b, kt, vt, *before(h, b, kw, vn), t),
            one_block(h, 0, kt, vt, *before(h, 0, kw, vn), None),
        )

    prepare(0)
    right_total = None
    for g in range(groups):
        group = slice(g * both, (g + 1) * both)
        found = []
        lam_rows = []
        for h in range(2 * g, min(2 * g + 2, heads)):
            lam_row, totals = all_blocks(h)
            lam_rows.append(lam_row)
            found.append(totals)
        if len(found) == 1:
            found.append((jnp.zeros((nodes, both), F32), jnp.zeros((nodes, both), F32)))
            lam_rows.append(jnp.zeros((1, both), F32))
        keep = min(both, width - g * both)
        key_grad = jnp.where(first_half, found[0][0], found[1][0]).T
        grads_ref[width + g * both : width + g * both + keep, :] = (
            key_grad[:keep] * scale
        ).astype(BF16)
        value_grad = jnp.where(first_half, found[0][1], found[1][1]).T
        grads_ref[2 * width + g * both : 2 * width + g * both + keep, :] = value_grad[
            :keep
        ].astype(BF16)
        right = jnp.where(first_half, found[1][0], found[0][0])
        sums = jnp.sum(wide * right, axis=0, keepdims=True)
        gw_ref[2 * g : 2 * g + 1, :] = sums[:, head_size:]
        if 2 * g + 1 < heads:
            gw_ref[2 * g + 1 : 2 * g + 2, :] = sums[:, :head_size]
        right = right * jnp.where(first_row, lam_rows[1], lam_rows[0])
        right_total = right if right_total is None else right_total + right

    flat = right_total.T
    eig_sum = left_acc[...] + flat[:head_size] + flat[head_size:]
    if not last:
        result_refs[0][...] = eig_sum
        return
    for r in prior_refs[1::2]:
        eig_sum += r[...]
    result_refs[0][...] = eig_sum[:, :size]
    for b in range(blocks):
        part = slice(b * size, (b + 1) * size)
        ret_ref, at = result_refs[1 + b], 0
        for r in (*prior_refs[::2], grads_ref):
            ret_ref[at : at + r.shape[0]] = r[:, part]
            at += r.shape[0]
        ret_ref[at:] = eig_sum[:, part].astype(BF16)


def terms_kernel(base, pieces, outs, target, ids_ref, *refs):
    row_refs, refs = refs[:pieces], refs[pieces:]
    cot_refs, (grads_ref, *head_outs, out_ref) = refs[: -2 - outs], refs[-2 - outs :]
    count = out_ref.shape[0]

    def columns(ref, index):
        if target % 128 == 0:
            return ref[:, pl.ds(pl.multiple_of(index * target, target), target)]
        fit = 128 // target
        both = ref[:, pl.ds(pl.multiple_of(index // fit * 128, 128), 128)]
        found = both[:, :target]
        for part in range(1, fit):
            here = both[:, part * target : (part + 1) * target]
            found = jnp.where(index % fit == part, here, found)
        return found

    def right_of(pieces, at):
        return jnp.concatenate(
            [jnp.concatenate([columns(ref, a) for ref in pieces], axis=0) for a in at], axis=1
        )

    group = 2 if count % 2 == 0 else 1
    for start in range(0, count, group):
        at = [ids_ref[base + start + i] for i in range(group)]
        found = [mm(grads_ref[...], right_of(row_refs, at)).astype(BF16)]
        if outs:
            right = right_of(cot_refs, at)
            found += [mm(r[...], right).astype(BF16) for r in head_outs]
        row = 0
        for value in found:
            for i in range(group):
                out_ref[start + i, row : row + value.shape[0]] = value[:, i * target : (i + 1) * target]
            row += value.shape[0]


def put_sums(ref, base, sums):
    rows, lanes = sums.shape
    high = sums.astype(BF16)
    ref[base:] = jnp.zeros((16, ref.shape[1]), BF16)
    ref[base : base + rows, :lanes] = high
    ref[base + 8 : base + 8 + rows, :lanes] = (sums - high.astype(F32)).astype(BF16)


def get_sums(ref, base, shape):
    rows, lanes = shape
    high = ref[base : base + rows, :lanes].astype(F32)
    return high + ref[base + 8 : base + 8 + rows, :lanes].astype(F32)


def pair_kernel(sums, keep_ref, got_ref, *refs):
    if sums:
        gw_refs, gw_got_ref, give_ref, near_ref, gw_out = refs[:sums], *refs[sums:]
    else:
        give_ref, near_ref = refs
    count, rows, _ = keep_ref.shape
    for s in range(count):
        total = keep_ref[s].astype(F32) + got_ref[s].astype(F32)
        if s % 2 == 0:
            near_ref[s // 2] = total
        else:
            give_ref[s // 2 * rows : (s // 2 + 1) * rows] = total.astype(BF16)
    if sums:
        total = jnp.concatenate([r[...] for r in gw_refs], axis=0) + gw_got_ref[...]
        gw_out[...] = total
        put_sums(give_ref, count // 2 * rows, total)


def near_kernel(sums, keep_ref, got_ref, *refs):
    if sums:
        gw_ref, own_ref, gw_out, *piece_refs = refs
    else:
        own_ref, *piece_refs = refs
    count, rows, _ = keep_ref.shape
    own_ref[...] = keep_ref[0] + got_ref[:rows].astype(F32)
    for s, ref in enumerate(piece_refs):
        part = slice((s + 1) * rows, (s + 2) * rows)
        ref[:rows] = (keep_ref[s + 1] + got_ref[part].astype(F32)).astype(BF16)
    if sums:
        total = gw_ref[...] + get_sums(got_ref, count * rows, gw_ref.shape)
        gw_out[...] = total
        for ref in piece_refs:
            put_sums(ref, rows, total)


def final_kernel(calls, count, *refs):
    groups, gw_ref, (out_ref, gw_out) = [], refs[-3], refs[-2:]
    for c in range(calls):
        at = c * (count + 1)
        groups.append((refs[at], refs[at + 1 : at + 1 + count]))
    width = out_ref.shape[2] // calls
    for c, (own_ref, piece_refs) in enumerate(groups):
        total = own_ref[...]
        rows = total.shape[0]
        for r in piece_refs:
            total += r[:rows].astype(F32)
        for a in range(3):
            out_ref[a, :, c * width : (c + 1) * width] = total[a * width : (a + 1) * width].T
        if c == calls - 1:
            out_ref[3] = total[3 * width :].T
            sums = gw_ref[...]
            for r in piece_refs:
                sums += get_sums(r, rows, sums.shape)
            gw_out[...] = sums


def nodes_kernel(blocks, width, calls, ids_ref, eig_ref, *refs):
    ret_refs = refs[:blocks]
    w_refs = refs[blocks : blocks + 3]
    out_ref, eig_out, joined = refs[blocks + 3 :]
    total = eig_ref[...]
    for s in range(blocks):
        part = width // calls
        for c in range(calls):
            at = pl.multiple_of(ids_ref[s] * width + c * part, part)
            for a in range(3):
                row = (3 * c + a) * part
                joined[a, pl.ds(at, part)] = ret_refs[s][row : row + part]
        if s > 0:
            total += ret_refs[s][3 * width :].astype(F32)
    eig_out[...] = total
    chunk = min(256, out_ref.shape[1])
    for c in range(0, out_ref.shape[1], chunk):
        part = slice(c, c + chunk)
        total = mm(w_refs[0][part], joined[0])
        total += mm(w_refs[1][part], joined[1])
        total += mm(w_refs[2][part], joined[2])
        out_ref[:, part] = total.T.astype(BF16)


def body(node_feats, cotangent, w_query, w_key, w_value, w_out, eigvec, eig_weight, block_mask):
    node_size = lax.axis_size("node")
    clus_size = lax.axis_size("clus")
    node_me = lax.axis_index("node")
    clus_me = lax.axis_index("clus")
    own_rows, own_cot = node_feats[0], cotangent[0]
    size, model = own_rows.shape
    heads, eig_count = eig_weight.shape
    nodes = size * node_size
    width = model // node_size
    head_size = width // heads
    scale = head_size ** (-0.5)
    assert math.frexp(scale)[0] == 0.5
    assert clus_size & (clus_size - 1) == 0
    block = nodes
    while block * nodes > SPAN * 512 and block > 128:
        block //= 2
    far_first = [s for s in range(node_size - 1, 0, -1)]

    rest = clus_size // 2
    order = jnp.arange(node_size, dtype=jnp.int32)
    order = order ^ node_me if node_size & (node_size - 1) == 0 else (order + node_me) % node_size
    slots = jnp.arange(clus_size, dtype=jnp.int32)
    slots = (2 * (slots % rest) + jnp.where(slots < rest, 1, 0)) ^ clus_me
    ids = jnp.concatenate([order, slots])

    smem, vmem = pl.BlockSpec(memory_space=pltpu.SMEM), pl.BlockSpec(memory_space=pltpu.VMEM)
    hbm = pl.BlockSpec(memory_space=pltpu.HBM)

    def call(kernel, in_specs, out_shapes, operands, flops, moved, scratch=()):
        return call_here(kernel, in_specs, out_shapes, operands, flops, moved, scratch)

    def call_here(kernel, in_specs, out_shapes, operands, flops, moved, scratch):
        return pl.pallas_call(
            kernel,
            in_specs=in_specs,
            out_specs=[vmem] * len(out_shapes),
            out_shape=[jax.ShapeDtypeStruct(*o) for o in out_shapes],
            scratch_shapes=scratch,
            cost_estimate=pl.CostEstimate(flops=flops, bytes_accessed=moved, transcendentals=0),
            compiler_params=LIMIT,
        )(*operands)

    crossed = node_size == 4 and size % 32 == 0
    rows = [own_rows] + [None] * (node_size - 1)
    for s in far_first:
        if s < 3 or not crossed:
            rows[s] = take(own_rows, "node", s, node_size)

    d_parts = call(
        functools.partial(out_grad_kernel, node_size, width),
        [smem, vmem, hbm],
        [((size, width), BF16)] * node_size,
        (ids, own_cot, pltpu.with_memory_space_constraint(column_blocks(w_out, width), pltpu.HBM)),
        3 * 10**8,
        3 * 2**20,
        [pltpu.VMEM((node_size, model, width), BF16), pltpu.SemaphoreType.DMA((node_size,))],
    )
    d_att = [d_parts[0]] + [None] * (node_size - 1)
    for s in far_first:
        d_att[s] = give(d_parts[s], "node", s, node_size)
    if crossed:
        top, bottom = call(
            split_kernel, [vmem] * 2, [((size // 2, model), BF16)] * 2, (rows[1], rows[2]), 0, 2**19
        )
        rows[3:] = [take(top, "node", 1, node_size), take(bottom, "node", 2, node_size)]
    cots = [own_cot] + [None] * (node_size - 1)
    for s in far_first:
        cots[s] = take(own_cot, "node", s, node_size)

    calls = -(-heads // 2)
    sub_heads = heads // calls
    part_width = width // calls
    assert sub_heads * calls == heads
    weights = call(
        functools.partial(weights_kernel, width, calls),
        [smem] + [hbm] * 3,
        [((model, part_width), BF16)] * (3 * calls),
        (
            ids,
            *[
                pltpu.with_memory_space_constraint(column_blocks(w, width), pltpu.HBM)
                for w in (w_query, w_key, w_value)
            ],
        ),
        0,
        3 * 2**20,
        [pltpu.SemaphoreType.DMA((3 * calls,))],
    )

    steps = nodes // block
    both = 2 * head_size
    groups = -(-sub_heads // 2)
    target = model // clus_size
    pairs = rest // 2
    lam_t = eig_weight.T

    def attention(c, prior):
        last = c == calls - 1
        shapes = [
            ((3 * part_width, nodes), BF16),
            ((part_width, nodes), BF16),
            ((sub_heads, eig_count), F32),
        ]
        if last:
            shapes += [((eig_count, size), F32)]
            shapes += [((3 * width + eig_count, size), BF16)] * node_size
        else:
            shapes += [((eig_count, nodes), F32)]
        return call(
            functools.partial(
                attention_kernel,
                scale,
                sub_heads,
                head_size,
                node_size,
                len(rows),
                c * sub_heads,
                last,
            ),
            [smem, smem] + [vmem] * (len(rows) + node_size + 6 + len(prior)),
            shapes,
            (
                ids,
                block_mask[0],
                *rows,
                *d_att,
                *weights[3 * c : 3 * c + 3],
                eigvec[0],
                eig_weight,
                lam_t,
                *prior,
            ),
            4 * 10**9,
            4 * 2**20,
            [
                pltpu.VMEM((sub_heads, steps, both, block), BF16),
                pltpu.VMEM((sub_heads, nodes, both), BF16),
                pltpu.VMEM((groups, steps, both, block), BF16),
                pltpu.VMEM((groups, nodes, both), BF16),
                pltpu.VMEM((eig_count, nodes), F32),
            ],
        )

    def terms(base, grads_t, outs):
        used = cots if outs else []
        return call(
            functools.partial(terms_kernel, node_size + base, len(rows), len(outs), target),
            [smem] + [vmem] * (len(rows) + len(used) + 1 + len(outs)),
            [((rest, grads_t.shape[0] + len(outs) * part_width, target), BF16)],
            (ids, *rows, *used, grads_t, *outs),
            10**9,
            2**20,
        )[0]

    near_keeps, near_gots, head_outs, weight_parts, prior = [], [], [], [], []
    for c in range(calls):
        last = c == calls - 1
        grads_t, head_out, weight_part, *others = attention(c, prior)
        head_outs.append(head_out)
        weight_parts.append(weight_part)
        prior += [grads_t, others[0]]
        outs = head_outs if last else []
        give_half = terms(0, grads_t, outs)
        got_half = give(give_half, "clus", 1, clus_size)
        keep_half = terms(rest, grads_t, outs)
        group_rows = keep_half.shape[1]
        extra = 16 if last else 0
        operands = [keep_half, got_half]
        shapes = [((pairs * group_rows + extra, target), BF16), ((pairs, group_rows, target), F32)]
        if last:
            mine = jnp.concatenate(weight_parts, axis=0) if calls > 1 else weight_part
            operands += [*weight_parts, give(mine, "clus", 1, clus_size)]
            shapes.append((eig_weight.shape, F32))
        near_give, near_keep, *gw_pair = call(
            functools.partial(pair_kernel, calls if last else 0),
            [vmem] * len(operands),
            shapes,
            operands,
            10**6,
            2**21,
        )
        near_keeps.append(near_keep)
        near_gots.append(give(near_give, "clus", 2, clus_size))
    eig_own, *parts = others

    returned = [parts[0]] + [None] * (node_size - 1)
    for s in far_first:
        returned[s] = give(parts[s], "node", s, node_size)

    totals = []
    for c in range(calls):
        group_rows = near_keeps[c].shape[1]
        last = c == calls - 1
        extra = 16 if last else 0
        shapes = [((group_rows, target), F32)] + ([(eig_weight.shape, F32)] if last else [])
        own, *others = call(
            functools.partial(near_kernel, last),
            [vmem] * (3 if last else 2),
            shapes + [((group_rows + extra, target), BF16)] * (pairs - 1),
            (near_keeps[c], near_gots[c], *(gw_pair if last else [])),
            10**6,
            2**20,
        )
        if last:
            gw_four, *others = others
        totals.append(own)
        found = [None] * (pairs - 1)
        for s in range(pairs - 1, 0, -1):
            found[s - 1] = give(others[s - 1], "clus", 4 * s, clus_size)
        totals += found

    grad_rows, grad_eig = call(
        functools.partial(nodes_kernel, node_size, width, calls),
        [smem] + [vmem] * (node_size + 4),
        [((size, model), BF16), ((eig_count, size), F32)],
        (ids, eig_own, *returned, w_query, w_key, w_value),
        10**9,
        7 * 2**20,
        [pltpu.VMEM((3, model, size), BF16)],
    )

    grad_proj, grad_weight = call(
        functools.partial(final_kernel, calls, pairs - 1),
        [vmem] * (len(totals) + 1),
        [((4, target, width), F32), (eig_weight.shape, F32)],
        (*totals, gw_four),
        10**6,
        2 * 2**20,
    )
    return (grad_rows[None], grad_eig[None], grad_weight, grad_proj)


def solution(mesh):
    placed = (
        P("clus", "node", None),
        P("clus", "node", None),
        P(),
        P(),
        P(),
        P(),
        P("clus", None, None),
        P("node", None),
        P("clus", "node", None, None),
    )

    return jax.shard_map(
        body,
        mesh=mesh,
        in_specs=placed,
        out_specs=(
            P("clus", "node", None),
            P("clus", None, "node"),
            P("node", None),
            P(None, "clus", "node"),
        ),
        check_vma=False,
    )
```

time: 68.8 us -> 66.7 us (0.969)
  starting transfers between devices: 26.3 us -> 23.1 us
  Pallas kernels: 20.5 us -> 21.5 us
    ppermute x19 -> x20, starting transfers between devices: 26.3 us -> 23.1 us  [take(): return lax.ppermute(value, axis, pairs)]
    pallas_call x9 -> x15, Pallas kernels: 20.5 us -> 21.5 us  [call_here(): pl.pallas_call(kernel, in_specs=in_specs, out_specs=[vmem] * len(out_shap...]
    ppermute x19 -> x20, waiting for transfers between devices: 19.8 us -> 19.8 us  [take(): return lax.ppermute(value, axis, pairs)]
  transfers between devices with their start and end apart: 19 -> 20, of which waited for: 7 -> 8; matrix products, arithmetic and copies ran while one was open for 0% -> 0% of each run, Pallas kernels for 26% -> 29%
where the time goes in v2:
time: 66.7 us; the launch traced here: 66.5 us
  starting transfers between devices  23.1 us (35%)
  Pallas kernels  21.5 us (32%)
  waiting for transfers between devices  19.8 us (30%)
  local copies, waits for them, and re-layouts  1.08 us (2%)
  between operations  0.86 us (1%)
    ppermute x20, starting transfers between devices, take(): return lax.ppermute(value, axis, pairs)  23.1 us
    pallas_call x15, Pallas kernels, call_here(): pl.pallas_call(kernel, in_specs=in_specs, out_specs=[vmem] * len(out_shap...  21.5 us
    ppermute x20, waiting for transfers between devices, take(): return lax.ppermute(value, axis, pairs)  19.8 us
  transfers between devices with their start and end apart: 20, of which 8 were waited for; matrix products, arithmetic and copies ran while one was open for 0% of the time, Pallas kernels for 29%

profile of v2, /device:TPU:0, one launch (start us, length us, event | category | flops | bytes accessed | tf_op | source)
XLA Modules:
  0.0 66.5 jit_solution(8316891724216905610)
XLA Ops:
  0.6 3.0 %collective-permute-start = (bf16[128,1024]{1,0:T(8,128)(2,1)}, bf16[128,1024]{1,0:T(8,128)(2,1)S(1)}, u32[]{:S(2)}, u32[]{:S(2)}) collective-permute-start(bf16[128,1024]{1,0:T(8,128)(2,1)} %bitcast.15), channel_id=1, source_target_pairs={{0,1},{1,0},{2,3},{3,2},{4,5},{5,4},{6,7},{7,6},{8,9},{9,8},{10,11... | collective-permute-start | bytes 786440 | tf_op jit(solution)/shard_map/ppermute | solution.py:27
  3.7 1.5 %collective-permute-start.1 = (bf16[128,1024]{1,0:T(8,128)(2,1)}, bf16[128,1024]{1,0:T(8,128)(2,1)S(1)}, u32[]{:S(2)}, u32[]{:S(2)}) collective-permute-start(bf16[128,1024]{1,0:T(8,128)(2,1)} %bitcast.16), channel_id=1, source_target_pairs={{0,2},{1,3},{2,0},{3,1},{4,6},{5,7},{6,4},{7,5},{8,10},{9,11},{10,... | collective-permute-start | bytes 786440 | tf_op jit(solution)/shard_map/ppermute | solution.py:27
  5.2 5.0 %collective-permute-done.first_ref.refs_1_ = bf16[128,1024]{1,0:T(8,128)(2,1)S(1)} collective-permute-done((bf16[128,1024]{1,0:T(8,128)(2,1)}, bf16[128,1024]{1,0:T(8,128)(2,1)S(1)}, u32[]{:S(2)}, u32[]{:S(2)}) %collective-permute-start) | collective-permute-done | bytes 262176 | tf_op jit(solution)/shard_map/ppermute | solution.py:27
  10.2 1.5 %collective-permute-done.1.second_ref.refs_2_ = bf16[128,1024]{1,0:T(8,128)(2,1)S(1)} collective-permute-done((bf16[128,1024]{1,0:T(8,128)(2,1)}, bf16[128,1024]{1,0:T(8,128)(2,1)S(1)}, u32[]{:S(2)}, u32[]{:S(2)}) %collective-permute-start.1) | collective-permute-done | bytes 262176 | tf_op jit(solution)/shard_map/ppermute | solution.py:27
  11.7 0.4 collective-permute-start.2
  12.1 1.7 %collective-permute-start.3 = (bf16[64,1024]{1,0:T(8,128)(2,1)S(1)}, bf16[64,1024]{1,0:T(8,128)(2,1)S(1)}, u32[]{:S(2)}, u32[]{:S(2)}) collective-permute-start(bf16[64,1024]{1,0:T(8,128)(2,1)S(1)} %get-tuple-element.43), channel_id=1, source_target_pairs={{0,2},{1,3},{2,0},{3,1},{4,6},{5,7},{6,4},{7,5},{8,10},{9,11},{10,... | collective-permute-start | bytes 393224 | tf_op jit(solution)/shard_map/ppermute | solution.py:27
  13.8 0.1 pad_add_fusion.ids_ref
  13.9 0.9 %copy-done.3 = bf16[1,128,1024]{2,1,0:T(8,128)(2,1)S(1)} copy-done((bf16[1,128,1024]{2,1,0:T(8,128)(2,1)S(1)}, bf16[1,128,1024]{2,1,0:T(8,128)(2,1)}, u32[]{:S(2)}) %copy-start.3) | copy-done | bytes 262168
  14.8 2.8 %shard_map.121 = (bf16[128,256]{1,0:T(8,128)(2,1)S(1)}, bf16[128,256]{1,0:T(8,128)(2,1)S(1)}, bf16[128,256]{1,0:T(8,128)(2,1)S(1)}, bf16[128,256]{1,0:T(8,128)(2,1)S(1)}) custom-call(s32[12]{0:T(128)S(1)} %pad_add_fusion.ids_ref, bf16[128,1024]{1,0:T(8,128)(2,1)S(1)} %bitcast.7, bf16[1024,1024]{1,0:T(8,128)(2,1)} %w_ref.1), custom_call_target="tpu_custom_call" | custom-call | flops 300000000 | bytes 3145728 | tf_op jit(solution)/shard_map/pallas_call | solution.py:442
  17.6 1.6 %collective-permute-start.4 = (bf16[128,256]{1,0:T(8,128)(2,1)S(1)}, bf16[128,256]{1,0:T(8,128)(2,1)S(1)}, u32[]{:S(2)}, u32[]{:S(2)}) collective-permute-start(bf16[128,256]{1,0:T(8,128)(2,1)S(1)} %get-tuple-element.45), channel_id=1, source_target_pairs={{0,1},{1,0},{2,3},{3,2},{4,5},{5,4},{6,7},{7,6},{8,9},{9,8},{10,11... | collective-permute-start | bytes 196616 | tf_op jit(solution)/shard_map/ppermute | solution.py:27
  19.1 0.5 collective-permute-start.5
  19.7 1.5 %collective-permute-start.6 = (bf16[128,256]{1,0:T(8,128)(2,1)S(1)}, bf16[128,256]{1,0:T(8,128)(2,1)S(1)}, u32[]{:S(2)}, u32[]{:S(2)}) collective-permute-start(bf16[128,256]{1,0:T(8,128)(2,1)S(1)} %get-tuple-element.47), channel_id=1, source_target_pairs={{0,3},{1,2},{2,1},{3,0},{4,7},{5,6},{6,5},{7,4},{8,11},{9,10},{10,... | collective-permute-start | bytes 196616 | tf_op jit(solution)/shard_map/ppermute | solution.py:27
  21.1 0.1 copy.13
  21.3 0.0 copy-start.7
  21.3 0.0 copy-start.8
  21.3 2.0 %shard_map.122 = (bf16[1024,128]{1,0:T(8,128)(2,1)S(1)}, bf16[1024,128]{1,0:T(8,128)(2,1)S(1)}, bf16[1024,128]{1,0:T(8,128)(2,1)S(1)}, bf16[1024,128]{1,0:T(8,12...) custom-call(s32[12]{0:T(128)S(1)} %pad_add_fusion.ids_ref, bf16[1024,1024]{1,0:T(8,128)(2,1)} %refs_4_.1, ...), custom_call_target="tpu_custom_call" | custom-call | bytes 3145728 | tf_op jit(solution)/shard_map/pallas_call | solution.py:442
  23.3 0.0 collective-permute-done.4.refs_6_
  23.3 0.0 copy-done.4
  23.3 1.6 %collective-permute-start.13 = (bf16[128,1024]{1,0:T(8,128)(2,1)S(1)}, bf16[128,1024]{1,0:T(8,128)(2,1)S(1)}, u32[]{:S(2)}, u32[]{:S(2)}) collective-permute-start(bf16[128,1024]{1,0:T(8,128)(2,1)S(1)} %bitcast.8), channel_id=1, source_target_pairs={{0,1},{1,0},{2,3},{3,2},{4,5},{5,4},{6,7},{7,6},{8,9},{9,8},{10,11... | collective-permute-start | bytes 786440 | tf_op jit(solution)/shard_map/ppermute | solution.py:27
  24.8 0.0 collective-permute-done.5.refs_7_
  24.9 0.6 collective-permute-start.14
  25.4 0.1 collective-permute-done.6.refs_8_
  25.5 1.5 %collective-permute-start.15 = (bf16[128,1024]{1,0:T(8,128)(2,1)S(1)}, bf16[128,1024]{1,0:T(8,128)(2,1)S(1)}, u32[]{:S(2)}, u32[]{:S(2)}) collective-permute-start(bf16[128,1024]{1,0:T(8,128)(2,1)S(1)} %bitcast.10), channel_id=1, source_target_pairs={{0,3},{1,2},{2,1},{3,0},{4,7},{5,6},{6,5},{7,4},{8,11},{9,10},{10,... | collective-permute-start | bytes 786440 | tf_op jit(solution)/shard_map/ppermute | solution.py:27
  27.0 0.0 collective-permute-done.2.refs_3_
  27.0 0.0 collective-permute-done.3.refs_4_
  27.0 0.0 copy-done.6
  27.0 0.0 copy-done.7
  27.0 0.0 copy-done.8
  27.0 4.0 %shard_map.123 = (bf16[384,512]{1,0:T(8,128)(2,1)S(1)}, bf16[128,512]{1,0:T(8,128)(2,1)S(1)}, f32[2,64]{1,0:T(2,128)S(1)}, f32[64,512]{1,0:T(8,128)S(1)}) custom-call(s32[12]{0:T(128)S(1)} %pad_add_fusion.ids_ref, s32[4,4,4]{2,1,0:T(4,128)S(1)} %bitcast.25, bf16[128,1024]{1,0:T(8,128)(2,1)S(1)} %bitcast.17, ...), custom_call_target="tpu_custom_call" | custom-call | flops 4000000000 | bytes 4194304 | tf_op jit(solution)/shard_map/pallas_call | solution.py:442
  31.0 4.1 %shard_map.124 = (bf16[384,512]{1,0:T(8,128)(2,1)S(1)}, bf16[128,512]{1,0:T(8,128)(2,1)S(1)}, f32[2,64]{1,0:T(2,128)S(1)}, f32[64,128]{1,0:T(8,128)S(1)}, bf16[8...) custom-call(s32[12]{0:T(128)S(1)} %pad_add_fusion.ids_ref, ...), custom_call_target="tpu_custom_call" | custom-call | flops 4000000000 | bytes 4194304 | tf_op jit(solution)/shard_map/pallas_call | solution.py:442
  35.0 0.0 collective-permute-done.13.refs_6_
  35.0 1.2 %collective-permute-done.14.refs_7_ = bf16[128,1024]{1,0:T(8,128)(2,1)S(1)} collective-permute-done((bf16[128,1024]{1,0:T(8,128)(2,1)S(1)}, bf16[128,1024]{1,0:T(8,128)(2,1)S(1)}, u32[]{:S(2)}, u32[]{:S(2)}) %collective-permute-start.14) | collective-permute-done | bytes 262176 | tf_op jit(solution)/shard_map/ppermute | solution.py:27
  36.2 0.0 collective-permute-done.15.refs_8_
  36.2 1.1 %shard_map.131 = bf16[4,640,128]{2,1,0:T(8,128)(2,1)S(1)} custom-call(s32[12]{0:T(128)S(1)} %pad_add_fusion.ids_ref, bf16[128,1024]{1,0:T(8,128)(2,1)S(1)} %bitcast.19, bf16[128,1024]{1,0:T(8,128)(2,1)S(1)} %collective-permute-done.first_ref.refs_1_, bf16[128,1024]{1,0:T(8,128)(2,1)S(1)} %collective-permute-done.1.second_ref.refs_2_, ...), custom_call_target="tpu_custom_call" | custom-call | flops 1000000000 | bytes 1048576 | tf_op jit(solution)/shard_map/pallas_call | solution.py:442
  37.4 0.1 collective-permute-start.16
  37.5 1.0 %shard_map.127 = bf16[4,384,128]{2,1,0:T(8,128)(2,1)S(1)} custom-call(s32[12]{0:T(128)S(1)} %pad_add_fusion.ids_ref, bf16[128,1024]{1,0:T(8,128)(2,1)S(1)} %bitcast.20, bf16[128,1024]{1,0:T(8,128)(2,1)S(1)} %collective-permute-done.first_ref.refs_1_, bf16[128,1024]{1,0:T(8,128)(2,1)S(1)} %collective-permute-done.1.second_ref.refs_2_, ...), custom_call_target="tpu_custom_call" | custom-call | flops 1000000000 | bytes 1048576 | tf_op jit(solution)/shard_map/pallas_call | solution.py:442
  38.4 0.6 collective-permute-start.10
  39.0 0.1 collective-permute-start.17
  39.1 1.1 %shard_map.130.keep_ref = bf16[4,640,128]{2,1,0:T(8,128)(2,1)S(1)} custom-call(s32[12]{0:T(128)S(1)} %pad_add_fusion.ids_ref, bf16[128,1024]{1,0:T(8,128)(2,1)S(1)} %bitcast.21, bf16[128,1024]{1,0:T(8,128)(2,1)S(1)} %collective-permute-done.first_ref.refs_1_, bf16[128,1024]{1,0:T(8,128)(2,1)S(1)} %collective-permute-done.1.second_ref.refs_2_, ...), custom_call_target="tpu_custom_call" | custom-call | flops 1000000000 | bytes 1048576 | tf_op jit(solution)/shard_map/pallas_call | solution.py:442
  40.2 0.1 collective-permute-done.17.refs_2_
  40.4 0.0 collective-permute-done.16.got_ref
  40.4 0.1 shard_map.132
  40.5 1.6 %collective-permute-start.18 = (bf16[1296,128]{1,0:T(8,128)(2,1)S(1)}, bf16[1296,128]{1,0:T(8,128)(2,1)S(1)}, u32[]{:S(2)}, u32[]{:S(2)}) collective-permute-start(bf16[1296,128]{1,0:T(8,128)(2,1)S(1)} %get-tuple-element.73), channel_id=1, source_target_pairs={{0,8},{4,12},{8,0},{12,4},{16,24},{20,28},{24,16},{28,20},{1,9},{5... | collective-permute-start | bytes 995336 | tf_op jit(solution)/shard_map/ppermute | solution.py:27
  42.1 0.6 collective-permute-start.7
  42.8 1.2 %collective-permute-start.8 = (bf16[832,128]{1,0:T(8,128)(2,1)S(1)}, bf16[832,128]{1,0:T(8,128)(2,1)S(1)}, u32[]{:S(2)}, u32[]{:S(2)}) collective-permute-start(bf16[832,128]{1,0:T(8,128)(2,1)S(1)} %get-tuple-element.59), channel_id=1, source_target_pairs={{0,2},{1,3},{2,0},{3,1},{4,6},{5,7},{6,4},{7,5},{8,10},{9,11},{10,... | collective-permute-start | bytes 638984 | tf_op jit(solution)/shard_map/ppermute | solution.py:27
  44.0 1.6 %collective-permute-start.9 = (bf16[832,128]{1,0:T(8,128)(2,1)S(1)}, bf16[832,128]{1,0:T(8,128)(2,1)S(1)}, u32[]{:S(2)}, u32[]{:S(2)}) collective-permute-start(bf16[832,128]{1,0:T(8,128)(2,1)S(1)} %get-tuple-element.60), channel_id=1, source_target_pairs={{0,3},{1,2},{2,1},{3,0},{4,7},{5,6},{6,5},{7,4},{8,11},{9,10},{10,... | collective-permute-start | bytes 638984 | tf_op jit(solution)/shard_map/ppermute | solution.py:27
  45.6 1.0 %shard_map.126.keep_ref = bf16[4,384,128]{2,1,0:T(8,128)(2,1)S(1)} custom-call(s32[12]{0:T(128)S(1)} %pad_add_fusion.ids_ref, bf16[128,1024]{1,0:T(8,128)(2,1)S(1)} %bitcast.22, bf16[128,1024]{1,0:T(8,128)(2,1)S(1)} %collective-permute-done.first_ref.refs_1_, bf16[128,1024]{1,0:T(8,128)(2,1)S(1)} %collective-permute-done.1.second_ref.refs_2_, ...), custom_call_target="tpu_custom_call" | custom-call | flops 1000000000 | bytes 1048576 | tf_op jit(solution)/shard_map/pallas_call | solution.py:442
  46.6 0.0 copy-start
  46.6 0.0 collective-permute-done.10.got_ref
  46.6 0.1 shard_map.128
  46.7 0.5 collective-permute-start.11
  47.3 4.0 %collective-permute-done.18.got_ref = bf16[1296,128]{1,0:T(8,128)(2,1)S(1)} collective-permute-done((bf16[1296,128]{1,0:T(8,128)(2,1)S(1)}, bf16[1296,128]{1,0:T(8,128)(2,1)S(1)}, u32[]{:S(2)}, u32[]{:S(2)}) %collective-permute-start.18) | collective-permute-done | bytes 331808 | tf_op jit(solution)/shard_map/ppermute | solution.py:27
  51.2 0.1 shard_map.133
  51.3 2.6 %collective-permute-start.19 = (bf16[656,128]{1,0:T(8,128)(2,1)S(1)}, bf16[656,128]{1,0:T(8,128)(2,1)S(1)}, u32[]{:S(2)}, u32[]{:S(2)}) collective-permute-start(bf16[656,128]{1,0:T(8,128)(2,1)S(1)} %get-tuple-element.76), channel_id=1, source_target_pairs={{0,16},{4,20},{8,24},{12,28},{16,0},{20,4},{24,8},{28,12},{1,17},{... | collective-permute-start | bytes 503816 | tf_op jit(solution)/shard_map/ppermute | solution.py:27
  54.0 3.9 %collective-permute-done.11.got_ref = bf16[768,128]{1,0:T(8,128)(2,1)S(1)} collective-permute-done((bf16[768,128]{1,0:T(8,128)(2,1)S(1)}, bf16[768,128]{1,0:T(8,128)(2,1)S(1)}, u32[]{:S(2)}, u32[]{:S(2)}) %collective-permute-start.11) | collective-permute-done | bytes 196640 | tf_op jit(solution)/shard_map/ppermute | solution.py:27
  57.9 0.3 collective-permute-start.12
  58.1 0.0 collective-permute-done.7.refs_1_
  58.1 0.0 collective-permute-done.8.refs_2_
  58.1 0.0 collective-permute-done.9.refs_3_
  58.2 0.0 copy-done.2
  58.2 3.2 %shard_map.125 = (bf16[128,1024]{1,0:T(8,128)(2,1)}, f32[64,128]{1,0:T(8,128)}) custom-call(s32[12]{0:T(128)S(1)} %pad_add_fusion.ids_ref, f32[64,128]{1,0:T(8,128)S(1)} %get-tuple-element.56.eig_ref, bf16[832,128]{1,0:T(8,128)(2,1)S(1)} %get-tuple-element.57.refs_0_, bf16[832,128]{1,0:T(8,128)(2,1)S(1)} %collective-permute-done.7.refs_1_, ...), custom_call_target="tpu_custom_call" | custom-call | flops 1000000000 | bytes 7340032 | tf_op jit(solution)/shard_map/pallas_call | solution.py:442
  61.4 4.1 %collective-permute-done.12.refs_1_ = bf16[384,128]{1,0:T(8,128)(2,1)S(1)} collective-permute-done((bf16[384,128]{1,0:T(8,128)(2,1)S(1)}, bf16[384,128]{1,0:T(8,128)(2,1)S(1)}, u32[]{:S(2)}, u32[]{:S(2)}) %collective-permute-start.12) | collective-permute-done | bytes 98336 | tf_op jit(solution)/shard_map/ppermute | solution.py:27
  65.4 0.0 collective-permute-done.19.refs_3_
  65.5 1.0 %shard_map.134 = (f32[4,128,256]{2,1,0:T(8,128)}, f32[4,64]{1,0:T(4,128)}) custom-call(f32[384,128]{1,0:T(8,128)S(1)} %get-tuple-element.65.refs_0_, bf16[384,128]{1,0:T(8,128)(2,1)S(1)} %collective-permute-done.12.refs_1_, f32[640,128]{1,0:T(8,128)S(1)} %get-tuple-element.75.refs_2_, bf16[656,128]{1,0:T(8,128)(2,1)S(1)} %collective-permute-done.19.refs_3_, ...), custom_call_target="tpu_custom_call" | custom-call | flops 1000000 | bytes 2097152 | tf_op jit(solution)/shard_map/pallas_call | solution.py:442
  (14 shorter events, 0.1 us)
Async XLA Ops:
  0.6 20.5 %copy-start.5 = (f32[4,64]{1,0:T(4,128)S(1)}, f32[4,64]{1,0:T(4,128)}, u32[]{:S(2)}) copy-start(f32[4,64]{1,0:T(4,128)} %refs_13_.3) | copy-start | bytes 3076
  0.6 9.6 %collective-permute-start = (bf16[128,1024]{1,0:T(8,128)(2,1)}, bf16[128,1024]{1,0:T(8,128)(2,1)S(1)}, u32[]{:S(2)}, u32[]{:S(2)}) collective-permute-start(bf16[128,1024]{1,0:T(8,128)(2,1)} %bitcast.15), channel_id=1, source_target_pairs={{0,1},{1,0},{2,3},{3,2},{4,5},{5,4},{6,7},{7,6},{8,9},{9,8},{10,11... | collective-permute-start | bytes 786440 | tf_op jit(solution)/shard_map/ppermute | solution.py:27
  3.7 8.0 %collective-permute-start.1 = (bf16[128,1024]{1,0:T(8,128)(2,1)}, bf16[128,1024]{1,0:T(8,128)(2,1)S(1)}, u32[]{:S(2)}, u32[]{:S(2)}) collective-permute-start(bf16[128,1024]{1,0:T(8,128)(2,1)} %bitcast.16), channel_id=1, source_target_pairs={{0,2},{1,3},{2,0},{3,1},{4,6},{5,7},{6,4},{7,5},{8,10},{9,11},{10,... | collective-permute-start | bytes 786440 | tf_op jit(solution)/shard_map/ppermute | solution.py:27
  11.7 15.3 %collective-permute-start.2 = (bf16[64,1024]{1,0:T(8,128)(2,1)S(1)}, bf16[64,1024]{1,0:T(8,128)(2,1)S(1)}, u32[]{:S(2)}, u32[]{:S(2)}) collective-permute-start(bf16[64,1024]{1,0:T(8,128)(2,1)S(1)} %get-tuple-element.42), channel_id=1, source_target_pairs={{0,1},{1,0},{2,3},{3,2},{4,5},{5,4},{6,7},{7,6},{8,9},{9,8},{10,11... | collective-permute-start | bytes 393224 | tf_op jit(solution)/shard_map/ppermute | solution.py:27
  12.1 14.9 %collective-permute-start.3 = (bf16[64,1024]{1,0:T(8,128)(2,1)S(1)}, bf16[64,1024]{1,0:T(8,128)(2,1)S(1)}, u32[]{:S(2)}, u32[]{:S(2)}) collective-permute-start(bf16[64,1024]{1,0:T(8,128)(2,1)S(1)} %get-tuple-element.43), channel_id=1, source_target_pairs={{0,2},{1,3},{2,0},{3,1},{4,6},{5,7},{6,4},{7,5},{8,10},{9,11},{10,... | collective-permute-start | bytes 393224 | tf_op jit(solution)/shard_map/ppermute | solution.py:27
  13.9 0.9 %copy-start.3 = (bf16[1,128,1024]{2,1,0:T(8,128)(2,1)S(1)}, bf16[1,128,1024]{2,1,0:T(8,128)(2,1)}, u32[]{:S(2)}) copy-start(bf16[1,128,1024]{2,1,0:T(8,128)(2,1)} %param.10) | copy-start | bytes 786436
  17.6 5.7 %collective-permute-start.4 = (bf16[128,256]{1,0:T(8,128)(2,1)S(1)}, bf16[128,256]{1,0:T(8,128)(2,1)S(1)}, u32[]{:S(2)}, u32[]{:S(2)}) collective-permute-start(bf16[128,256]{1,0:T(8,128)(2,1)S(1)} %get-tuple-element.45), channel_id=1, source_target_pairs={{0,1},{1,0},{2,3},{3,2},{4,5},{5,4},{6,7},{7,6},{8,9},{9,8},{10,11... | collective-permute-start | bytes 196616 | tf_op jit(solution)/shard_map/ppermute | solution.py:27
  19.1 5.7 %collective-permute-start.5 = (bf16[128,256]{1,0:T(8,128)(2,1)S(1)}, bf16[128,256]{1,0:T(8,128)(2,1)S(1)}, u32[]{:S(2)}, u32[]{:S(2)}) collective-permute-start(bf16[128,256]{1,0:T(8,128)(2,1)S(1)} %get-tuple-element.46), channel_id=1, source_target_pairs={{0,2},{1,3},{2,0},{3,1},{4,6},{5,7},{6,4},{7,5},{8,10},{9,11},{10,... | collective-permute-start | bytes 196616 | tf_op jit(solution)/shard_map/ppermute | solution.py:27
  19.7 5.9 %collective-permute-start.6 = (bf16[128,256]{1,0:T(8,128)(2,1)S(1)}, bf16[128,256]{1,0:T(8,128)(2,1)S(1)}, u32[]{:S(2)}, u32[]{:S(2)}) collective-permute-start(bf16[128,256]{1,0:T(8,128)(2,1)S(1)} %get-tuple-element.47), channel_id=1, source_target_pairs={{0,3},{1,2},{2,1},{3,0},{4,7},{5,6},{6,5},{7,4},{8,11},{9,10},{10,... | collective-permute-start | bytes 196616 | tf_op jit(solution)/shard_map/ppermute | solution.py:27
  21.2 2.0 %copy-start.4 = (bf16[1,128,1024]{2,1,0:T(8,128)(2,1)S(1)}, bf16[1,128,1024]{2,1,0:T(8,128)(2,1)}, u32[]{:S(2)}) copy-start(bf16[1,128,1024]{2,1,0:T(8,128)(2,1)} %param.10) | copy-start | bytes 786436
  21.2 5.7 %copy-start.6 = (bf16[1,128,1024]{2,1,0:T(8,128)(2,1)S(1)}, bf16[1,128,1024]{2,1,0:T(8,128)(2,1)}, u32[]{:S(2)}) copy-start(bf16[1,128,1024]{2,1,0:T(8,128)(2,1)} %param.9) | copy-start | bytes 786436
  21.3 5.7 %copy-start.7 = (bf16[1,64,512]{2,1,0:T(8,128)(2,1)S(1)}, bf16[1,64,512]{2,1,0:T(8,128)(2,1)}, u32[]{:S(2)}) copy-start(bf16[1,64,512]{2,1,0:T(8,128)(2,1)} %param.15) | copy-start | bytes 196612
  21.3 5.7 %copy-start.8 = (s32[1,4,4,4]{3,2,1,0:T(4,128)S(1)}, s32[1,4,4,4]{3,2,1,0:T(4,128)}, u32[]{:S(2)}) copy-start(s32[1,4,4,4]{3,2,1,0:T(4,128)} %param.17) | copy-start | bytes 772
  23.3 11.7 %collective-permute-start.13 = (bf16[128,1024]{1,0:T(8,128)(2,1)S(1)}, bf16[128,1024]{1,0:T(8,128)(2,1)S(1)}, u32[]{:S(2)}, u32[]{:S(2)}) collective-permute-start(bf16[128,1024]{1,0:T(8,128)(2,1)S(1)} %bitcast.8), channel_id=1, source_target_pairs={{0,1},{1,0},{2,3},{3,2},{4,5},{5,4},{6,7},{7,6},{8,9},{9,8},{10,11... | collective-permute-start | bytes 786440 | tf_op jit(solution)/shard_map/ppermute | solution.py:27
  24.9 11.4 %collective-permute-start.14 = (bf16[128,1024]{1,0:T(8,128)(2,1)S(1)}, bf16[128,1024]{1,0:T(8,128)(2,1)S(1)}, u32[]{:S(2)}, u32[]{:S(2)}) collective-permute-start(bf16[128,1024]{1,0:T(8,128)(2,1)S(1)} %bitcast.9), channel_id=1, source_target_pairs={{0,2},{1,3},{2,0},{3,1},{4,6},{5,7},{6,4},{7,5},{8,10},{9,11},{10,... | collective-permute-start | bytes 786440 | tf_op jit(solution)/shard_map/ppermute | solution.py:27
  25.5 10.7 %collective-permute-start.15 = (bf16[128,1024]{1,0:T(8,128)(2,1)S(1)}, bf16[128,1024]{1,0:T(8,128)(2,1)S(1)}, u32[]{:S(2)}, u32[]{:S(2)}) collective-permute-start(bf16[128,1024]{1,0:T(8,128)(2,1)S(1)} %bitcast.10), channel_id=1, source_target_pairs={{0,3},{1,2},{2,1},{3,0},{4,7},{5,6},{6,5},{7,4},{8,11},{9,10},{10,... | collective-permute-start | bytes 786440 | tf_op jit(solution)/shard_map/ppermute | solution.py:27
  37.4 3.0 %collective-permute-start.16 = (bf16[4,640,128]{2,1,0:T(8,128)(2,1)S(1)}, bf16[4,640,128]{2,1,0:T(8,128)(2,1)S(1)}, u32[]{:S(2)}, u32[]{:S(2)}) collective-permute-start(bf16[4,640,128]{2,1,0:T(8,128)(2,1)S(1)} %shard_map.131), channel_id=1, source_target_pairs={{0,4},{4,0},{8,12},{12,8},{16,20},{20,16},{24,28},{28,24},{1,5},{5... | collective-permute-start | bytes 1966088 | tf_op jit(solution)/shard_map/ppermute | solution.py:27
  38.4 8.2 %collective-permute-start.10 = (bf16[4,384,128]{2,1,0:T(8,128)(2,1)S(1)}, bf16[4,384,128]{2,1,0:T(8,128)(2,1)S(1)}, u32[]{:S(2)}, u32[]{:S(2)}) collective-permute-start(bf16[4,384,128]{2,1,0:T(8,128)(2,1)S(1)} %shard_map.127), channel_id=1, source_target_pairs={{0,4},{4,0},{8,12},{12,8},{16,20},{20,16},{24,28},{28,24},{1,5},{5... | collective-permute-start | bytes 1179656 | tf_op jit(solution)/shard_map/ppermute | solution.py:27
  39.0 1.3 %collective-permute-start.17 = (f32[4,64]{1,0:T(4,128)S(1)}, f32[4,64]{1,0:T(4,128)S(1)}, u32[]{:S(2)}, u32[]{:S(2)}) collective-permute-start(f32[4,64]{1,0:T(4,128)S(1)} %pad_maximum_fusion), channel_id=1, source_target_pairs={{0,4},{4,0},{8,12},{12,8},{16,20},{20,16},{24,28},{28,24},{1,5},{5... | collective-permute-start | bytes 3080 | tf_op jit(solution)/shard_map/ppermute | solution.py:27
  40.4 17.8 %copy-start.2 = (bf16[1024,1024]{1,0:T(8,128)(2,1)S(1)}, bf16[1024,1024]{1,0:T(8,128)(2,1)}, u32[]{:S(2)}) copy-start(bf16[1024,1024]{1,0:T(8,128)(2,1)} %refs_6_.1) | copy-start | bytes 6291460
  40.5 10.7 %collective-permute-start.18 = (bf16[1296,128]{1,0:T(8,128)(2,1)S(1)}, bf16[1296,128]{1,0:T(8,128)(2,1)S(1)}, u32[]{:S(2)}, u32[]{:S(2)}) collective-permute-start(bf16[1296,128]{1,0:T(8,128)(2,1)S(1)} %get-tuple-element.73), channel_id=1, source_target_pairs={{0,8},{4,12},{8,0},{12,4},{16,24},{20,28},{24,16},{28,20},{1,9},{5... | collective-permute-start | bytes 995336 | tf_op jit(solution)/shard_map/ppermute | solution.py:27
  42.1 16.0 %collective-permute-start.7 = (bf16[832,128]{1,0:T(8,128)(2,1)S(1)}, bf16[832,128]{1,0:T(8,128)(2,1)S(1)}, u32[]{:S(2)}, u32[]{:S(2)}) collective-permute-start(bf16[832,128]{1,0:T(8,128)(2,1)S(1)} %get-tuple-element.58), channel_id=1, source_target_pairs={{0,1},{1,0},{2,3},{3,2},{4,5},{5,4},{6,7},{7,6},{8,9},{9,8},{10,11... | collective-permute-start | bytes 638984 | tf_op jit(solution)/shard_map/ppermute | solution.py:27
  42.8 15.4 %collective-permute-start.8 = (bf16[832,128]{1,0:T(8,128)(2,1)S(1)}, bf16[832,128]{1,0:T(8,128)(2,1)S(1)}, u32[]{:S(2)}, u32[]{:S(2)}) collective-permute-start(bf16[832,128]{1,0:T(8,128)(2,1)S(1)} %get-tuple-element.59), channel_id=1, source_target_pairs={{0,2},{1,3},{2,0},{3,1},{4,6},{5,7},{6,4},{7,5},{8,10},{9,11},{10,... | collective-permute-start | bytes 638984 | tf_op jit(solution)/shard_map/ppermute | solution.py:27
  44.0 14.1 %collective-permute-start.9 = (bf16[832,128]{1,0:T(8,128)(2,1)S(1)}, bf16[832,128]{1,0:T(8,128)(2,1)S(1)}, u32[]{:S(2)}, u32[]{:S(2)}) collective-permute-start(bf16[832,128]{1,0:T(8,128)(2,1)S(1)} %get-tuple-element.60), channel_id=1, source_target_pairs={{0,3},{1,2},{2,1},{3,0},{4,7},{5,6},{6,5},{7,4},{8,11},{9,10},{10,... | collective-permute-start | bytes 638984 | tf_op jit(solution)/shard_map/ppermute | solution.py:27
  45.6 12.5 %copy-start.1 = (bf16[1024,1024]{1,0:T(8,128)(2,1)S(1)}, bf16[1024,1024]{1,0:T(8,128)(2,1)}, u32[]{:S(2)}) copy-start(bf16[1024,1024]{1,0:T(8,128)(2,1)} %refs_5_.1) | copy-start | bytes 6291460
  46.6 11.6 %copy-start = (bf16[1024,1024]{1,0:T(8,128)(2,1)S(1)}, bf16[1024,1024]{1,0:T(8,128)(2,1)}, u32[]{:S(2)}) copy-start(bf16[1024,1024]{1,0:T(8,128)(2,1)} %refs_4_.1) | copy-start | bytes 6291460
  46.7 11.1 %collective-permute-start.11 = (bf16[768,128]{1,0:T(8,128)(2,1)S(1)}, bf16[768,128]{1,0:T(8,128)(2,1)S(1)}, u32[]{:S(2)}, u32[]{:S(2)}) collective-permute-start(bf16[768,128]{1,0:T(8,128)(2,1)S(1)} %get-tuple-element.64), channel_id=1, source_target_pairs={{0,8},{4,12},{8,0},{12,4},{16,24},{20,28},{24,16},{28,20},{1,9},{5... | collective-permute-start | bytes 589832 | tf_op jit(solution)/shard_map/ppermute | solution.py:27
  51.3 14.1 %collective-permute-start.19 = (bf16[656,128]{1,0:T(8,128)(2,1)S(1)}, bf16[656,128]{1,0:T(8,128)(2,1)S(1)}, u32[]{:S(2)}, u32[]{:S(2)}) collective-permute-start(bf16[656,128]{1,0:T(8,128)(2,1)S(1)} %get-tuple-element.76), channel_id=1, source_target_pairs={{0,16},{4,20},{8,24},{12,28},{16,0},{20,4},{24,8},{28,12},{1,17},{... | collective-permute-start | bytes 503816 | tf_op jit(solution)/shard_map/ppermute | solution.py:27
  57.9 7.6 %collective-permute-start.12 = (bf16[384,128]{1,0:T(8,128)(2,1)S(1)}, bf16[384,128]{1,0:T(8,128)(2,1)S(1)}, u32[]{:S(2)}, u32[]{:S(2)}) collective-permute-start(bf16[384,128]{1,0:T(8,128)(2,1)S(1)} %get-tuple-element.66), channel_id=1, source_target_pairs={{0,16},{4,20},{8,24},{12,28},{16,0},{20,4},{24,8},{28,12},{1,17},{... | collective-permute-start | bytes 294920 | tf_op jit(solution)/shard_map/ppermute | solution.py:27

commit v3 on v2

--- a/solution.py
+++ b/solution.py
@@ -47,14 +47,26 @@
 
 
 def out_grad_kernel(count, width, ids_ref, rows_ref, w_ref, *refs):
-    out_refs, (held, sems) = refs[:count], refs[count:]
+    sources, out_refs, targets = refs[:3], refs[3 : 3 + count], refs[3 + count : 6 + count]
+    rows, held, sems = refs[6 + count :]
+    row_copy = pltpu.make_async_copy(rows_ref, rows, sems.at[count + 3])
+    row_copy.start()
     order = list(range(count - 1, -1, -1))
     copies = {s: column_copy(w_ref, ids_ref[s], width, held.at[s], sems.at[s]) for s in order}
     for s in order:
         copies[s].start()
+    others = [
+        column_copy(sources[a], ids_ref[0], width, targets[a], sems.at[count + a])
+        for a in range(3)
+    ]
+    for c in others:
+        c.start()
+    row_copy.wait()
     for s in order:
         copies[s].wait()
-        out_refs[s][...] = mm(rows_ref[...], held[s]).astype(BF16)
+        out_refs[s][...] = mm(rows[...], held[s]).astype(BF16)
+    for c in others:
+        c.wait()
 
 
 def split_kernel(first_ref, second_ref, top_ref, bottom_ref):
@@ -63,38 +75,12 @@
     bottom_ref[...] = first_ref[half:]
 
 
-def weights_kernel(width, calls, ids_ref, *refs):
-    sources, targets, sems = refs[:3], refs[3:-1], refs[-1]
-    copies = []
-    for c in range(calls):
-        for a in range(3):
-            at = 3 * c + a
-            if calls == 1:
-                copies.append(column_copy(sources[a], ids_ref[0], width, targets[at], sems.at[at]))
-            else:
-                copies.append(
-                    column_copy(
-                        sources[a],
-                        ids_ref[0] * calls + c,
-                        width // calls,
-                        targets[at],
-                        sems.at[at],
-                    )
-                )
-    for c in copies:
-        c.start()
-    for c in copies:
-        c.wait()
-
-
-def attention_kernel(scale, heads, head_size, blocks, pieces, base, last, ids_ref, mask_ref, *refs):
+def attention_kernel(scale, heads, head_size, blocks, pieces, ids_ref, mask_ref, *refs):
     row_refs, d_refs = refs[:pieces], refs[pieces : pieces + blocks]
     refs = refs[pieces + blocks :]
     wq_ref, wk_ref, wv_ref, eig_ref, lam_ref, lam_t_ref = refs[:6]
-    earlier = base // heads
-    prior_refs, refs = refs[6 : 6 + 2 * earlier], refs[6 + 2 * earlier :]
-    grads_ref, out_ref, gw_ref = refs[:3]
-    result_refs = refs[3:-5]
+    grads_ref, out_ref, gw_ref, eig_out = refs[6:10]
+    ret_refs = refs[10:-5]
     qe, qn, dt, dn, left_acc = refs[-5:]
     eig_count, nodes = eig_ref.shape
     width = heads * head_size
@@ -123,10 +109,7 @@
     query = fit(mm(rows, wq_ref[...]).astype(BF16))
     keys = fit(mm(rows, wk_ref[...]).astype(BF16))
     values = fit(mm(rows, wv_ref[...]).astype(BF16))
-    first_column = base * head_size
-    d_att = fit(
-        jnp.concatenate([r[:, first_column : first_column + width] for r in d_refs], axis=0)
-    )
+    d_att = fit(jnp.concatenate([r[...] for r in d_refs], axis=0))
     query_t = (query.astype(F32) * scale).astype(BF16).T
     keys_t = keys.T
     values_t = values.T
@@ -169,7 +152,7 @@
             for j in range(tile_count):
                 j_at = ids_ref[j // per] * per + j % per
                 part = scores[j * tile : (j + 1) * tile, i * tile : (i + 1) * tile]
-                found.append(jnp.where(mask_ref[base + head, i_at, j_at] > 0, part, -jnp.inf))
+                found.append(jnp.where(mask_ref[head, i_at, j_at] > 0, part, -jnp.inf))
             columns.append(jnp.concatenate(found, axis=0))
         masked = jnp.concatenate(columns, axis=1)
         top = jnp.max(masked, axis=0, keepdims=True)
@@ -184,7 +167,7 @@
         dscore = (prob * (dprob - delta)).astype(BF16)
         left = mm(kt, dscore)
         grads_ref[first : first + head_size, here] = (left[:head_size] * scale).astype(BF16)
-        weighted = lam_t_ref[:, base + head : base + head + 1] * left[head_size:]
+        weighted = lam_t_ref[:, head : head + 1] * left[head_size:]
         if head == 0:
             left_acc[:, here] = weighted
         else:
@@ -198,7 +181,7 @@
         even, g = h % 2 == 0, h // 2
         group = slice(g * both, (g + 1) * both)
         part = slice(h * head_size, (h + 1) * head_size)
-        lam_row = jnp.concatenate([lam_ref[base + h : base + h + 1, :]] * 2, axis=1)
+        lam_row = jnp.concatenate([lam_ref[h : h + 1, :]] * 2, axis=1)
         kw = pick(even, keys[:, group], (wide * lam_row).astype(BF16))
         kt = jnp.concatenate([keys_t[part], eig], axis=0)
         vn = pick(even, values[:, group], jnp.zeros((nodes, both), BF16))
@@ -262,24 +245,15 @@
 
     flat = right_total.T
     eig_sum = left_acc[...] + flat[:head_size] + flat[head_size:]
-    if not last:
-        result_refs[0][...] = eig_sum
-        return
-    for r in prior_refs[1::2]:
-        eig_sum += r[...]
-    result_refs[0][...] = eig_sum[:, :size]
+    eig_out[...] = eig_sum[:, :size]
     for b in range(blocks):
         part = slice(b * size, (b + 1) * size)
-        ret_ref, at = result_refs[1 + b], 0
-        for r in (*prior_refs[::2], grads_ref):
-            ret_ref[at : at + r.shape[0]] = r[:, part]
-            at += r.shape[0]
-        ret_ref[at:] = eig_sum[:, part].astype(BF16)
-
-
-def terms_kernel(base, pieces, outs, target, ids_ref, *refs):
-    row_refs, refs = refs[:pieces], refs[pieces:]
-    cot_refs, (grads_ref, *head_outs, out_ref) = refs[: -2 - outs], refs[-2 - outs :]
+        ret_refs[b][: 3 * width] = grads_ref[:, part]
+        ret_refs[b][3 * width :] = eig_sum[:, part].astype(BF16)
+
+
+def terms_kernel(base, pieces, target, ids_ref, *refs):
+    row_refs, (grads_ref, out_ref) = refs[:pieces], refs[pieces:]
     count = out_ref.shape[0]
 
     def columns(ref, index):
@@ -301,15 +275,9 @@
     group = 2 if count % 2 == 0 else 1
     for start in range(0, count, group):
         at = [ids_ref[base + start + i] for i in range(group)]
-        found = [mm(grads_ref[...], right_of(row_refs, at)).astype(BF16)]
-        if outs:
-            right = right_of(cot_refs, at)
-            found += [mm(r[...], right).astype(BF16) for r in head_outs]
-        row = 0
-        for value in found:
-            for i in range(group):
-                out_ref[start + i, row : row + value.shape[0]] = value[:, i * target : (i + 1) * target]
-            row += value.shape[0]
+        value = mm(grads_ref[...], right_of(row_refs, at)).astype(BF16)
+        for i in range(group):
+            out_ref[start + i] = value[:, i * target : (i + 1) * target]
 
 
 def put_sums(ref, base, sums):
@@ -328,7 +296,7 @@
 
 def pair_kernel(sums, keep_ref, got_ref, *refs):
     if sums:
-        gw_refs, gw_got_ref, give_ref, near_ref, gw_out = refs[:sums], *refs[sums:]
+        gw_ref, gw_got_ref, give_ref, near_ref, gw_out = refs
     else:
         give_ref, near_ref = refs
     count, rows, _ = keep_ref.shape
@@ -339,7 +307,7 @@
         else:
             give_ref[s // 2 * rows : (s // 2 + 1) * rows] = total.astype(BF16)
     if sums:
-        total = jnp.concatenate([r[...] for r in gw_refs], axis=0) + gw_got_ref[...]
+        total = gw_ref[...] + gw_got_ref[...]
         gw_out[...] = total
         put_sums(give_ref, count // 2 * rows, total)
 
@@ -361,39 +329,35 @@
             put_sums(ref, rows, total)
 
 
-def final_kernel(calls, count, *refs):
-    groups, gw_ref, (out_ref, gw_out) = [], refs[-3], refs[-2:]
-    for c in range(calls):
-        at = c * (count + 1)
-        groups.append((refs[at], refs[at + 1 : at + 1 + count]))
-    width = out_ref.shape[2] // calls
-    for c, (own_ref, piece_refs) in enumerate(groups):
+def final_kernel(count, *refs):
+    gw_ref, out_ref, gw_out = refs[-3:]
+    width = out_ref.shape[2]
+    found = []
+    for c in range(2):
+        own_ref, *piece_refs = refs[c * (count + 1) : (c + 1) * (count + 1)]
+        rows = own_ref.shape[0]
         total = own_ref[...]
-        rows = total.shape[0]
         for r in piece_refs:
             total += r[:rows].astype(F32)
-        for a in range(3):
-            out_ref[a, :, c * width : (c + 1) * width] = total[a * width : (a + 1) * width].T
-        if c == calls - 1:
-            out_ref[3] = total[3 * width :].T
+        found += [total[at : at + width] for at in range(0, rows, width)]
+        if c == 0:
             sums = gw_ref[...]
             for r in piece_refs:
                 sums += get_sums(r, rows, sums.shape)
             gw_out[...] = sums
-
-
-def nodes_kernel(blocks, width, calls, ids_ref, eig_ref, *refs):
+    for a, total in enumerate(found):
+        out_ref[a] = total.T
+
+
+def nodes_kernel(blocks, width, ids_ref, eig_ref, *refs):
     ret_refs = refs[:blocks]
     w_refs = refs[blocks : blocks + 3]
     out_ref, eig_out, joined = refs[blocks + 3 :]
     total = eig_ref[...]
     for s in range(blocks):
-        part = width // calls
-        for c in range(calls):
-            at = pl.multiple_of(ids_ref[s] * width + c * part, part)
-            for a in range(3):
-                row = (3 * c + a) * part
-                joined[a, pl.ds(at, part)] = ret_refs[s][row : row + part]
+        at = pl.multiple_of(ids_ref[s] * width, width)
+        for a in range(3):
+            joined[a, pl.ds(at, width)] = ret_refs[s][a * width : (a + 1) * width]
         if s > 0:
             total += ret_refs[s][3 * width :].astype(F32)
     eig_out[...] = total
@@ -455,15 +419,27 @@
         if s < 3 or not crossed:
             rows[s] = take(own_rows, "node", s, node_size)
 
-    d_parts = call(
+    def held(array):
+        return pltpu.with_memory_space_constraint(array, pltpu.HBM)
+
+    made = call(
         functools.partial(out_grad_kernel, node_size, width),
-        [smem, vmem, hbm],
-        [((size, width), BF16)] * node_size,
-        (ids, own_cot, pltpu.with_memory_space_constraint(column_blocks(w_out, width), pltpu.HBM)),
+        [smem] + [hbm] * 5,
+        [((size, width), BF16)] * node_size + [((model, width), BF16)] * 3,
+        (
+            ids,
+            held(own_cot),
+            *[held(column_blocks(w, width)) for w in (w_out, w_query, w_key, w_value)],
+        ),
         3 * 10**8,
         3 * 2**20,
-        [pltpu.VMEM((node_size, model, width), BF16), pltpu.SemaphoreType.DMA((node_size,))],
+        [
+            pltpu.VMEM((size, model), BF16),
+            pltpu.VMEM((node_size, model, width), BF16),
+            pltpu.SemaphoreType.DMA((node_size + 4,)),
+        ],
     )
+    d_parts, weights = made[:node_size], made[node_size:]
     d_att = [d_parts[0]] + [None] * (node_size - 1)
     for s in far_first:
         d_att[s] = give(d_parts[s], "node", s, node_size)
@@ -476,141 +452,88 @@
     for s in far_first:
         cots[s] = take(own_cot, "node", s, node_size)
 
-    calls = -(-heads // 2)
-    sub_heads = heads // calls
-    part_width = width // calls
-    assert sub_heads * calls == heads
-    weights = call(
-        functools.partial(weights_kernel, width, calls),
-        [smem] + [hbm] * 3,
-        [((model, part_width), BF16)] * (3 * calls),
-        (
-            ids,
-            *[
-                pltpu.with_memory_space_constraint(column_blocks(w, width), pltpu.HBM)
-                for w in (w_query, w_key, w_value)
-            ],
-        ),
-        0,
-        3 * 2**20,
-        [pltpu.SemaphoreType.DMA((3 * calls,))],
-    )
-
     steps = nodes // block
     both = 2 * head_size
-    groups = -(-sub_heads // 2)
+    groups = -(-heads // 2)
     target = model // clus_size
     pairs = rest // 2
-    lam_t = eig_weight.T
-
-    def attention(c, prior):
-        last = c == calls - 1
-        shapes = [
-            ((3 * part_width, nodes), BF16),
-            ((part_width, nodes), BF16),
-            ((sub_heads, eig_count), F32),
+    grads_t, out_t, gw_own, eig_own, *parts = call(
+        functools.partial(attention_kernel, scale, heads, head_size, node_size, len(rows)),
+        [smem, smem] + [vmem] * (len(rows) + node_size + 6),
+        [
+            ((3 * width, nodes), BF16),
+            ((width, nodes), BF16),
+            ((heads, eig_count), F32),
+            ((eig_count, size), F32),
         ]
-        if last:
-            shapes += [((eig_count, size), F32)]
-            shapes += [((3 * width + eig_count, size), BF16)] * node_size
-        else:
-            shapes += [((eig_count, nodes), F32)]
+        + [((3 * width + eig_count, size), BF16)] * node_size,
+        (ids, block_mask[0], *rows, *d_att, *weights, eigvec[0], eig_weight, eig_weight.T),
+        8 * 10**9,
+        8 * 2**20,
+        [
+            pltpu.VMEM((heads, steps, both, block), BF16),
+            pltpu.VMEM((heads, nodes, both), BF16),
+            pltpu.VMEM((groups, steps, both, block), BF16),
+            pltpu.VMEM((groups, nodes, both), BF16),
+            pltpu.VMEM((eig_count, nodes), F32),
+        ],
+    )
+
+    def terms(base, left, pieces):
         return call(
-            functools.partial(
-                attention_kernel,
-                scale,
-                sub_heads,
-                head_size,
-                node_size,
-                len(rows),
-                c * sub_heads,
-                last,
-            ),
-            [smem, smem] + [vmem] * (len(rows) + node_size + 6 + len(prior)),
-            shapes,
-            (
-                ids,
-                block_mask[0],
-                *rows,
-                *d_att,
-                *weights[3 * c : 3 * c + 3],
-                eigvec[0],
-                eig_weight,
-                lam_t,
-                *prior,
-            ),
-            4 * 10**9,
-            4 * 2**20,
-            [
-                pltpu.VMEM((sub_heads, steps, both, block), BF16),
-                pltpu.VMEM((sub_heads, nodes, both), BF16),
-                pltpu.VMEM((groups, steps, both, block), BF16),
-                pltpu.VMEM((groups, nodes, both), BF16),
-                pltpu.VMEM((eig_count, nodes), F32),
-            ],
-        )
-
-    def terms(base, grads_t, outs):
-        used = cots if outs else []
-        return call(
-            functools.partial(terms_kernel, node_size + base, len(rows), len(outs), target),
-            [smem] + [vmem] * (len(rows) + len(used) + 1 + len(outs)),
-            [((rest, grads_t.shape[0] + len(outs) * part_width, target), BF16)],
-            (ids, *rows, *used, grads_t, *outs),
+            functools.partial(terms_kernel, node_size + base, len(pieces), target),
+            [smem] + [vmem] * (len(pieces) + 1),
+            [((rest, left.shape[0], target), BF16)],
+            (ids, *pieces, left),
             10**9,
             2**20,
         )[0]
 
-    near_keeps, near_gots, head_outs, weight_parts, prior = [], [], [], [], []
-    for c in range(calls):
-        last = c == calls - 1
-        grads_t, head_out, weight_part, *others = attention(c, prior)
-        head_outs.append(head_out)
-        weight_parts.append(weight_part)
-        prior += [grads_t, others[0]]
-        outs = head_outs if last else []
-        give_half = terms(0, grads_t, outs)
+    near_keeps, near_gots = [], []
+    for c, (left, pieces) in enumerate(((grads_t, rows), (out_t, cots))):
+        give_half = terms(0, left, pieces)
         got_half = give(give_half, "clus", 1, clus_size)
-        keep_half = terms(rest, grads_t, outs)
-        group_rows = keep_half.shape[1]
-        extra = 16 if last else 0
+        keep_half = terms(rest, left, pieces)
+        group_rows = left.shape[0]
         operands = [keep_half, got_half]
-        shapes = [((pairs * group_rows + extra, target), BF16), ((pairs, group_rows, target), F32)]
-        if last:
-            mine = jnp.concatenate(weight_parts, axis=0) if calls > 1 else weight_part
-            operands += [*weight_parts, give(mine, "clus", 1, clus_size)]
+        shapes = [
+            ((pairs * group_rows + (16 if c == 0 else 0), target), BF16),
+            ((pairs, group_rows, target), F32),
+        ]
+        if c == 0:
+            operands += [gw_own, give(gw_own, "clus", 1, clus_size)]
             shapes.append((eig_weight.shape, F32))
-        near_give, near_keep, *gw_pair = call(
-            functools.partial(pair_kernel, calls if last else 0),
+        near_give, near_keep, *others = call(
+            functools.partial(pair_kernel, c == 0),
             [vmem] * len(operands),
             shapes,
             operands,
             10**6,
             2**21,
         )
+        if c == 0:
+            gw_pair = others[0]
         near_keeps.append(near_keep)
         near_gots.append(give(near_give, "clus", 2, clus_size))
-    eig_own, *parts = others
 
     returned = [parts[0]] + [None] * (node_size - 1)
     for s in far_first:
         returned[s] = give(parts[s], "node", s, node_size)
 
     totals = []
-    for c in range(calls):
+    for c in range(2):
         group_rows = near_keeps[c].shape[1]
-        last = c == calls - 1
-        extra = 16 if last else 0
-        shapes = [((group_rows, target), F32)] + ([(eig_weight.shape, F32)] if last else [])
+        extra = 16 if c == 0 else 0
+        shapes = [((group_rows, target), F32)] + ([(eig_weight.shape, F32)] if c == 0 else [])
         own, *others = call(
-            functools.partial(near_kernel, last),
-            [vmem] * (3 if last else 2),
+            functools.partial(near_kernel, c == 0),
+            [vmem] * (3 if c == 0 else 2),
             shapes + [((group_rows + extra, target), BF16)] * (pairs - 1),
-            (near_keeps[c], near_gots[c], *(gw_pair if last else [])),
+            (near_keeps[c], near_gots[c], *([gw_pair] if c == 0 else [])),
             10**6,
             2**20,
         )
-        if last:
+        if c == 0:
             gw_four, *others = others
         totals.append(own)
         found = [None] * (pairs - 1)
@@ -619,7 +542,7 @@
         totals += found
 
     grad_rows, grad_eig = call(
-        functools.partial(nodes_kernel, node_size, width, calls),
+        functools.partial(nodes_kernel, node_size, width),
         [smem] + [vmem] * (node_size + 4),
         [((size, model), BF16), ((eig_count, size), F32)],
         (ids, eig_own, *returned, w_query, w_key, w_value),
@@ -629,7 +552,7 @@
     )
 
     grad_proj, grad_weight = call(
-        functools.partial(final_kernel, calls, pairs - 1),
+        functools.partial(final_kernel, pairs - 1),
         [vmem] * (len(totals) + 1),
         [((4, target, width), F32), (eig_weight.shape, F32)],
         (*totals, gw_four),

time: 66.7 us -> 69.2 us (1.037)
  waiting for transfers between devices: 19.8 us -> 24.6 us
  Pallas kernels: 21.5 us -> 17.4 us
  starting transfers between devices: 23.1 us -> 26 us
  local copies, waits for them, and re-layouts: 1.08 us -> 0.13 us
    ppermute x20, waiting for transfers between devices: 19.8 us -> 24.6 us  [take(): return lax.ppermute(value, axis, pairs)]
    pallas_call x15 -> x13, Pallas kernels: 21.5 us -> 17.4 us  [call_here(): pl.pallas_call(kernel, in_specs=in_specs, out_specs=[vmem] * len(out_shap...]
    ppermute x20, starting transfers between devices: 23.1 us -> 26 us  [take(): return lax.ppermute(value, axis, pairs)]
    unnamed x19 -> x17, local copies, waits for them, and re-layouts: 1.08 us -> 0.13 us
  transfers between devices with their start and end apart: 20 -> 20, of which waited for: 8 -> 10; matrix products, arithmetic and copies ran while one was open for 0% -> 0% of each run, Pallas kernels for 29% -> 14%
where the time goes in v3:
time: 69.2 us; the launch traced here: 69.1 us
  starting transfers between devices  26 us (38%)
  waiting for transfers between devices  24.6 us (36%)
  Pallas kernels  17.4 us (25%)
  between operations  0.82 us (1%)
    ppermute x20, starting transfers between devices, take(): return lax.ppermute(value, axis, pairs)  26 us
    ppermute x20, waiting for transfers between devices, take(): return lax.ppermute(value, axis, pairs)  24.6 us
    pallas_call x13, Pallas kernels, call_here(): pl.pallas_call(kernel, in_specs=in_specs, out_specs=[vmem] * len(out_shap...  17.4 us
  transfers between devices with their start and end apart: 20, of which 10 were waited for; matrix products, arithmetic and copies ran while one was open for 0% of the time, Pallas kernels for 14%

profile of v3, /device:TPU:0, one launch (start us, length us, event | category | flops | bytes accessed | tf_op | source)
XLA Modules:
  0.0 69.1 jit_solution(17980870746036296427)
XLA Ops:
  0.6 3.0 %collective-permute-start = (bf16[128,1024]{1,0:T(8,128)(2,1)}, bf16[128,1024]{1,0:T(8,128)(2,1)S(1)}, u32[]{:S(2)}, u32[]{:S(2)}) collective-permute-start(bf16[128,1024]{1,0:T(8,128)(2,1)} %bitcast.14), channel_id=1, source_target_pairs={{0,1},{1,0},{2,3},{3,2},{4,5},{5,4},{6,7},{7,6},{8,9},{9,8},{10,11... | collective-permute-start | bytes 786440 | tf_op jit(solution)/shard_map/ppermute | solution.py:27
  3.7 1.5 %collective-permute-start.1 = (bf16[128,1024]{1,0:T(8,128)(2,1)}, bf16[128,1024]{1,0:T(8,128)(2,1)S(1)}, u32[]{:S(2)}, u32[]{:S(2)}) collective-permute-start(bf16[128,1024]{1,0:T(8,128)(2,1)} %bitcast.15), channel_id=1, source_target_pairs={{0,2},{1,3},{2,0},{3,1},{4,6},{5,7},{6,4},{7,5},{8,10},{9,11},{10,... | collective-permute-start | bytes 786440 | tf_op jit(solution)/shard_map/ppermute | solution.py:27
  5.2 5.0 %collective-permute-done.first_ref.refs_1_ = bf16[128,1024]{1,0:T(8,128)(2,1)S(1)} collective-permute-done((bf16[128,1024]{1,0:T(8,128)(2,1)}, bf16[128,1024]{1,0:T(8,128)(2,1)S(1)}, u32[]{:S(2)}, u32[]{:S(2)}) %collective-permute-start) | collective-permute-done | bytes 262176 | tf_op jit(solution)/shard_map/ppermute | solution.py:27
  10.2 1.5 %collective-permute-done.1.second_ref.refs_2_ = bf16[128,1024]{1,0:T(8,128)(2,1)S(1)} collective-permute-done((bf16[128,1024]{1,0:T(8,128)(2,1)}, bf16[128,1024]{1,0:T(8,128)(2,1)S(1)}, u32[]{:S(2)}, u32[]{:S(2)}) %collective-permute-start.1) | collective-permute-done | bytes 262176 | tf_op jit(solution)/shard_map/ppermute | solution.py:27
  11.7 0.4 collective-permute-start.2
  12.1 1.7 %collective-permute-start.3 = (bf16[64,1024]{1,0:T(8,128)(2,1)S(1)}, bf16[64,1024]{1,0:T(8,128)(2,1)S(1)}, u32[]{:S(2)}, u32[]{:S(2)}) collective-permute-start(bf16[64,1024]{1,0:T(8,128)(2,1)S(1)} %get-tuple-element.36), channel_id=1, source_target_pairs={{0,2},{1,3},{2,0},{3,1},{4,6},{5,7},{6,4},{7,5},{8,10},{9,11},{10,... | collective-permute-start | bytes 393224 | tf_op jit(solution)/shard_map/ppermute | solution.py:27
  13.8 0.1 pad_add_fusion.ids_ref
  13.9 0.0 copy-start.4
  13.9 0.0 copy-start.5
  13.9 2.9 %shard_map.121 = (bf16[128,256]{1,0:T(8,128)(2,1)S(1)}, bf16[128,256]{1,0:T(8,128)(2,1)S(1)}, bf16[128,256]{1,0:T(8,128)(2,1)S(1)}, bf16[128,256]{1,0:T(8,128)(2...) custom-call(s32[12]{0:T(128)S(1)} %pad_add_fusion.ids_ref, ...), custom_call_target="tpu_custom_call" | custom-call | flops 300000000 | bytes 3145728 | tf_op jit(solution)/shard_map/pallas_call | solution.py:406
  16.8 1.6 %collective-permute-start.4 = (bf16[128,256]{1,0:T(8,128)(2,1)S(1)}, bf16[128,256]{1,0:T(8,128)(2,1)S(1)}, u32[]{:S(2)}, u32[]{:S(2)}) collective-permute-start(bf16[128,256]{1,0:T(8,128)(2,1)S(1)} %get-tuple-element.38), channel_id=1, source_target_pairs={{0,1},{1,0},{2,3},{3,2},{4,5},{5,4},{6,7},{7,6},{8,9},{9,8},{10,11... | collective-permute-start | bytes 196616 | tf_op jit(solution)/shard_map/ppermute | solution.py:27
  18.3 0.5 collective-permute-start.5
  18.8 1.5 %collective-permute-start.6 = (bf16[128,256]{1,0:T(8,128)(2,1)S(1)}, bf16[128,256]{1,0:T(8,128)(2,1)S(1)}, u32[]{:S(2)}, u32[]{:S(2)}) collective-permute-start(bf16[128,256]{1,0:T(8,128)(2,1)S(1)} %get-tuple-element.40), channel_id=1, source_target_pairs={{0,3},{1,2},{2,1},{3,0},{4,7},{5,6},{6,5},{7,4},{8,11},{9,10},{10,... | collective-permute-start | bytes 196616 | tf_op jit(solution)/shard_map/ppermute | solution.py:27
  20.3 0.0 copy-done.4
  20.3 0.1 copy.13
  20.4 0.9 %collective-permute-done.4.refs_6_ = bf16[128,256]{1,0:T(8,128)(2,1)S(1)} collective-permute-done((bf16[128,256]{1,0:T(8,128)(2,1)S(1)}, bf16[128,256]{1,0:T(8,128)(2,1)S(1)}, u32[]{:S(2)}, u32[]{:S(2)}) %collective-permute-start.4) | collective-permute-done | bytes 65568 | tf_op jit(solution)/shard_map/ppermute | solution.py:27
  21.4 1.2 %collective-permute-done.5.refs_7_ = bf16[128,256]{1,0:T(8,128)(2,1)S(1)} collective-permute-done((bf16[128,256]{1,0:T(8,128)(2,1)S(1)}, bf16[128,256]{1,0:T(8,128)(2,1)S(1)}, u32[]{:S(2)}, u32[]{:S(2)}) %collective-permute-start.5) | collective-permute-done | bytes 65568 | tf_op jit(solution)/shard_map/ppermute | solution.py:27
  22.6 1.4 %collective-permute-done.6.refs_8_ = bf16[128,256]{1,0:T(8,128)(2,1)S(1)} collective-permute-done((bf16[128,256]{1,0:T(8,128)(2,1)S(1)}, bf16[128,256]{1,0:T(8,128)(2,1)S(1)}, u32[]{:S(2)}, u32[]{:S(2)}) %collective-permute-start.6) | collective-permute-done | bytes 65568 | tf_op jit(solution)/shard_map/ppermute | solution.py:27
  24.0 0.0 collective-permute-done.2.refs_3_
  24.0 0.0 collective-permute-done.3.refs_4_
  24.0 0.0 copy-done.5
  24.0 0.0 copy-done.6
  24.0 0.0 copy-done.7
  24.0 5.8 %shard_map.122 = (bf16[768,512]{1,0:T(8,128)(2,1)S(1)}, bf16[256,512]{1,0:T(8,128)(2,1)S(1)}, f32[4,64]{1,0:T(4,128)S(1)}, f32[64,128]{1,0:T(8,128)S(1)}, bf16[8...) custom-call(s32[12]{0:T(128)S(1)} %pad_add_fusion.ids_ref, ...), custom_call_target="tpu_custom_call" | custom-call | flops 8000000000 | bytes 8388608 | tf_op jit(solution)/shard_map/pallas_call | solution.py:406
  29.8 0.0 copy-start.3
  29.9 1.2 %shard_map.125 = bf16[4,768,128]{2,1,0:T(8,128)(2,1)S(1)} custom-call(s32[12]{0:T(128)S(1)} %pad_add_fusion.ids_ref, bf16[128,1024]{1,0:T(8,128)(2,1)S(1)} %bitcast.17, bf16[128,1024]{1,0:T(8,128)(2,1)S(1)} %collective-permute-done.first_ref.refs_1_, bf16[128,1024]{1,0:T(8,128)(2,1)S(1)} %collective-permute-done.1.second_ref.refs_2_, ...), custom_call_target="tpu_custom_call" | custom-call | flops 1000000000 | bytes 1048576 | tf_op jit(solution)/shard_map/pallas_call | solution.py:406
  31.0 0.1 collective-permute-start.10
  31.1 0.0 copy-done.3
  31.1 0.4 collective-permute-start.14
  31.6 1.7 %collective-permute-start.15 = (bf16[128,1024]{1,0:T(8,128)(2,1)S(1)}, bf16[128,1024]{1,0:T(8,128)(2,1)S(1)}, u32[]{:S(2)}, u32[]{:S(2)}) collective-permute-start(bf16[128,1024]{1,0:T(8,128)(2,1)S(1)} %bitcast.9), channel_id=1, source_target_pairs={{0,2},{1,3},{2,0},{3,1},{4,6},{5,7},{6,4},{7,5},{8,10},{9,11},{10,... | collective-permute-start | bytes 786440 | tf_op jit(solution)/shard_map/ppermute | solution.py:27
  33.3 1.4 %collective-permute-start.16 = (bf16[128,1024]{1,0:T(8,128)(2,1)S(1)}, bf16[128,1024]{1,0:T(8,128)(2,1)S(1)}, u32[]{:S(2)}, u32[]{:S(2)}) collective-permute-start(bf16[128,1024]{1,0:T(8,128)(2,1)S(1)} %bitcast.10), channel_id=1, source_target_pairs={{0,3},{1,2},{2,1},{3,0},{4,7},{5,6},{6,5},{7,4},{8,11},{9,10},{10,... | collective-permute-start | bytes 786440 | tf_op jit(solution)/shard_map/ppermute | solution.py:27
  34.7 0.0 collective-permute-start.11
  34.7 1.2 %shard_map.124.keep_ref = bf16[4,768,128]{2,1,0:T(8,128)(2,1)S(1)} custom-call(s32[12]{0:T(128)S(1)} %pad_add_fusion.ids_ref, bf16[128,1024]{1,0:T(8,128)(2,1)S(1)} %bitcast.18, bf16[128,1024]{1,0:T(8,128)(2,1)S(1)} %collective-permute-done.first_ref.refs_1_, bf16[128,1024]{1,0:T(8,128)(2,1)S(1)} %collective-permute-done.1.second_ref.refs_2_, ...), custom_call_target="tpu_custom_call" | custom-call | flops 1000000000 | bytes 1048576 | tf_op jit(solution)/shard_map/pallas_call | solution.py:406
  35.9 0.0 collective-permute-done.11.refs_1_
  35.9 0.0 collective-permute-done.10.got_ref
  35.9 0.2 shard_map.126
  36.1 1.6 %collective-permute-start.12 = (bf16[1552,128]{1,0:T(8,128)(2,1)S(1)}, bf16[1552,128]{1,0:T(8,128)(2,1)S(1)}, u32[]{:S(2)}, u32[]{:S(2)}) collective-permute-start(bf16[1552,128]{1,0:T(8,128)(2,1)S(1)} %get-tuple-element.54), channel_id=1, source_target_pairs={{0,8},{4,12},{8,0},{12,4},{16,24},{20,28},{24,16},{28,20},{1,9},{5... | collective-permute-start | bytes 1191944 | tf_op jit(solution)/shard_map/ppermute | solution.py:27
  37.8 2.6 %collective-permute-done.14.refs_1_ = bf16[128,1024]{1,0:T(8,128)(2,1)S(1)} collective-permute-done((bf16[128,1024]{1,0:T(8,128)(2,1)S(1)}, bf16[128,1024]{1,0:T(8,128)(2,1)S(1)}, u32[]{:S(2)}, u32[]{:S(2)}) %collective-permute-start.14) | collective-permute-done | bytes 262176 | tf_op jit(solution)/shard_map/ppermute | solution.py:27
  40.4 4.4 %collective-permute-done.15.refs_2_ = bf16[128,1024]{1,0:T(8,128)(2,1)S(1)} collective-permute-done((bf16[128,1024]{1,0:T(8,128)(2,1)S(1)}, bf16[128,1024]{1,0:T(8,128)(2,1)S(1)}, u32[]{:S(2)}, u32[]{:S(2)}) %collective-permute-start.15) | collective-permute-done | bytes 262176 | tf_op jit(solution)/shard_map/ppermute | solution.py:27
  44.8 1.6 %collective-permute-done.16.refs_3_ = bf16[128,1024]{1,0:T(8,128)(2,1)S(1)} collective-permute-done((bf16[128,1024]{1,0:T(8,128)(2,1)S(1)}, bf16[128,1024]{1,0:T(8,128)(2,1)S(1)}, u32[]{:S(2)}, u32[]{:S(2)}) %collective-permute-start.16) | collective-permute-done | bytes 262176 | tf_op jit(solution)/shard_map/ppermute | solution.py:27
  46.4 0.9 %shard_map.129 = bf16[4,256,128]{2,1,0:T(8,128)(2,1)S(1)} custom-call(s32[12]{0:T(128)S(1)} %pad_add_fusion.ids_ref, bf16[128,1024]{1,0:T(8,128)(2,1)S(1)} %bitcast.11, bf16[128,1024]{1,0:T(8,128)(2,1)S(1)} %collective-permute-done.14.refs_1_, bf16[128,1024]{1,0:T(8,128)(2,1)S(1)} %collective-permute-done.15.refs_2_, ...), custom_call_target="tpu_custom_call" | custom-call | flops 1000000000 | bytes 1048576 | tf_op jit(solution)/shard_map/pallas_call | solution.py:406
  47.3 0.1 collective-permute-start.17
  47.4 0.8 %collective-permute-start.7 = (bf16[832,128]{1,0:T(8,128)(2,1)S(1)}, bf16[832,128]{1,0:T(8,128)(2,1)S(1)}, u32[]{:S(2)}, u32[]{:S(2)}) collective-permute-start(bf16[832,128]{1,0:T(8,128)(2,1)S(1)} %get-tuple-element.46), channel_id=1, source_target_pairs={{0,1},{1,0},{2,3},{3,2},{4,5},{5,4},{6,7},{7,6},{8,9},{9,8},{10,11... | collective-permute-start | bytes 638984 | tf_op jit(solution)/shard_map/ppermute | solution.py:27
  48.3 1.5 %collective-permute-start.8 = (bf16[832,128]{1,0:T(8,128)(2,1)S(1)}, bf16[832,128]{1,0:T(8,128)(2,1)S(1)}, u32[]{:S(2)}, u32[]{:S(2)}) collective-permute-start(bf16[832,128]{1,0:T(8,128)(2,1)S(1)} %get-tuple-element.47), channel_id=1, source_target_pairs={{0,2},{1,3},{2,0},{3,1},{4,6},{5,7},{6,4},{7,5},{8,10},{9,11},{10,... | collective-permute-start | bytes 638984 | tf_op jit(solution)/shard_map/ppermute | solution.py:27
  49.8 1.2 %collective-permute-start.9 = (bf16[832,128]{1,0:T(8,128)(2,1)S(1)}, bf16[832,128]{1,0:T(8,128)(2,1)S(1)}, u32[]{:S(2)}, u32[]{:S(2)}) collective-permute-start(bf16[832,128]{1,0:T(8,128)(2,1)S(1)} %get-tuple-element.48), channel_id=1, source_target_pairs={{0,3},{1,2},{2,1},{3,0},{4,7},{5,6},{6,5},{7,4},{8,11},{9,10},{10,... | collective-permute-start | bytes 638984 | tf_op jit(solution)/shard_map/ppermute | solution.py:27
  51.0 0.9 %shard_map.128.keep_ref = bf16[4,256,128]{2,1,0:T(8,128)(2,1)S(1)} custom-call(s32[12]{0:T(128)S(1)} %pad_add_fusion.ids_ref, bf16[128,1024]{1,0:T(8,128)(2,1)S(1)} %bitcast.12, bf16[128,1024]{1,0:T(8,128)(2,1)S(1)} %collective-permute-done.14.refs_1_, bf16[128,1024]{1,0:T(8,128)(2,1)S(1)} %collective-permute-done.15.refs_2_, ...), custom_call_target="tpu_custom_call" | custom-call | flops 1000000000 | bytes 1048576 | tf_op jit(solution)/shard_map/pallas_call | solution.py:406
  51.9 0.0 collective-permute-done.17.got_ref
  51.9 0.1 shard_map.130
  52.0 1.7 %collective-permute-start.18 = (bf16[512,128]{1,0:T(8,128)(2,1)S(1)}, bf16[512,128]{1,0:T(8,128)(2,1)S(1)}, u32[]{:S(2)}, u32[]{:S(2)}) collective-permute-start(bf16[512,128]{1,0:T(8,128)(2,1)S(1)} %get-tuple-element.60), channel_id=1, source_target_pairs={{0,8},{4,12},{8,0},{12,4},{16,24},{20,28},{24,16},{28,20},{1,9},{5... | collective-permute-start | bytes 393224 | tf_op jit(solution)/shard_map/ppermute | solution.py:27
  53.6 0.0 collective-permute-done.12.got_ref
  53.6 0.1 shard_map.127
  53.7 2.7 %collective-permute-start.13 = (bf16[784,128]{1,0:T(8,128)(2,1)S(1)}, bf16[784,128]{1,0:T(8,128)(2,1)S(1)}, u32[]{:S(2)}, u32[]{:S(2)}) collective-permute-start(bf16[784,128]{1,0:T(8,128)(2,1)S(1)} %get-tuple-element.57), channel_id=1, source_target_pairs={{0,16},{4,20},{8,24},{12,28},{16,0},{20,4},{24,8},{28,12},{1,17},{... | collective-permute-start | bytes 602120 | tf_op jit(solution)/shard_map/ppermute | solution.py:27
  56.4 2.1 %collective-permute-done.18.got_ref = bf16[512,128]{1,0:T(8,128)(2,1)S(1)} collective-permute-done((bf16[512,128]{1,0:T(8,128)(2,1)S(1)}, bf16[512,128]{1,0:T(8,128)(2,1)S(1)}, u32[]{:S(2)}, u32[]{:S(2)}) %collective-permute-start.18) | collective-permute-done | bytes 131104 | tf_op jit(solution)/shard_map/ppermute | solution.py:27
  58.5 2.6 %collective-permute-start.19 = (bf16[256,128]{1,0:T(8,128)(2,1)S(1)}, bf16[256,128]{1,0:T(8,128)(2,1)S(1)}, u32[]{:S(2)}, u32[]{:S(2)}) collective-permute-start(bf16[256,128]{1,0:T(8,128)(2,1)S(1)} %get-tuple-element.62), channel_id=1, source_target_pairs={{0,16},{4,20},{8,24},{12,28},{16,0},{20,4},{24,8},{28,12},{1,17},{... | collective-permute-start | bytes 196616 | tf_op jit(solution)/shard_map/ppermute | solution.py:27
  61.1 0.0 collective-permute-done.7.refs_1_
  61.1 0.0 collective-permute-done.8.refs_2_
  61.1 0.0 collective-permute-done.9.refs_3_
  61.1 0.0 copy-done.2
  61.1 0.0 copy-done
  61.1 0.0 copy-done.1
  61.1 3.2 %shard_map.123 = (bf16[128,1024]{1,0:T(8,128)(2,1)}, f32[64,128]{1,0:T(8,128)}) custom-call(s32[12]{0:T(128)S(1)} %pad_add_fusion.ids_ref, f32[64,128]{1,0:T(8,128)S(1)} %get-tuple-element.44.eig_ref, bf16[832,128]{1,0:T(8,128)(2,1)S(1)} %get-tuple-element.45.refs_0_, bf16[832,128]{1,0:T(8,128)(2,1)S(1)} %collective-permute-done.7.refs_1_, ...), custom_call_target="tpu_custom_call" | custom-call | flops 1000000000 | bytes 7340032 | tf_op jit(solution)/shard_map/pallas_call | solution.py:406
  64.3 3.7 %collective-permute-done.19.refs_3_ = bf16[256,128]{1,0:T(8,128)(2,1)S(1)} collective-permute-done((bf16[256,128]{1,0:T(8,128)(2,1)S(1)}, bf16[256,128]{1,0:T(8,128)(2,1)S(1)}, u32[]{:S(2)}, u32[]{:S(2)}) %collective-permute-start.19) | collective-permute-done | bytes 65568 | tf_op jit(solution)/shard_map/ppermute | solution.py:27
  68.0 0.0 collective-permute-done.13.refs_1_
  68.0 1.0 %shard_map.132 = (f32[4,128,256]{2,1,0:T(8,128)}, f32[4,64]{1,0:T(4,128)}) custom-call(f32[768,128]{1,0:T(8,128)S(1)} %get-tuple-element.56.refs_0_, bf16[784,128]{1,0:T(8,128)(2,1)S(1)} %collective-permute-done.13.refs_1_, f32[256,128]{1,0:T(8,128)S(1)} %get-tuple-element.61.refs_2_, bf16[256,128]{1,0:T(8,128)(2,1)S(1)} %collective-permute-done.19.refs_3_, ...), custom_call_target="tpu_custom_call" | custom-call | flops 1000000 | bytes 2097152 | tf_op jit(solution)/shard_map/pallas_call | solution.py:406
  (9 shorter events, 0.1 us)
Async XLA Ops:
  0.6 9.6 %collective-permute-start = (bf16[128,1024]{1,0:T(8,128)(2,1)}, bf16[128,1024]{1,0:T(8,128)(2,1)S(1)}, u32[]{:S(2)}, u32[]{:S(2)}) collective-permute-start(bf16[128,1024]{1,0:T(8,128)(2,1)} %bitcast.14), channel_id=1, source_target_pairs={{0,1},{1,0},{2,3},{3,2},{4,5},{5,4},{6,7},{7,6},{8,9},{9,8},{10,11... | collective-permute-start | bytes 786440 | tf_op jit(solution)/shard_map/ppermute | solution.py:27
  3.7 8.0 %collective-permute-start.1 = (bf16[128,1024]{1,0:T(8,128)(2,1)}, bf16[128,1024]{1,0:T(8,128)(2,1)S(1)}, u32[]{:S(2)}, u32[]{:S(2)}) collective-permute-start(bf16[128,1024]{1,0:T(8,128)(2,1)} %bitcast.15), channel_id=1, source_target_pairs={{0,2},{1,3},{2,0},{3,1},{4,6},{5,7},{6,4},{7,5},{8,10},{9,11},{10,... | collective-permute-start | bytes 786440 | tf_op jit(solution)/shard_map/ppermute | solution.py:27
  11.7 12.3 %collective-permute-start.2 = (bf16[64,1024]{1,0:T(8,128)(2,1)S(1)}, bf16[64,1024]{1,0:T(8,128)(2,1)S(1)}, u32[]{:S(2)}, u32[]{:S(2)}) collective-permute-start(bf16[64,1024]{1,0:T(8,128)(2,1)S(1)} %get-tuple-element.35), channel_id=1, source_target_pairs={{0,1},{1,0},{2,3},{3,2},{4,5},{5,4},{6,7},{7,6},{8,9},{9,8},{10,11... | collective-permute-start | bytes 393224 | tf_op jit(solution)/shard_map/ppermute | solution.py:27
  12.1 11.9 %collective-permute-start.3 = (bf16[64,1024]{1,0:T(8,128)(2,1)S(1)}, bf16[64,1024]{1,0:T(8,128)(2,1)S(1)}, u32[]{:S(2)}, u32[]{:S(2)}) collective-permute-start(bf16[64,1024]{1,0:T(8,128)(2,1)S(1)} %get-tuple-element.36), channel_id=1, source_target_pairs={{0,2},{1,3},{2,0},{3,1},{4,6},{5,7},{6,4},{7,5},{8,10},{9,11},{10,... | collective-permute-start | bytes 393224 | tf_op jit(solution)/shard_map/ppermute | solution.py:27
  13.9 6.5 %copy-start.4 = (f32[4,64]{1,0:T(4,128)S(1)}, f32[4,64]{1,0:T(4,128)}, u32[]{:S(2)}) copy-start(f32[4,64]{1,0:T(4,128)} %refs_13_.1) | copy-start | bytes 3076
  13.9 10.1 %copy-start.5 = (bf16[1,128,1024]{2,1,0:T(8,128)(2,1)S(1)}, bf16[1,128,1024]{2,1,0:T(8,128)(2,1)}, u32[]{:S(2)}) copy-start(bf16[1,128,1024]{2,1,0:T(8,128)(2,1)} %param.9) | copy-start | bytes 786436
  13.9 10.1 %copy-start.6 = (bf16[1,64,512]{2,1,0:T(8,128)(2,1)S(1)}, bf16[1,64,512]{2,1,0:T(8,128)(2,1)}, u32[]{:S(2)}) copy-start(bf16[1,64,512]{2,1,0:T(8,128)(2,1)} %param.15) | copy-start | bytes 196612
  13.9 10.2 %copy-start.7 = (s32[1,4,4,4]{3,2,1,0:T(4,128)S(1)}, s32[1,4,4,4]{3,2,1,0:T(4,128)}, u32[]{:S(2)}) copy-start(s32[1,4,4,4]{3,2,1,0:T(4,128)} %param.17) | copy-start | bytes 772
  16.8 4.6 %collective-permute-start.4 = (bf16[128,256]{1,0:T(8,128)(2,1)S(1)}, bf16[128,256]{1,0:T(8,128)(2,1)S(1)}, u32[]{:S(2)}, u32[]{:S(2)}) collective-permute-start(bf16[128,256]{1,0:T(8,128)(2,1)S(1)} %get-tuple-element.38), channel_id=1, source_target_pairs={{0,1},{1,0},{2,3},{3,2},{4,5},{5,4},{6,7},{7,6},{8,9},{9,8},{10,11... | collective-permute-start | bytes 196616 | tf_op jit(solution)/shard_map/ppermute | solution.py:27
  18.3 4.3 %collective-permute-start.5 = (bf16[128,256]{1,0:T(8,128)(2,1)S(1)}, bf16[128,256]{1,0:T(8,128)(2,1)S(1)}, u32[]{:S(2)}, u32[]{:S(2)}) collective-permute-start(bf16[128,256]{1,0:T(8,128)(2,1)S(1)} %get-tuple-element.39), channel_id=1, source_target_pairs={{0,2},{1,3},{2,0},{3,1},{4,6},{5,7},{6,4},{7,5},{8,10},{9,11},{10,... | collective-permute-start | bytes 196616 | tf_op jit(solution)/shard_map/ppermute | solution.py:27
  18.8 5.2 %collective-permute-start.6 = (bf16[128,256]{1,0:T(8,128)(2,1)S(1)}, bf16[128,256]{1,0:T(8,128)(2,1)S(1)}, u32[]{:S(2)}, u32[]{:S(2)}) collective-permute-start(bf16[128,256]{1,0:T(8,128)(2,1)S(1)} %get-tuple-element.40), channel_id=1, source_target_pairs={{0,3},{1,2},{2,1},{3,0},{4,7},{5,6},{6,5},{7,4},{8,11},{9,10},{10,... | collective-permute-start | bytes 196616 | tf_op jit(solution)/shard_map/ppermute | solution.py:27
  29.8 1.3 %copy-start.3 = (bf16[1,128,1024]{2,1,0:T(8,128)(2,1)S(1)}, bf16[1,128,1024]{2,1,0:T(8,128)(2,1)}, u32[]{:S(2)}) copy-start(bf16[1,128,1024]{2,1,0:T(8,128)(2,1)} %param.10) | copy-start | bytes 786436
  31.0 4.8 %collective-permute-start.10 = (bf16[4,768,128]{2,1,0:T(8,128)(2,1)S(1)}, bf16[4,768,128]{2,1,0:T(8,128)(2,1)S(1)}, u32[]{:S(2)}, u32[]{:S(2)}) collective-permute-start(bf16[4,768,128]{2,1,0:T(8,128)(2,1)S(1)} %shard_map.125), channel_id=1, source_target_pairs={{0,4},{4,0},{8,12},{12,8},{16,20},{20,16},{24,28},{28,24},{1,5},{5... | collective-permute-start | bytes 2359304 | tf_op jit(solution)/shard_map/ppermute | solution.py:27
  31.1 9.2 %collective-permute-start.14 = (bf16[128,1024]{1,0:T(8,128)(2,1)S(1)}, bf16[128,1024]{1,0:T(8,128)(2,1)S(1)}, u32[]{:S(2)}, u32[]{:S(2)}) collective-permute-start(bf16[128,1024]{1,0:T(8,128)(2,1)S(1)} %bitcast.8), channel_id=1, source_target_pairs={{0,1},{1,0},{2,3},{3,2},{4,5},{5,4},{6,7},{7,6},{8,9},{9,8},{10,11... | collective-permute-start | bytes 786440 | tf_op jit(solution)/shard_map/ppermute | solution.py:27
  31.6 13.2 %collective-permute-start.15 = (bf16[128,1024]{1,0:T(8,128)(2,1)S(1)}, bf16[128,1024]{1,0:T(8,128)(2,1)S(1)}, u32[]{:S(2)}, u32[]{:S(2)}) collective-permute-start(bf16[128,1024]{1,0:T(8,128)(2,1)S(1)} %bitcast.9), channel_id=1, source_target_pairs={{0,2},{1,3},{2,0},{3,1},{4,6},{5,7},{6,4},{7,5},{8,10},{9,11},{10,... | collective-permute-start | bytes 786440 | tf_op jit(solution)/shard_map/ppermute | solution.py:27
  33.3 13.2 %collective-permute-start.16 = (bf16[128,1024]{1,0:T(8,128)(2,1)S(1)}, bf16[128,1024]{1,0:T(8,128)(2,1)S(1)}, u32[]{:S(2)}, u32[]{:S(2)}) collective-permute-start(bf16[128,1024]{1,0:T(8,128)(2,1)S(1)} %bitcast.10), channel_id=1, source_target_pairs={{0,3},{1,2},{2,1},{3,0},{4,7},{5,6},{6,5},{7,4},{8,11},{9,10},{10,... | collective-permute-start | bytes 786440 | tf_op jit(solution)/shard_map/ppermute | solution.py:27
  34.7 1.2 %collective-permute-start.11 = (f32[4,64]{1,0:T(4,128)S(1)}, f32[4,64]{1,0:T(4,128)S(1)}, u32[]{:S(2)}, u32[]{:S(2)}) collective-permute-start(f32[4,64]{1,0:T(4,128)S(1)} %get-tuple-element.52.refs_0_), channel_id=1, source_target_pairs={{0,4},{4,0},{8,12},{12,8},{16,20},{20,16},{24,28},{28,24},{1,5},{5... | collective-permute-start | bytes 3080 | tf_op jit(solution)/shard_map/ppermute | solution.py:27
  36.1 17.5 %collective-permute-start.12 = (bf16[1552,128]{1,0:T(8,128)(2,1)S(1)}, bf16[1552,128]{1,0:T(8,128)(2,1)S(1)}, u32[]{:S(2)}, u32[]{:S(2)}) collective-permute-start(bf16[1552,128]{1,0:T(8,128)(2,1)S(1)} %get-tuple-element.54), channel_id=1, source_target_pairs={{0,8},{4,12},{8,0},{12,4},{16,24},{20,28},{24,16},{28,20},{1,9},{5... | collective-permute-start | bytes 1191944 | tf_op jit(solution)/shard_map/ppermute | solution.py:27
  46.4 14.7 %copy-start.2 = (bf16[1024,1024]{1,0:T(8,128)(2,1)S(1)}, bf16[1024,1024]{1,0:T(8,128)(2,1)}, u32[]{:S(2)}) copy-start(bf16[1024,1024]{1,0:T(8,128)(2,1)} %refs_6_.1) | copy-start | bytes 6291460
  47.3 4.6 %collective-permute-start.17 = (bf16[4,256,128]{2,1,0:T(8,128)(2,1)S(1)}, bf16[4,256,128]{2,1,0:T(8,128)(2,1)S(1)}, u32[]{:S(2)}, u32[]{:S(2)}) collective-permute-start(bf16[4,256,128]{2,1,0:T(8,128)(2,1)S(1)} %shard_map.129), channel_id=1, source_target_pairs={{0,4},{4,0},{8,12},{12,8},{16,20},{20,16},{24,28},{28,24},{1,5},{5... | collective-permute-start | bytes 786440 | tf_op jit(solution)/shard_map/ppermute | solution.py:27
  47.4 13.7 %collective-permute-start.7 = (bf16[832,128]{1,0:T(8,128)(2,1)S(1)}, bf16[832,128]{1,0:T(8,128)(2,1)S(1)}, u32[]{:S(2)}, u32[]{:S(2)}) collective-permute-start(bf16[832,128]{1,0:T(8,128)(2,1)S(1)} %get-tuple-element.46), channel_id=1, source_target_pairs={{0,1},{1,0},{2,3},{3,2},{4,5},{5,4},{6,7},{7,6},{8,9},{9,8},{10,11... | collective-permute-start | bytes 638984 | tf_op jit(solution)/shard_map/ppermute | solution.py:27
  48.3 12.8 %collective-permute-start.8 = (bf16[832,128]{1,0:T(8,128)(2,1)S(1)}, bf16[832,128]{1,0:T(8,128)(2,1)S(1)}, u32[]{:S(2)}, u32[]{:S(2)}) collective-permute-start(bf16[832,128]{1,0:T(8,128)(2,1)S(1)} %get-tuple-element.47), channel_id=1, source_target_pairs={{0,2},{1,3},{2,0},{3,1},{4,6},{5,7},{6,4},{7,5},{8,10},{9,11},{10,... | collective-permute-start | bytes 638984 | tf_op jit(solution)/shard_map/ppermute | solution.py:27
  49.8 11.3 %copy-start = (bf16[1024,1024]{1,0:T(8,128)(2,1)S(1)}, bf16[1024,1024]{1,0:T(8,128)(2,1)}, u32[]{:S(2)}) copy-start(bf16[1024,1024]{1,0:T(8,128)(2,1)} %refs_4_.1) | copy-start | bytes 6291460
  49.8 11.3 %copy-start.1 = (bf16[1024,1024]{1,0:T(8,128)(2,1)S(1)}, bf16[1024,1024]{1,0:T(8,128)(2,1)}, u32[]{:S(2)}) copy-start(bf16[1024,1024]{1,0:T(8,128)(2,1)} %refs_5_.1) | copy-start | bytes 6291460
  49.8 11.3 %collective-permute-start.9 = (bf16[832,128]{1,0:T(8,128)(2,1)S(1)}, bf16[832,128]{1,0:T(8,128)(2,1)S(1)}, u32[]{:S(2)}, u32[]{:S(2)}) collective-permute-start(bf16[832,128]{1,0:T(8,128)(2,1)S(1)} %get-tuple-element.48), channel_id=1, source_target_pairs={{0,3},{1,2},{2,1},{3,0},{4,7},{5,6},{6,5},{7,4},{8,11},{9,10},{10,... | collective-permute-start | bytes 638984 | tf_op jit(solution)/shard_map/ppermute | solution.py:27
  52.0 6.5 %collective-permute-start.18 = (bf16[512,128]{1,0:T(8,128)(2,1)S(1)}, bf16[512,128]{1,0:T(8,128)(2,1)S(1)}, u32[]{:S(2)}, u32[]{:S(2)}) collective-permute-start(bf16[512,128]{1,0:T(8,128)(2,1)S(1)} %get-tuple-element.60), channel_id=1, source_target_pairs={{0,8},{4,12},{8,0},{12,4},{16,24},{20,28},{24,16},{28,20},{1,9},{5... | collective-permute-start | bytes 393224 | tf_op jit(solution)/shard_map/ppermute | solution.py:27
  53.7 14.3 %collective-permute-start.13 = (bf16[784,128]{1,0:T(8,128)(2,1)S(1)}, bf16[784,128]{1,0:T(8,128)(2,1)S(1)}, u32[]{:S(2)}, u32[]{:S(2)}) collective-permute-start(bf16[784,128]{1,0:T(8,128)(2,1)S(1)} %get-tuple-element.57), channel_id=1, source_target_pairs={{0,16},{4,20},{8,24},{12,28},{16,0},{20,4},{24,8},{28,12},{1,17},{... | collective-permute-start | bytes 602120 | tf_op jit(solution)/shard_map/ppermute | solution.py:27
  58.5 9.5 %collective-permute-start.19 = (bf16[256,128]{1,0:T(8,128)(2,1)S(1)}, bf16[256,128]{1,0:T(8,128)(2,1)S(1)}, u32[]{:S(2)}, u32[]{:S(2)}) collective-permute-start(bf16[256,128]{1,0:T(8,128)(2,1)S(1)} %get-tuple-element.62), channel_id=1, source_target_pairs={{0,16},{4,20},{8,24},{12,28},{16,0},{20,4},{24,8},{28,12},{1,17},{... | collective-permute-start | bytes 196616 | tf_op jit(solution)/shard_map/ppermute | solution.py:27

commit v4 on v3

--- a/solution.py
+++ b/solution.py
@@ -252,8 +252,11 @@
         ret_refs[b][3 * width :] = eig_sum[:, part].astype(BF16)
 
 
-def terms_kernel(base, pieces, target, ids_ref, *refs):
-    row_refs, (grads_ref, out_ref) = refs[:pieces], refs[pieces:]
+def terms_kernel(base, layout, target, ids_ref, *refs):
+    out_ref, operands, at = refs[-1], [], 0
+    for lanes, pieces in layout:
+        operands.append((refs[at], lanes, refs[at + 1 : at + 1 + pieces]))
+        at += 1 + pieces
     count = out_ref.shape[0]
 
     def columns(ref, index):
@@ -275,9 +278,12 @@
     group = 2 if count % 2 == 0 else 1
     for start in range(0, count, group):
         at = [ids_ref[base + start + i] for i in range(group)]
-        value = mm(grads_ref[...], right_of(row_refs, at)).astype(BF16)
-        for i in range(group):
-            out_ref[start + i] = value[:, i * target : (i + 1) * target]
+        row = 0
+        for left_ref, (low, high), pieces in operands:
+            value = mm(left_ref[low:high], right_of(pieces, at)).astype(BF16)
+            for i in range(group):
+                out_ref[start + i, row : row + high - low] = value[:, i * target : (i + 1) * target]
+            row += high - low
 
 
 def put_sums(ref, base, sums):
@@ -479,22 +485,31 @@
         ],
     )
 
-    def terms(base, left, pieces):
+    def terms(base, parts):
+        operands = [ids]
+        for left, _, pieces in parts:
+            operands += [left, *pieces]
+        layout = tuple((lanes, len(pieces)) for _, lanes, pieces in parts)
         return call(
-            functools.partial(terms_kernel, node_size + base, len(pieces), target),
-            [smem] + [vmem] * (len(pieces) + 1),
-            [((rest, left.shape[0], target), BF16)],
-            (ids, *pieces, left),
+            functools.partial(terms_kernel, node_size + base, layout, target),
+            [smem] + [vmem] * (len(operands) - 1),
+            [((rest, sum(high - low for low, high in (p[1] for p in parts)), target), BF16)],
+            operands,
             10**9,
             2**20,
         )[0]
 
     near_keeps, near_gots = [], []
-    for c, (left, pieces) in enumerate(((grads_t, rows), (out_t, cots))):
-        give_half = terms(0, left, pieces)
+    lanes = (0, 2 * width), (2 * width, 3 * width), (0, width)
+    plan = (
+        [(grads_t, lanes[0], rows)],
+        [(grads_t, lanes[1], rows), (out_t, lanes[2], cots)],
+    )
+    for c, products in enumerate(plan):
+        give_half = terms(0, products)
         got_half = give(give_half, "clus", 1, clus_size)
-        keep_half = terms(rest, left, pieces)
-        group_rows = left.shape[0]
+        keep_half = terms(rest, products)
+        group_rows = keep_half.shape[1]
         operands = [keep_half, got_half]
         shapes = [
             ((pairs * group_rows + (16 if c == 0 else 0), target), BF16),

time: 69.2 us -> 65.3 us (0.944)
  starting transfers between devices: 26 us -> 23.2 us
  waiting for transfers between devices: 24.6 us -> 22.7 us
  Pallas kernels: 17.4 us -> 18.2 us
    ppermute x20, starting transfers between devices: 26 us -> 23.2 us  [take(): return lax.ppermute(value, axis, pairs)]
    ppermute x20, waiting for transfers between devices: 24.6 us -> 22.7 us  [take(): return lax.ppermute(value, axis, pairs)]
    pallas_call x13, Pallas kernels: 17.4 us -> 18.2 us  [call_here(): pl.pallas_call(kernel, in_specs=in_specs, out_specs=[vmem] * len(out_shap...]
  transfers between devices with their start and end apart: 20 -> 20, of which waited for: 10 -> 10; matrix products, arithmetic and copies ran while one was open for 0% -> 0% of each run, Pallas kernels for 14% -> 26%
where the time goes in v4:
time: 65.3 us; the launch traced here: 65.2 us
  starting transfers between devices  23.2 us (36%)
  waiting for transfers between devices  22.7 us (35%)
  Pallas kernels  18.2 us (28%)
  between operations  0.82 us (1%)
    ppermute x20, starting transfers between devices, take(): return lax.ppermute(value, axis, pairs)  23.2 us
    ppermute x20, waiting for transfers between devices, take(): return lax.ppermute(value, axis, pairs)  22.7 us
    pallas_call x13, Pallas kernels, call_here(): pl.pallas_call(kernel, in_specs=in_specs, out_specs=[vmem] * len(out_shap...  18.2 us
  transfers between devices with their start and end apart: 20, of which 10 were waited for; matrix products, arithmetic and copies ran while one was open for 0% of the time, Pallas kernels for 26%

profile of v4, /device:TPU:0, one launch (start us, length us, event | category | flops | bytes accessed | tf_op | source)
XLA Modules:
  0.0 65.2 jit_solution(8083862320797978414)
XLA Ops:
  0.6 3.0 %collective-permute-start = (bf16[128,1024]{1,0:T(8,128)(2,1)}, bf16[128,1024]{1,0:T(8,128)(2,1)S(1)}, u32[]{:S(2)}, u32[]{:S(2)}) collective-permute-start(bf16[128,1024]{1,0:T(8,128)(2,1)} %bitcast.14), channel_id=1, source_target_pairs={{0,1},{1,0},{2,3},{3,2},{4,5},{5,4},{6,7},{7,6},{8,9},{9,8},{10,11... | collective-permute-start | bytes 786440 | tf_op jit(solution)/shard_map/ppermute | solution.py:27
  3.7 1.5 %collective-permute-start.1 = (bf16[128,1024]{1,0:T(8,128)(2,1)}, bf16[128,1024]{1,0:T(8,128)(2,1)S(1)}, u32[]{:S(2)}, u32[]{:S(2)}) collective-permute-start(bf16[128,1024]{1,0:T(8,128)(2,1)} %bitcast.15), channel_id=1, source_target_pairs={{0,2},{1,3},{2,0},{3,1},{4,6},{5,7},{6,4},{7,5},{8,10},{9,11},{10,... | collective-permute-start | bytes 786440 | tf_op jit(solution)/shard_map/ppermute | solution.py:27
  5.2 5.0 %collective-permute-done.first_ref.refs_1_.refs_2_ = bf16[128,1024]{1,0:T(8,128)(2,1)S(1)} collective-permute-done((bf16[128,1024]{1,0:T(8,128)(2,1)}, bf16[128,1024]{1,0:T(8,128)(2,1)S(1)}, u32[]{:S(2)}, u32[]{:S(2)}) %collective-permute-start) | collective-permute-done | bytes 262176 | tf_op jit(solution)/shard_map/ppermute | solution.py:27
  10.2 1.5 %collective-permute-done.1.second_ref.refs_2_.refs_3_ = bf16[128,1024]{1,0:T(8,128)(2,1)S(1)} collective-permute-done((bf16[128,1024]{1,0:T(8,128)(2,1)}, bf16[128,1024]{1,0:T(8,128)(2,1)S(1)}, u32[]{:S(2)}, u32[]{:S(2)}) %collective-permute-start.1) | collective-permute-done | bytes 262176 | tf_op jit(solution)/shard_map/ppermute | solution.py:27
  11.7 0.4 collective-permute-start.2
  12.1 1.7 %collective-permute-start.3 = (bf16[64,1024]{1,0:T(8,128)(2,1)S(1)}, bf16[64,1024]{1,0:T(8,128)(2,1)S(1)}, u32[]{:S(2)}, u32[]{:S(2)}) collective-permute-start(bf16[64,1024]{1,0:T(8,128)(2,1)S(1)} %get-tuple-element.36), channel_id=1, source_target_pairs={{0,2},{1,3},{2,0},{3,1},{4,6},{5,7},{6,4},{7,5},{8,10},{9,11},{10,... | collective-permute-start | bytes 393224 | tf_op jit(solution)/shard_map/ppermute | solution.py:27
  13.8 0.1 pad_add_fusion.ids_ref
  13.9 0.0 copy-start.7
  13.9 3.6 %shard_map.121 = (bf16[128,256]{1,0:T(8,128)(2,1)S(1)}, bf16[128,256]{1,0:T(8,128)(2,1)}, bf16[128,256]{1,0:T(8,128)(2,1)}, bf16[128,256]{1,0:T(8,128)(2,1)}, bf...) custom-call(s32[12]{0:T(128)S(1)} %pad_add_fusion.ids_ref, ...), custom_call_target="tpu_custom_call" | custom-call | flops 300000000 | bytes 3145728 | tf_op jit(solution)/shard_map/pallas_call | solution.py:412
  17.4 1.6 %collective-permute-start.4 = (bf16[128,256]{1,0:T(8,128)(2,1)}, bf16[128,256]{1,0:T(8,128)(2,1)S(1)}, u32[]{:S(2)}, u32[]{:S(2)}) collective-permute-start(bf16[128,256]{1,0:T(8,128)(2,1)} %get-tuple-element.38), channel_id=1, source_target_pairs={{0,1},{1,0},{2,3},{3,2},{4,5},{5,4},{6,7},{7,6},{8,9},{9,8},{10,11... | collective-permute-start | bytes 196616 | tf_op jit(solution)/shard_map/ppermute | solution.py:27
  19.0 0.5 collective-permute-start.5
  19.5 1.5 %collective-permute-start.6 = (bf16[128,256]{1,0:T(8,128)(2,1)}, bf16[128,256]{1,0:T(8,128)(2,1)S(1)}, u32[]{:S(2)}, u32[]{:S(2)}) collective-permute-start(bf16[128,256]{1,0:T(8,128)(2,1)} %get-tuple-element.40), channel_id=1, source_target_pairs={{0,3},{1,2},{2,1},{3,0},{4,7},{5,6},{6,5},{7,4},{8,11},{9,10},{10,... | collective-permute-start | bytes 196616 | tf_op jit(solution)/shard_map/ppermute | solution.py:27
  21.0 0.0 copy-done.4
  21.0 0.1 copy.13
  21.1 1.6 %collective-permute-done.4.refs_6_ = bf16[128,256]{1,0:T(8,128)(2,1)S(1)} collective-permute-done((bf16[128,256]{1,0:T(8,128)(2,1)}, bf16[128,256]{1,0:T(8,128)(2,1)S(1)}, u32[]{:S(2)}, u32[]{:S(2)}) %collective-permute-start.4) | collective-permute-done | bytes 65568 | tf_op jit(solution)/shard_map/ppermute | solution.py:27
  22.7 0.0 copy-done.3
  22.7 1.2 %collective-permute-start.14 = (bf16[128,1024]{1,0:T(8,128)(2,1)S(1)}, bf16[128,1024]{1,0:T(8,128)(2,1)S(1)}, u32[]{:S(2)}, u32[]{:S(2)}) collective-permute-start(bf16[128,1024]{1,0:T(8,128)(2,1)S(1)} %bitcast.8), channel_id=1, source_target_pairs={{0,1},{1,0},{2,3},{3,2},{4,5},{5,4},{6,7},{7,6},{8,9},{9,8},{10,11... | collective-permute-start | bytes 786440 | tf_op jit(solution)/shard_map/ppermute | solution.py:27
  23.9 0.3 collective-permute-done.5.refs_7_
  24.2 0.5 collective-permute-start.15
  24.7 0.9 %collective-permute-done.6.refs_8_ = bf16[128,256]{1,0:T(8,128)(2,1)S(1)} collective-permute-done((bf16[128,256]{1,0:T(8,128)(2,1)}, bf16[128,256]{1,0:T(8,128)(2,1)S(1)}, u32[]{:S(2)}, u32[]{:S(2)}) %collective-permute-start.6) | collective-permute-done | bytes 65568 | tf_op jit(solution)/shard_map/ppermute | solution.py:27
  25.6 1.5 %collective-permute-start.16 = (bf16[128,1024]{1,0:T(8,128)(2,1)S(1)}, bf16[128,1024]{1,0:T(8,128)(2,1)S(1)}, u32[]{:S(2)}, u32[]{:S(2)}) collective-permute-start(bf16[128,1024]{1,0:T(8,128)(2,1)S(1)} %bitcast.10), channel_id=1, source_target_pairs={{0,3},{1,2},{2,1},{3,0},{4,7},{5,6},{6,5},{7,4},{8,11},{9,10},{10,... | collective-permute-start | bytes 786440 | tf_op jit(solution)/shard_map/ppermute | solution.py:27
  27.1 0.0 collective-permute-done.2.refs_3_.refs_4_
  27.1 0.0 collective-permute-done.3.refs_4_.refs_5_
  27.1 0.0 copy-done.5
  27.1 0.0 copy-done.6
  27.1 0.0 copy-done.7
  27.1 5.8 %shard_map.122 = (bf16[768,512]{1,0:T(8,128)(2,1)S(1)}, bf16[256,512]{1,0:T(8,128)(2,1)S(1)}, f32[4,64]{1,0:T(4,128)S(1)}, f32[64,128]{1,0:T(8,128)S(1)}, bf16[8...) custom-call(s32[12]{0:T(128)S(1)} %pad_add_fusion.ids_ref, ...), custom_call_target="tpu_custom_call" | custom-call | flops 8000000000 | bytes 8388608 | tf_op jit(solution)/shard_map/pallas_call | solution.py:412
  32.9 1.0 %shard_map.125 = bf16[4,512,128]{2,1,0:T(8,128)(2,1)S(1)} custom-call(s32[12]{0:T(128)S(1)} %pad_add_fusion.ids_ref, bf16[768,512]{1,0:T(8,128)(2,1)S(1)} %get-tuple-element.51.refs_0_, bf16[128,1024]{1,0:T(8,128)(2,1)S(1)} %bitcast.17, bf16[128,1024]{1,0:T(8,128)(2,1)S(1)} %collective-permute-done.first_ref.refs_1_.refs_2_, ...), custom_call_target="tpu_custom_call" | custom-call | flops 1000000000 | bytes 1048576 | tf_op jit(solution)/shard_map/pallas_call | solution.py:412
  34.0 0.1 collective-permute-start.10
  34.1 0.0 collective-permute-done.14.refs_8_
  34.1 1.3 %collective-permute-done.15.refs_9_ = bf16[128,1024]{1,0:T(8,128)(2,1)S(1)} collective-permute-done((bf16[128,1024]{1,0:T(8,128)(2,1)S(1)}, bf16[128,1024]{1,0:T(8,128)(2,1)S(1)}, u32[]{:S(2)}, u32[]{:S(2)}) %collective-permute-start.15) | collective-permute-done | bytes 262176 | tf_op jit(solution)/shard_map/ppermute | solution.py:27
  35.4 0.0 collective-permute-done.16.refs_10_
  35.4 1.1 %shard_map.129 = bf16[4,512,128]{2,1,0:T(8,128)(2,1)S(1)} custom-call(s32[12]{0:T(128)S(1)} %pad_add_fusion.ids_ref, bf16[768,512]{1,0:T(8,128)(2,1)S(1)} %get-tuple-element.51.refs_0_, bf16[128,1024]{1,0:T(8,128)(2,1)S(1)} %bitcast.18, bf16[128,1024]{1,0:T(8,128)(2,1)S(1)} %collective-permute-done.first_ref.refs_1_.refs_2_, ...), custom_call_target="tpu_custom_call" | custom-call | flops 1000000000 | bytes 1048576 | tf_op jit(solution)/shard_map/pallas_call | solution.py:412
  36.5 0.1 collective-permute-start.17
  36.6 0.5 collective-permute-start.11
  37.1 1.0 %shard_map.124.keep_ref = bf16[4,512,128]{2,1,0:T(8,128)(2,1)S(1)} custom-call(s32[12]{0:T(128)S(1)} %pad_add_fusion.ids_ref, bf16[768,512]{1,0:T(8,128)(2,1)S(1)} %get-tuple-element.51.refs_0_, bf16[128,1024]{1,0:T(8,128)(2,1)S(1)} %bitcast.19, bf16[128,1024]{1,0:T(8,128)(2,1)S(1)} %collective-permute-done.first_ref.refs_1_.refs_2_, ...), custom_call_target="tpu_custom_call" | custom-call | flops 1000000000 | bytes 1048576 | tf_op jit(solution)/shard_map/pallas_call | solution.py:412
  38.2 0.4 collective-permute-done.11.refs_1_
  38.5 0.0 collective-permute-done.10.got_ref
  38.5 0.1 shard_map.126
  38.6 1.6 %collective-permute-start.12 = (bf16[1040,128]{1,0:T(8,128)(2,1)S(1)}, bf16[1040,128]{1,0:T(8,128)(2,1)S(1)}, u32[]{:S(2)}, u32[]{:S(2)}) collective-permute-start(bf16[1040,128]{1,0:T(8,128)(2,1)S(1)} %get-tuple-element.54), channel_id=1, source_target_pairs={{0,8},{4,12},{8,0},{12,4},{16,24},{20,28},{24,16},{28,20},{1,9},{5... | collective-permute-start | bytes 798728 | tf_op jit(solution)/shard_map/ppermute | solution.py:27
  40.3 1.1 %shard_map.128.keep_ref = bf16[4,512,128]{2,1,0:T(8,128)(2,1)S(1)} custom-call(s32[12]{0:T(128)S(1)} %pad_add_fusion.ids_ref, bf16[768,512]{1,0:T(8,128)(2,1)S(1)} %get-tuple-element.51.refs_0_, bf16[128,1024]{1,0:T(8,128)(2,1)S(1)} %bitcast.20, bf16[128,1024]{1,0:T(8,128)(2,1)S(1)} %collective-permute-done.first_ref.refs_1_.refs_2_, ...), custom_call_target="tpu_custom_call" | custom-call | flops 1000000000 | bytes 1048576 | tf_op jit(solution)/shard_map/pallas_call | solution.py:412
  41.4 0.0 copy-start
  41.4 0.0 collective-permute-done.17.got_ref
  41.4 0.1 shard_map.130
  41.5 0.5 collective-permute-start.18
  42.0 0.5 collective-permute-start.7
  42.6 0.9 %collective-permute-start.8 = (bf16[832,128]{1,0:T(8,128)(2,1)S(1)}, bf16[832,128]{1,0:T(8,128)(2,1)S(1)}, u32[]{:S(2)}, u32[]{:S(2)}) collective-permute-start(bf16[832,128]{1,0:T(8,128)(2,1)S(1)} %get-tuple-element.47), channel_id=1, source_target_pairs={{0,2},{1,3},{2,0},{3,1},{4,6},{5,7},{6,4},{7,5},{8,10},{9,11},{10,... | collective-permute-start | bytes 638984 | tf_op jit(solution)/shard_map/ppermute | solution.py:27
  43.5 2.0 %collective-permute-start.9 = (bf16[832,128]{1,0:T(8,128)(2,1)S(1)}, bf16[832,128]{1,0:T(8,128)(2,1)S(1)}, u32[]{:S(2)}, u32[]{:S(2)}) collective-permute-start(bf16[832,128]{1,0:T(8,128)(2,1)S(1)} %get-tuple-element.48), channel_id=1, source_target_pairs={{0,3},{1,2},{2,1},{3,0},{4,7},{5,6},{6,5},{7,4},{8,11},{9,10},{10,... | collective-permute-start | bytes 638984 | tf_op jit(solution)/shard_map/ppermute | solution.py:27
  45.5 2.4 %collective-permute-done.12.got_ref = bf16[1040,128]{1,0:T(8,128)(2,1)S(1)} collective-permute-done((bf16[1040,128]{1,0:T(8,128)(2,1)S(1)}, bf16[1040,128]{1,0:T(8,128)(2,1)S(1)}, u32[]{:S(2)}, u32[]{:S(2)}) %collective-permute-start.12) | collective-permute-done | bytes 266272 | tf_op jit(solution)/shard_map/ppermute | solution.py:27
  48.0 0.1 shard_map.127
  48.0 2.7 %collective-permute-start.13 = (bf16[528,128]{1,0:T(8,128)(2,1)S(1)}, bf16[528,128]{1,0:T(8,128)(2,1)S(1)}, u32[]{:S(2)}, u32[]{:S(2)}) collective-permute-start(bf16[528,128]{1,0:T(8,128)(2,1)S(1)} %get-tuple-element.57), channel_id=1, source_target_pairs={{0,16},{4,20},{8,24},{12,28},{16,0},{20,4},{24,8},{28,12},{1,17},{... | collective-permute-start | bytes 405512 | tf_op jit(solution)/shard_map/ppermute | solution.py:27
  50.7 5.0 %collective-permute-done.18.got_ref = bf16[1024,128]{1,0:T(8,128)(2,1)S(1)} collective-permute-done((bf16[1024,128]{1,0:T(8,128)(2,1)S(1)}, bf16[1024,128]{1,0:T(8,128)(2,1)S(1)}, u32[]{:S(2)}, u32[]{:S(2)}) %collective-permute-start.18) | collective-permute-done | bytes 262176 | tf_op jit(solution)/shard_map/ppermute | solution.py:27
  55.6 0.1 shard_map.131
  55.7 0.8 %collective-permute-start.19 = (bf16[512,128]{1,0:T(8,128)(2,1)S(1)}, bf16[512,128]{1,0:T(8,128)(2,1)S(1)}, u32[]{:S(2)}, u32[]{:S(2)}) collective-permute-start(bf16[512,128]{1,0:T(8,128)(2,1)S(1)} %get-tuple-element.62), channel_id=1, source_target_pairs={{0,16},{4,20},{8,24},{12,28},{16,0},{20,4},{24,8},{28,12},{1,17},{... | collective-permute-start | bytes 393224 | tf_op jit(solution)/shard_map/ppermute | solution.py:27
  56.5 0.0 collective-permute-done.7.refs_1_
  56.5 0.0 collective-permute-done.8.refs_2_
  56.5 0.0 collective-permute-done.9.refs_3_
  56.5 0.0 copy-done.1
  56.5 0.0 copy-done.2
  56.6 0.0 copy-done
  56.6 3.2 %shard_map.123 = (bf16[128,1024]{1,0:T(8,128)(2,1)}, f32[64,128]{1,0:T(8,128)}) custom-call(s32[12]{0:T(128)S(1)} %pad_add_fusion.ids_ref, f32[64,128]{1,0:T(8,128)S(1)} %get-tuple-element.44.eig_ref, bf16[832,128]{1,0:T(8,128)(2,1)S(1)} %get-tuple-element.45.refs_0_, bf16[832,128]{1,0:T(8,128)(2,1)S(1)} %collective-permute-done.7.refs_1_, ...), custom_call_target="tpu_custom_call" | custom-call | flops 1000000000 | bytes 7340032 | tf_op jit(solution)/shard_map/pallas_call | solution.py:412
  59.8 4.4 %collective-permute-done.19.refs_3_ = bf16[512,128]{1,0:T(8,128)(2,1)S(1)} collective-permute-done((bf16[512,128]{1,0:T(8,128)(2,1)S(1)}, bf16[512,128]{1,0:T(8,128)(2,1)S(1)}, u32[]{:S(2)}, u32[]{:S(2)}) %collective-permute-start.19) | collective-permute-done | bytes 131104 | tf_op jit(solution)/shard_map/ppermute | solution.py:27
  64.2 0.0 collective-permute-done.13.refs_1_
  64.2 1.0 %shard_map.132 = (f32[4,128,256]{2,1,0:T(8,128)}, f32[4,64]{1,0:T(4,128)}) custom-call(f32[512,128]{1,0:T(8,128)S(1)} %get-tuple-element.56.refs_0_, bf16[528,128]{1,0:T(8,128)(2,1)S(1)} %collective-permute-done.13.refs_1_, f32[512,128]{1,0:T(8,128)S(1)} %get-tuple-element.61.refs_2_, bf16[512,128]{1,0:T(8,128)(2,1)S(1)} %collective-permute-done.19.refs_3_, ...), custom_call_target="tpu_custom_call" | custom-call | flops 1000000 | bytes 2097152 | tf_op jit(solution)/shard_map/pallas_call | solution.py:412
  (9 shorter events, 0.0 us)
Async XLA Ops:
  0.6 9.6 %collective-permute-start = (bf16[128,1024]{1,0:T(8,128)(2,1)}, bf16[128,1024]{1,0:T(8,128)(2,1)S(1)}, u32[]{:S(2)}, u32[]{:S(2)}) collective-permute-start(bf16[128,1024]{1,0:T(8,128)(2,1)} %bitcast.14), channel_id=1, source_target_pairs={{0,1},{1,0},{2,3},{3,2},{4,5},{5,4},{6,7},{7,6},{8,9},{9,8},{10,11... | collective-permute-start | bytes 786440 | tf_op jit(solution)/shard_map/ppermute | solution.py:27
  3.7 8.0 %collective-permute-start.1 = (bf16[128,1024]{1,0:T(8,128)(2,1)}, bf16[128,1024]{1,0:T(8,128)(2,1)S(1)}, u32[]{:S(2)}, u32[]{:S(2)}) collective-permute-start(bf16[128,1024]{1,0:T(8,128)(2,1)} %bitcast.15), channel_id=1, source_target_pairs={{0,2},{1,3},{2,0},{3,1},{4,6},{5,7},{6,4},{7,5},{8,10},{9,11},{10,... | collective-permute-start | bytes 786440 | tf_op jit(solution)/shard_map/ppermute | solution.py:27
  11.7 15.4 %collective-permute-start.2 = (bf16[64,1024]{1,0:T(8,128)(2,1)S(1)}, bf16[64,1024]{1,0:T(8,128)(2,1)S(1)}, u32[]{:S(2)}, u32[]{:S(2)}) collective-permute-start(bf16[64,1024]{1,0:T(8,128)(2,1)S(1)} %get-tuple-element.35), channel_id=1, source_target_pairs={{0,1},{1,0},{2,3},{3,2},{4,5},{5,4},{6,7},{7,6},{8,9},{9,8},{10,11... | collective-permute-start | bytes 393224 | tf_op jit(solution)/shard_map/ppermute | solution.py:27
  12.1 15.0 %collective-permute-start.3 = (bf16[64,1024]{1,0:T(8,128)(2,1)S(1)}, bf16[64,1024]{1,0:T(8,128)(2,1)S(1)}, u32[]{:S(2)}, u32[]{:S(2)}) collective-permute-start(bf16[64,1024]{1,0:T(8,128)(2,1)S(1)} %get-tuple-element.36), channel_id=1, source_target_pairs={{0,2},{1,3},{2,0},{3,1},{4,6},{5,7},{6,4},{7,5},{8,10},{9,11},{10,... | collective-permute-start | bytes 393224 | tf_op jit(solution)/shard_map/ppermute | solution.py:27
  13.9 7.1 %copy-start.4 = (f32[4,64]{1,0:T(4,128)S(1)}, f32[4,64]{1,0:T(4,128)}, u32[]{:S(2)}) copy-start(f32[4,64]{1,0:T(4,128)} %refs_13_.1) | copy-start | bytes 3076
  13.9 8.8 %copy-start.3 = (bf16[1,128,1024]{2,1,0:T(8,128)(2,1)S(1)}, bf16[1,128,1024]{2,1,0:T(8,128)(2,1)}, u32[]{:S(2)}) copy-start(bf16[1,128,1024]{2,1,0:T(8,128)(2,1)} %param.10) | copy-start | bytes 786436
  13.9 13.2 %copy-start.5 = (bf16[1,128,1024]{2,1,0:T(8,128)(2,1)S(1)}, bf16[1,128,1024]{2,1,0:T(8,128)(2,1)}, u32[]{:S(2)}) copy-start(bf16[1,128,1024]{2,1,0:T(8,128)(2,1)} %param.9) | copy-start | bytes 786436
  13.9 13.2 %copy-start.6 = (bf16[1,64,512]{2,1,0:T(8,128)(2,1)S(1)}, bf16[1,64,512]{2,1,0:T(8,128)(2,1)}, u32[]{:S(2)}) copy-start(bf16[1,64,512]{2,1,0:T(8,128)(2,1)} %param.15) | copy-start | bytes 196612
  13.9 13.2 %copy-start.7 = (s32[1,4,4,4]{3,2,1,0:T(4,128)S(1)}, s32[1,4,4,4]{3,2,1,0:T(4,128)}, u32[]{:S(2)}) copy-start(s32[1,4,4,4]{3,2,1,0:T(4,128)} %param.17) | copy-start | bytes 772
  17.4 5.2 %collective-permute-start.4 = (bf16[128,256]{1,0:T(8,128)(2,1)}, bf16[128,256]{1,0:T(8,128)(2,1)S(1)}, u32[]{:S(2)}, u32[]{:S(2)}) collective-permute-start(bf16[128,256]{1,0:T(8,128)(2,1)} %get-tuple-element.38), channel_id=1, source_target_pairs={{0,1},{1,0},{2,3},{3,2},{4,5},{5,4},{6,7},{7,6},{8,9},{9,8},{10,11... | collective-permute-start | bytes 196616 | tf_op jit(solution)/shard_map/ppermute | solution.py:27
  19.0 5.2 %collective-permute-start.5 = (bf16[128,256]{1,0:T(8,128)(2,1)}, bf16[128,256]{1,0:T(8,128)(2,1)S(1)}, u32[]{:S(2)}, u32[]{:S(2)}) collective-permute-start(bf16[128,256]{1,0:T(8,128)(2,1)} %get-tuple-element.39), channel_id=1, source_target_pairs={{0,2},{1,3},{2,0},{3,1},{4,6},{5,7},{6,4},{7,5},{8,10},{9,11},{10,... | collective-permute-start | bytes 196616 | tf_op jit(solution)/shard_map/ppermute | solution.py:27
  19.5 6.1 %collective-permute-start.6 = (bf16[128,256]{1,0:T(8,128)(2,1)}, bf16[128,256]{1,0:T(8,128)(2,1)S(1)}, u32[]{:S(2)}, u32[]{:S(2)}) collective-permute-start(bf16[128,256]{1,0:T(8,128)(2,1)} %get-tuple-element.40), channel_id=1, source_target_pairs={{0,3},{1,2},{2,1},{3,0},{4,7},{5,6},{6,5},{7,4},{8,11},{9,10},{10,... | collective-permute-start | bytes 196616 | tf_op jit(solution)/shard_map/ppermute | solution.py:27
  22.7 11.4 %collective-permute-start.14 = (bf16[128,1024]{1,0:T(8,128)(2,1)S(1)}, bf16[128,1024]{1,0:T(8,128)(2,1)S(1)}, u32[]{:S(2)}, u32[]{:S(2)}) collective-permute-start(bf16[128,1024]{1,0:T(8,128)(2,1)S(1)} %bitcast.8), channel_id=1, source_target_pairs={{0,1},{1,0},{2,3},{3,2},{4,5},{5,4},{6,7},{7,6},{8,9},{9,8},{10,11... | collective-permute-start | bytes 786440 | tf_op jit(solution)/shard_map/ppermute | solution.py:27
  24.2 11.3 %collective-permute-start.15 = (bf16[128,1024]{1,0:T(8,128)(2,1)S(1)}, bf16[128,1024]{1,0:T(8,128)(2,1)S(1)}, u32[]{:S(2)}, u32[]{:S(2)}) collective-permute-start(bf16[128,1024]{1,0:T(8,128)(2,1)S(1)} %bitcast.9), channel_id=1, source_target_pairs={{0,2},{1,3},{2,0},{3,1},{4,6},{5,7},{6,4},{7,5},{8,10},{9,11},{10,... | collective-permute-start | bytes 786440 | tf_op jit(solution)/shard_map/ppermute | solution.py:27
  25.6 9.8 %collective-permute-start.16 = (bf16[128,1024]{1,0:T(8,128)(2,1)S(1)}, bf16[128,1024]{1,0:T(8,128)(2,1)S(1)}, u32[]{:S(2)}, u32[]{:S(2)}) collective-permute-start(bf16[128,1024]{1,0:T(8,128)(2,1)S(1)} %bitcast.10), channel_id=1, source_target_pairs={{0,3},{1,2},{2,1},{3,0},{4,7},{5,6},{6,5},{7,4},{8,11},{9,10},{10,... | collective-permute-start | bytes 786440 | tf_op jit(solution)/shard_map/ppermute | solution.py:27
  34.0 4.5 %collective-permute-start.10 = (bf16[4,512,128]{2,1,0:T(8,128)(2,1)S(1)}, bf16[4,512,128]{2,1,0:T(8,128)(2,1)S(1)}, u32[]{:S(2)}, u32[]{:S(2)}) collective-permute-start(bf16[4,512,128]{2,1,0:T(8,128)(2,1)S(1)} %shard_map.125), channel_id=1, source_target_pairs={{0,4},{4,0},{8,12},{12,8},{16,20},{20,16},{24,28},{28,24},{1,5},{5... | collective-permute-start | bytes 1572872 | tf_op jit(solution)/shard_map/ppermute | solution.py:27
  36.5 4.9 %collective-permute-start.17 = (bf16[4,512,128]{2,1,0:T(8,128)(2,1)S(1)}, bf16[4,512,128]{2,1,0:T(8,128)(2,1)S(1)}, u32[]{:S(2)}, u32[]{:S(2)}) collective-permute-start(bf16[4,512,128]{2,1,0:T(8,128)(2,1)S(1)} %shard_map.129), channel_id=1, source_target_pairs={{0,4},{4,0},{8,12},{12,8},{16,20},{20,16},{24,28},{28,24},{1,5},{5... | collective-permute-start | bytes 1572872 | tf_op jit(solution)/shard_map/ppermute | solution.py:27
  36.6 1.9 %collective-permute-start.11 = (f32[4,64]{1,0:T(4,128)S(1)}, f32[4,64]{1,0:T(4,128)S(1)}, u32[]{:S(2)}, u32[]{:S(2)}) collective-permute-start(f32[4,64]{1,0:T(4,128)S(1)} %get-tuple-element.52.refs_0_), channel_id=1, source_target_pairs={{0,4},{4,0},{8,12},{12,8},{16,20},{20,16},{24,28},{28,24},{1,5},{5... | collective-permute-start | bytes 3080 | tf_op jit(solution)/shard_map/ppermute | solution.py:27
  38.6 9.3 %collective-permute-start.12 = (bf16[1040,128]{1,0:T(8,128)(2,1)S(1)}, bf16[1040,128]{1,0:T(8,128)(2,1)S(1)}, u32[]{:S(2)}, u32[]{:S(2)}) collective-permute-start(bf16[1040,128]{1,0:T(8,128)(2,1)S(1)} %get-tuple-element.54), channel_id=1, source_target_pairs={{0,8},{4,12},{8,0},{12,4},{16,24},{20,28},{24,16},{28,20},{1,9},{5... | collective-permute-start | bytes 798728 | tf_op jit(solution)/shard_map/ppermute | solution.py:27
  40.3 16.3 %copy-start.1 = (bf16[1024,1024]{1,0:T(8,128)(2,1)S(1)}, bf16[1024,1024]{1,0:T(8,128)(2,1)}, u32[]{:S(2)}) copy-start(bf16[1024,1024]{1,0:T(8,128)(2,1)} %refs_5_.1) | copy-start | bytes 6291460
  40.3 16.3 %copy-start.2 = (bf16[1024,1024]{1,0:T(8,128)(2,1)S(1)}, bf16[1024,1024]{1,0:T(8,128)(2,1)}, u32[]{:S(2)}) copy-start(bf16[1024,1024]{1,0:T(8,128)(2,1)} %refs_6_.1) | copy-start | bytes 6291460
  41.4 15.2 %copy-start = (bf16[1024,1024]{1,0:T(8,128)(2,1)S(1)}, bf16[1024,1024]{1,0:T(8,128)(2,1)}, u32[]{:S(2)}) copy-start(bf16[1024,1024]{1,0:T(8,128)(2,1)} %refs_4_.1) | copy-start | bytes 6291460
  41.5 14.1 %collective-permute-start.18 = (bf16[1024,128]{1,0:T(8,128)(2,1)S(1)}, bf16[1024,128]{1,0:T(8,128)(2,1)S(1)}, u32[]{:S(2)}, u32[]{:S(2)}) collective-permute-start(bf16[1024,128]{1,0:T(8,128)(2,1)S(1)} %get-tuple-element.60), channel_id=1, source_target_pairs={{0,8},{4,12},{8,0},{12,4},{16,24},{20,28},{24,16},{28,20},{1,9},{5... | collective-permute-start | bytes 786440 | tf_op jit(solution)/shard_map/ppermute | solution.py:27
  42.0 14.5 %collective-permute-start.7 = (bf16[832,128]{1,0:T(8,128)(2,1)S(1)}, bf16[832,128]{1,0:T(8,128)(2,1)S(1)}, u32[]{:S(2)}, u32[]{:S(2)}) collective-permute-start(bf16[832,128]{1,0:T(8,128)(2,1)S(1)} %get-tuple-element.46), channel_id=1, source_target_pairs={{0,1},{1,0},{2,3},{3,2},{4,5},{5,4},{6,7},{7,6},{8,9},{9,8},{10,11... | collective-permute-start | bytes 638984 | tf_op jit(solution)/shard_map/ppermute | solution.py:27
  42.6 14.0 %collective-permute-start.8 = (bf16[832,128]{1,0:T(8,128)(2,1)S(1)}, bf16[832,128]{1,0:T(8,128)(2,1)S(1)}, u32[]{:S(2)}, u32[]{:S(2)}) collective-permute-start(bf16[832,128]{1,0:T(8,128)(2,1)S(1)} %get-tuple-element.47), channel_id=1, source_target_pairs={{0,2},{1,3},{2,0},{3,1},{4,6},{5,7},{6,4},{7,5},{8,10},{9,11},{10,... | collective-permute-start | bytes 638984 | tf_op jit(solution)/shard_map/ppermute | solution.py:27
  43.5 13.0 %collective-permute-start.9 = (bf16[832,128]{1,0:T(8,128)(2,1)S(1)}, bf16[832,128]{1,0:T(8,128)(2,1)S(1)}, u32[]{:S(2)}, u32[]{:S(2)}) collective-permute-start(bf16[832,128]{1,0:T(8,128)(2,1)S(1)} %get-tuple-element.48), channel_id=1, source_target_pairs={{0,3},{1,2},{2,1},{3,0},{4,7},{5,6},{6,5},{7,4},{8,11},{9,10},{10,... | collective-permute-start | bytes 638984 | tf_op jit(solution)/shard_map/ppermute | solution.py:27
  48.0 16.2 %collective-permute-start.13 = (bf16[528,128]{1,0:T(8,128)(2,1)S(1)}, bf16[528,128]{1,0:T(8,128)(2,1)S(1)}, u32[]{:S(2)}, u32[]{:S(2)}) collective-permute-start(bf16[528,128]{1,0:T(8,128)(2,1)S(1)} %get-tuple-element.57), channel_id=1, source_target_pairs={{0,16},{4,20},{8,24},{12,28},{16,0},{20,4},{24,8},{28,12},{1,17},{... | collective-permute-start | bytes 405512 | tf_op jit(solution)/shard_map/ppermute | solution.py:27
  55.7 8.5 %collective-permute-start.19 = (bf16[512,128]{1,0:T(8,128)(2,1)S(1)}, bf16[512,128]{1,0:T(8,128)(2,1)S(1)}, u32[]{:S(2)}, u32[]{:S(2)}) collective-permute-start(bf16[512,128]{1,0:T(8,128)(2,1)S(1)} %get-tuple-element.62), channel_id=1, source_target_pairs={{0,16},{4,20},{8,24},{12,28},{16,0},{20,4},{24,8},{28,12},{1,17},{... | collective-permute-start | bytes 393224 | tf_op jit(solution)/shard_map/ppermute | solution.py:27

commit v5 on v4

--- a/solution.py
+++ b/solution.py
@@ -69,18 +69,69 @@
         c.wait()
 
 
-def split_kernel(first_ref, second_ref, top_ref, bottom_ref):
-    half = top_ref.shape[0]
-    top_ref[...] = second_ref[:half]
-    bottom_ref[...] = first_ref[half:]
-
-
-def attention_kernel(scale, heads, head_size, blocks, pieces, ids_ref, mask_ref, *refs):
-    row_refs, d_refs = refs[:pieces], refs[pieces : pieces + blocks]
-    refs = refs[pieces + blocks :]
+def pack_kernel(first_ref, second_ref, first_d, second_d, first_out, second_out):
+    half = first_ref.shape[0] // 2
+    for rows, d_ref, out_ref in (
+        (second_ref[:half], first_d, first_out),
+        (first_ref[half:], second_d, second_out),
+    ):
+        out_ref[:half] = rows
+        count = rows.shape[1] // d_ref.shape[1]
+        high = d_ref.shape[0] // count
+        for c in range(count):
+            lanes = slice(c * d_ref.shape[1], (c + 1) * d_ref.shape[1])
+            out_ref[half:, lanes] = d_ref[c * high : (c + 1) * high]
+
+
+def unpack(ref, half, width):
+    return jnp.concatenate(
+        [ref[half:, at : at + width] for at in range(0, ref.shape[1], width)], axis=0
+    )
+
+
+def column_block(ref, rows, index, target):
+    if target % 128 == 0:
+        return ref[:rows, pl.ds(pl.multiple_of(index * target, target), target)]
+    fit = 128 // target
+    both = ref[:rows, pl.ds(pl.multiple_of(index // fit * 128, 128), 128)]
+    found = both[:, :target]
+    for part in range(1, fit):
+        here = both[:, part * target : (part + 1) * target]
+        found = jnp.where(index % fit == part, here, found)
+    return found
+
+
+def write_terms(base, count, target, ids_ref, operands, put):
+    group = 2 if count % 2 == 0 else 1
+    for start in range(0, count, group):
+        at = [ids_ref[base + start + i] for i in range(group)]
+        row = 0
+        for left, pieces, sizes in operands:
+            right = jnp.concatenate(
+                [
+                    jnp.concatenate(
+                        [column_block(r, n, a, target) for r, n in zip(pieces, sizes)], axis=0
+                    )
+                    for a in at
+                ],
+                axis=1,
+            )
+            value = mm(left, right).astype(BF16)
+            for i in range(group):
+                put(start + i, row, value[:, i * target : (i + 1) * target])
+            row += left.shape[0]
+
+
+def attention_kernel(
+    scale, heads, head_size, blocks, sizes, packed, count, target, ids_ref, mask_ref, *refs
+):
+    pieces = len(sizes)
+    row_refs, refs = refs[:pieces], refs[pieces:]
+    d_count = blocks - 2 if packed else blocks
+    d_refs, refs = refs[:d_count], refs[d_count:]
     wq_ref, wk_ref, wv_ref, eig_ref, lam_ref, lam_t_ref = refs[:6]
-    grads_ref, out_ref, gw_ref, eig_out = refs[6:10]
-    ret_refs = refs[10:-5]
+    grads_ref, out_ref, gw_ref, eig_out, give_ref = refs[6:11]
+    ret_refs = refs[11:-5]
     qe, qn, dt, dn, left_acc = refs[-5:]
     eig_count, nodes = eig_ref.shape
     width = heads * head_size
@@ -105,11 +156,14 @@
     eig = jnp.concatenate(parts, axis=1)
     turned = jnp.concatenate([eig, eig], axis=0).T
     wide = turned.astype(F32)
-    rows = jnp.concatenate([r[...] for r in row_refs], axis=0)
+    rows = jnp.concatenate([r[:n] for r, n in zip(row_refs, sizes)], axis=0)
     query = fit(mm(rows, wq_ref[...]).astype(BF16))
     keys = fit(mm(rows, wk_ref[...]).astype(BF16))
     values = fit(mm(rows, wv_ref[...]).astype(BF16))
-    d_att = fit(jnp.concatenate([r[...] for r in d_refs], axis=0))
+    d_parts = [r[...] for r in d_refs]
+    if packed:
+        d_parts[1:1] = [unpack(r, n, width) for r, n in zip(row_refs[3:], sizes[3:])]
+    d_att = fit(jnp.concatenate(d_parts, axis=0))
     query_t = (query.astype(F32) * scale).astype(BF16).T
     keys_t = keys.T
     values_t = values.T
@@ -250,40 +304,34 @@
         part = slice(b * size, (b + 1) * size)
         ret_refs[b][: 3 * width] = grads_ref[:, part]
         ret_refs[b][3 * width :] = eig_sum[:, part].astype(BF16)
-
-
-def terms_kernel(base, layout, target, ids_ref, *refs):
+    left = grads_ref[: 2 * width]
+    span = left.shape[0]
+
+    def put(block, row, value):
+        at = block * span + row
+        give_ref[at : at + value.shape[0]] = value
+
+    write_terms(blocks, count, target, ids_ref, [(left, row_refs, sizes)], put)
+    put_sums(give_ref, count * span, gw_ref[...])
+
+
+def terms_kernel(base, layout, target, flat, ids_ref, *refs):
     out_ref, operands, at = refs[-1], [], 0
-    for lanes, pieces in layout:
-        operands.append((refs[at], lanes, refs[at + 1 : at + 1 + pieces]))
-        at += 1 + pieces
-    count = out_ref.shape[0]
-
-    def columns(ref, index):
-        if target % 128 == 0:
-            return ref[:, pl.ds(pl.multiple_of(index * target, target), target)]
-        fit = 128 // target
-        both = ref[:, pl.ds(pl.multiple_of(index // fit * 128, 128), 128)]
-        found = both[:, :target]
-        for part in range(1, fit):
-            here = both[:, part * target : (part + 1) * target]
-            found = jnp.where(index % fit == part, here, found)
-        return found
-
-    def right_of(pieces, at):
-        return jnp.concatenate(
-            [jnp.concatenate([columns(ref, a) for ref in pieces], axis=0) for a in at], axis=1
-        )
-
-    group = 2 if count % 2 == 0 else 1
-    for start in range(0, count, group):
-        at = [ids_ref[base + start + i] for i in range(group)]
-        row = 0
-        for left_ref, (low, high), pieces in operands:
-            value = mm(left_ref[low:high], right_of(pieces, at)).astype(BF16)
-            for i in range(group):
-                out_ref[start + i, row : row + high - low] = value[:, i * target : (i + 1) * target]
-            row += high - low
+    for (low, high), sizes in layout:
+        pieces = refs[at + 1 : at + 1 + len(sizes)]
+        operands.append((refs[at][low:high], pieces, sizes))
+        at += 1 + len(sizes)
+    span = sum(high - low for (low, high), _ in layout)
+
+    def put(block, row, value):
+        if flat:
+            at = block * span + row
+            out_ref[at : at + value.shape[0]] = value
+        else:
+            out_ref[block, row : row + value.shape[0]] = value
+
+    count = out_ref.shape[0] // span if flat else out_ref.shape[0]
+    write_terms(base, count, target, ids_ref, operands, put)
 
 
 def put_sums(ref, base, sums):
@@ -302,18 +350,18 @@
 
 def pair_kernel(sums, keep_ref, got_ref, *refs):
     if sums:
-        gw_ref, gw_got_ref, give_ref, near_ref, gw_out = refs
+        gw_ref, give_ref, near_ref, gw_out = refs
     else:
         give_ref, near_ref = refs
     count, rows, _ = keep_ref.shape
     for s in range(count):
-        total = keep_ref[s].astype(F32) + got_ref[s].astype(F32)
+        total = keep_ref[s].astype(F32) + got_ref[s * rows : (s + 1) * rows].astype(F32)
         if s % 2 == 0:
             near_ref[s // 2] = total
         else:
             give_ref[s // 2 * rows : (s // 2 + 1) * rows] = total.astype(BF16)
     if sums:
-        total = gw_ref[...] + gw_got_ref[...]
+        total = gw_ref[...] + get_sums(got_ref, count * rows, gw_ref.shape)
         gw_out[...] = total
         put_sums(give_ref, count // 2 * rows, total)
 
@@ -419,7 +467,7 @@
             compiler_params=LIMIT,
         )(*operands)
 
-    crossed = node_size == 4 and size % 32 == 0
+    crossed = node_size == 4 and size % 64 == 0
     rows = [own_rows] + [None] * (node_size - 1)
     for s in far_first:
         if s < 3 or not crossed:
@@ -448,12 +496,24 @@
     d_parts, weights = made[:node_size], made[node_size:]
     d_att = [d_parts[0]] + [None] * (node_size - 1)
     for s in far_first:
+        if s < 3 and crossed:
+            continue
         d_att[s] = give(d_parts[s], "node", s, node_size)
+    sizes = [size] * node_size
     if crossed:
-        top, bottom = call(
-            split_kernel, [vmem] * 2, [((size // 2, model), BF16)] * 2, (rows[1], rows[2]), 0, 2**19
+        high = size // 2 + size * width // model
+        packed = call(
+            pack_kernel,
+            [vmem] * 4,
+            [((high, model), BF16)] * 2,
+            (rows[1], rows[2], d_parts[1], d_parts[2]),
+            0,
+            2**19,
         )
-        rows[3:] = [take(top, "node", 1, node_size), take(bottom, "node", 2, node_size)]
+        rows[3:] = [give(packed[i], "node", i + 1, node_size) for i in range(2)]
+        sizes[3:] = [size // 2] * 2
+        d_att = [d_att[0], d_att[3]]
+    sizes = tuple(sizes)
     cots = [own_cot] + [None] * (node_size - 1)
     for s in far_first:
         cots[s] = take(own_cot, "node", s, node_size)
@@ -463,14 +523,25 @@
     groups = -(-heads // 2)
     target = model // clus_size
     pairs = rest // 2
-    grads_t, out_t, gw_own, eig_own, *parts = call(
-        functools.partial(attention_kernel, scale, heads, head_size, node_size, len(rows)),
-        [smem, smem] + [vmem] * (len(rows) + node_size + 6),
+    grads_t, out_t, gw_own, eig_own, give_first, *parts = call(
+        functools.partial(
+            attention_kernel,
+            scale,
+            heads,
+            head_size,
+            node_size,
+            sizes,
+            crossed,
+            rest,
+            target,
+        ),
+        [smem, smem] + [vmem] * (len(rows) + len(d_att) + 6),
         [
             ((3 * width, nodes), BF16),
             ((width, nodes), BF16),
             ((heads, eig_count), F32),
             ((eig_count, size), F32),
+            ((rest * 2 * width + 16, target), BF16),
         ]
         + [((3 * width + eig_count, size), BF16)] * node_size,
         (ids, block_mask[0], *rows, *d_att, *weights, eigvec[0], eig_weight, eig_weight.T),
@@ -485,15 +556,16 @@
         ],
     )
 
-    def terms(base, parts):
+    def terms(base, products, flat):
         operands = [ids]
-        for left, _, pieces in parts:
+        for left, _, pieces, _ in products:
             operands += [left, *pieces]
-        layout = tuple((lanes, len(pieces)) for _, lanes, pieces in parts)
+        layout = tuple((lanes, sizes) for _, lanes, _, sizes in products)
+        span = sum(high - low for (low, high), _ in layout)
         return call(
-            functools.partial(terms_kernel, node_size + base, layout, target),
+            functools.partial(terms_kernel, node_size + base, layout, target, flat),
             [smem] + [vmem] * (len(operands) - 1),
-            [((rest, sum(high - low for low, high in (p[1] for p in parts)), target), BF16)],
+            [((rest * span, target) if flat else (rest, span, target), BF16)],
             operands,
             10**9,
             2**20,
@@ -502,13 +574,13 @@
     near_keeps, near_gots = [], []
     lanes = (0, 2 * width), (2 * width, 3 * width), (0, width)
     plan = (
-        [(grads_t, lanes[0], rows)],
-        [(grads_t, lanes[1], rows), (out_t, lanes[2], cots)],
+        [(grads_t, lanes[0], rows, sizes)],
+        [(grads_t, lanes[1], rows, sizes), (out_t, lanes[2], cots, (size,) * node_size)],
     )
     for c, products in enumerate(plan):
-        give_half = terms(0, products)
+        give_half = give_first if c == 0 else terms(0, products, True)
         got_half = give(give_half, "clus", 1, clus_size)
-        keep_half = terms(rest, products)
+        keep_half = terms(rest, products, False)
         group_rows = keep_half.shape[1]
         operands = [keep_half, got_half]
         shapes = [
@@ -516,7 +588,7 @@
             ((pairs, group_rows, target), F32),
         ]
         if c == 0:
-            operands += [gw_own, give(gw_own, "clus", 1, clus_size)]
+            operands.append(gw_own)
             shapes.append((eig_weight.shape, F32))
         near_give, near_keep, *others = call(
             functools.partial(pair_kernel, c == 0),

time: 65.3 us -> 60.7 us (0.930)
  starting transfers between devices: 23.2 us -> 19.4 us
  waiting for transfers between devices: 22.7 us -> 20.5 us
  local copies, waits for them, and re-layouts: 0.13 us -> 2.02 us
    ppermute x20 -> x17, starting transfers between devices: 23.2 us -> 19.4 us  [take(): return lax.ppermute(value, axis, pairs)]
    ppermute x20 -> x17, waiting for transfers between devices: 22.7 us -> 20.5 us  [take(): return lax.ppermute(value, axis, pairs)]
    unnamed x17 -> x25, local copies, waits for them, and re-layouts: 0.13 us -> 2.02 us
    pallas_call x13 -> x12, Pallas kernels: 18.2 us -> 17.6 us  [call_here(): pl.pallas_call(kernel, in_specs=in_specs, out_specs=[vmem] * len(out_shap...]
  transfers between devices with their start and end apart: 20 -> 17, of which waited for: 10 -> 7; matrix products, arithmetic and copies ran while one was open for 0% -> 0% of each run, Pallas kernels for 26% -> 27%
where the time goes in v5:
time: 60.7 us; the launch traced here: 60.5 us
  waiting for transfers between devices  20.5 us (34%)
  starting transfers between devices  19.4 us (32%)
  Pallas kernels  17.6 us (29%)
  local copies, waits for them, and re-layouts  2.02 us (3%)
  between operations  0.85 us (1%)
    ppermute x17, waiting for transfers between devices, take(): return lax.ppermute(value, axis, pairs)  20.5 us
    ppermute x17, starting transfers between devices, take(): return lax.ppermute(value, axis, pairs)  19.4 us
    pallas_call x12, Pallas kernels, call_here(): pl.pallas_call(kernel, in_specs=in_specs, out_specs=[vmem] * len(out_shap...  17.6 us
    unnamed x25, local copies, waits for them, and re-layouts  2.02 us
  transfers between devices with their start and end apart: 17, of which 7 were waited for; matrix products, arithmetic and copies ran while one was open for 0% of the time, Pallas kernels for 27%

profile of v5, /device:TPU:0, one launch (start us, length us, event | category | flops | bytes accessed | tf_op | source)
XLA Modules:
  0.0 60.5 jit_solution(16282462534705465299)
XLA Ops:
  0.6 3.0 %collective-permute-start = (bf16[128,1024]{1,0:T(8,128)(2,1)}, bf16[128,1024]{1,0:T(8,128)(2,1)S(1)}, u32[]{:S(2)}, u32[]{:S(2)}) collective-permute-start(bf16[128,1024]{1,0:T(8,128)(2,1)} %bitcast.13), channel_id=1, source_target_pairs={{0,1},{1,0},{2,3},{3,2},{4,5},{5,4},{6,7},{7,6},{8,9},{9,8},{10,11... | collective-permute-start | bytes 786440 | tf_op jit(solution)/shard_map/ppermute | solution.py:27
  3.7 1.5 %collective-permute-start.1 = (bf16[128,1024]{1,0:T(8,128)(2,1)}, bf16[128,1024]{1,0:T(8,128)(2,1)S(1)}, u32[]{:S(2)}, u32[]{:S(2)}) collective-permute-start(bf16[128,1024]{1,0:T(8,128)(2,1)} %bitcast.14), channel_id=1, source_target_pairs={{0,2},{1,3},{2,0},{3,1},{4,6},{5,7},{6,4},{7,5},{8,10},{9,11},{10,... | collective-permute-start | bytes 786440 | tf_op jit(solution)/shard_map/ppermute | solution.py:27
  5.2 0.1 pad_add_fusion.ids_ref
  5.3 0.0 copy-start.3
  5.3 0.0 copy-start.11
  5.3 3.5 %shard_map.120 = (bf16[128,256]{1,0:T(8,128)(2,1)S(1)}, bf16[128,256]{1,0:T(8,128)(2,1)S(1)}, bf16[128,256]{1,0:T(8,128)(2,1)S(1)}, bf16[128,256]{1,0:T(8,128)(2...) custom-call(s32[12]{0:T(128)S(1)} %pad_add_fusion.ids_ref, ...), custom_call_target="tpu_custom_call" | custom-call | flops 300000000 | bytes 3145728 | tf_op jit(solution)/shard_map/pallas_call | solution.py:460
  8.8 0.0 copy-start.6
  8.8 0.0 copy-start.9
  8.8 1.3 %collective-permute-done.first_ref.refs_1_.refs_2_ = bf16[128,1024]{1,0:T(8,128)(2,1)S(1)} collective-permute-done((bf16[128,1024]{1,0:T(8,128)(2,1)}, bf16[128,1024]{1,0:T(8,128)(2,1)S(1)}, u32[]{:S(2)}, u32[]{:S(2)}) %collective-permute-start) | collective-permute-done | bytes 262176 | tf_op jit(solution)/shard_map/ppermute | solution.py:27
  10.2 1.5 %collective-permute-done.1.second_ref.refs_2_.refs_3_ = bf16[128,1024]{1,0:T(8,128)(2,1)S(1)} collective-permute-done((bf16[128,1024]{1,0:T(8,128)(2,1)}, bf16[128,1024]{1,0:T(8,128)(2,1)S(1)}, u32[]{:S(2)}, u32[]{:S(2)}) %collective-permute-start.1) | collective-permute-done | bytes 262176 | tf_op jit(solution)/shard_map/ppermute | solution.py:27
  11.7 0.4 collective-permute-start.2
  12.1 1.7 %collective-permute-start.3 = (bf16[96,1024]{1,0:T(8,128)(2,1)S(1)}, bf16[96,1024]{1,0:T(8,128)(2,1)S(1)}, u32[]{:S(2)}, u32[]{:S(2)}) collective-permute-start(bf16[96,1024]{1,0:T(8,128)(2,1)S(1)} %get-tuple-element.39), channel_id=1, source_target_pairs={{0,2},{1,3},{2,0},{3,1},{4,6},{5,7},{6,4},{7,5},{8,10},{9,11},{10,... | collective-permute-start | bytes 589832 | tf_op jit(solution)/shard_map/ppermute | solution.py:27
  13.8 0.0 copy-done.6
  13.8 1.4 %collective-permute-start.4 = (bf16[128,256]{1,0:T(8,128)(2,1)}, bf16[128,256]{1,0:T(8,128)(2,1)}, u32[]{:S(2)}, u32[]{:S(2)}) collective-permute-start(bf16[128,256]{1,0:T(8,128)(2,1)} %get-tuple-element.41), channel_id=1, source_target_pairs={{0,3},{1,2},{2,1},{3,0},{4,7},{5,6},{6,5},{7,4},{8,11},{9,10},{10,... | collective-permute-start | bytes 196616 | tf_op jit(solution)/shard_map/ppermute | solution.py:27
  15.2 0.0 copy-done.3
  15.2 0.4 collective-permute-start.11
  15.6 0.0 copy-done.9
  15.6 1.7 %collective-permute-start.12 = (bf16[128,1024]{1,0:T(8,128)(2,1)S(1)}, bf16[128,1024]{1,0:T(8,128)(2,1)S(1)}, u32[]{:S(2)}, u32[]{:S(2)}) collective-permute-start(bf16[128,1024]{1,0:T(8,128)(2,1)S(1)} %bitcast.9), channel_id=1, source_target_pairs={{0,2},{1,3},{2,0},{3,1},{4,6},{5,7},{6,4},{7,5},{8,10},{9,11},{10,... | collective-permute-start | bytes 786440 | tf_op jit(solution)/shard_map/ppermute | solution.py:27
  17.3 0.0 copy-done.5
  17.3 0.1 copy.13
  17.4 4.6 %collective-permute-done.4.refs_6_ = bf16[128,256]{1,0:T(8,128)(2,1)} collective-permute-done((bf16[128,256]{1,0:T(8,128)(2,1)}, bf16[128,256]{1,0:T(8,128)(2,1)}, u32[]{:S(2)}, u32[]{:S(2)}) %collective-permute-start.4) | collective-permute-done | bytes 65568 | tf_op jit(solution)/shard_map/ppermute | solution.py:27
  22.0 0.1 collective-permute-start.13
  22.0 0.0 collective-permute-done.2.refs_3_.refs_4_
  22.0 0.0 collective-permute-done.3.refs_4_.refs_5_
  22.0 0.0 copy-done.4
  22.1 0.0 copy-done.8
  22.1 0.0 copy-done.11
  22.1 0.0 copy-start.7
  22.1 1.0 %copy-done.7 = bf16[1024,256]{1,0:T(8,128)(2,1)S(1)} copy-done((bf16[1024,256]{1,0:T(8,128)(2,1)S(1)}, bf16[1024,256]{1,0:T(8,128)(2,1)}, u32[]{:S(2)}) %copy-start.7) | copy-done | bytes 524312
  23.1 0.8 %copy-done.10 = bf16[128,256]{1,0:T(8,128)(2,1)S(1)} copy-done((bf16[128,256]{1,0:T(8,128)(2,1)S(1)}, bf16[128,256]{1,0:T(8,128)(2,1)}, u32[]{:S(2)}) %copy-start.10) | copy-done | bytes 65560
  24.0 6.2 %shard_map.122 = (bf16[768,512]{1,0:T(8,128)(2,1)S(1)}, bf16[256,512]{1,0:T(8,128)(2,1)S(1)}, f32[4,64]{1,0:T(4,128)S(1)}, f32[64,128]{1,0:T(8,128)S(1)}, bf16[2...) custom-call(s32[12]{0:T(128)S(1)} %pad_add_fusion.ids_ref, ...), custom_call_target="tpu_custom_call" | custom-call | flops 8000000000 | bytes 8388608 | tf_op jit(solution)/shard_map/pallas_call | solution.py:460
  30.2 0.1 collective-permute-start.8
  30.2 0.0 collective-permute-done.11.refs_8_
  30.2 0.0 collective-permute-done.12.refs_9_
  30.3 0.6 collective-permute-done.13.refs_10_
  30.8 1.1 %shard_map.128 = bf16[2048,128]{1,0:T(8,128)(2,1)S(1)} custom-call(s32[12]{0:T(128)S(1)} %pad_add_fusion.ids_ref, bf16[768,512]{1,0:T(8,128)(2,1)S(1)} %get-tuple-element.52.refs_0_, bf16[128,1024]{1,0:T(8,128)(2,1)S(1)} %bitcast.16, bf16[128,1024]{1,0:T(8,128)(2,1)S(1)} %collective-permute-done.first_ref.refs_1_.refs_2_, ...), custom_call_target="tpu_custom_call" | custom-call | flops 1000000000 | bytes 1048576 | tf_op jit(solution)/shard_map/pallas_call | solution.py:460
  31.9 0.1 collective-permute-start.14
  32.0 1.0 %shard_map.124.keep_ref = bf16[4,512,128]{2,1,0:T(8,128)(2,1)S(1)} custom-call(s32[12]{0:T(128)S(1)} %pad_add_fusion.ids_ref, bf16[768,512]{1,0:T(8,128)(2,1)S(1)} %get-tuple-element.52.refs_0_, bf16[128,1024]{1,0:T(8,128)(2,1)S(1)} %bitcast.17, bf16[128,1024]{1,0:T(8,128)(2,1)S(1)} %collective-permute-done.first_ref.refs_1_.refs_2_, ...), custom_call_target="tpu_custom_call" | custom-call | flops 1000000000 | bytes 1048576 | tf_op jit(solution)/shard_map/pallas_call | solution.py:460
  33.1 0.0 collective-permute-done.8.got_ref
  33.1 0.1 shard_map.125
  33.2 1.6 %collective-permute-start.9 = (bf16[1040,128]{1,0:T(8,128)(2,1)S(1)}, bf16[1040,128]{1,0:T(8,128)(2,1)S(1)}, u32[]{:S(2)}, u32[]{:S(2)}) collective-permute-start(bf16[1040,128]{1,0:T(8,128)(2,1)S(1)} %get-tuple-element.56), channel_id=1, source_target_pairs={{0,8},{4,12},{8,0},{12,4},{16,24},{20,28},{24,16},{28,20},{1,9},{5... | collective-permute-start | bytes 798728 | tf_op jit(solution)/shard_map/ppermute | solution.py:27
  34.9 1.1 %shard_map.127.keep_ref = bf16[4,512,128]{2,1,0:T(8,128)(2,1)S(1)} custom-call(s32[12]{0:T(128)S(1)} %pad_add_fusion.ids_ref, bf16[768,512]{1,0:T(8,128)(2,1)S(1)} %get-tuple-element.52.refs_0_, bf16[128,1024]{1,0:T(8,128)(2,1)S(1)} %bitcast.18, bf16[128,1024]{1,0:T(8,128)(2,1)S(1)} %collective-permute-done.first_ref.refs_1_.refs_2_, ...), custom_call_target="tpu_custom_call" | custom-call | flops 1000000000 | bytes 1048576 | tf_op jit(solution)/shard_map/pallas_call | solution.py:460
  36.0 0.0 copy-start
  36.0 0.0 collective-permute-done.14.got_ref
  36.0 0.1 shard_map.129
  36.1 0.5 collective-permute-start.15
  36.6 1.8 %collective-permute-start.5 = (bf16[832,128]{1,0:T(8,128)(2,1)S(1)}, bf16[832,128]{1,0:T(8,128)(2,1)S(1)}, u32[]{:S(2)}, u32[]{:S(2)}) collective-permute-start(bf16[832,128]{1,0:T(8,128)(2,1)S(1)} %get-tuple-element.47), channel_id=1, source_target_pairs={{0,1},{1,0},{2,3},{3,2},{4,5},{5,4},{6,7},{7,6},{8,9},{9,8},{10,11... | collective-permute-start | bytes 638984 | tf_op jit(solution)/shard_map/ppermute | solution.py:27
  38.4 1.5 %collective-permute-start.6 = (bf16[832,128]{1,0:T(8,128)(2,1)S(1)}, bf16[832,128]{1,0:T(8,128)(2,1)S(1)}, u32[]{:S(2)}, u32[]{:S(2)}) collective-permute-start(bf16[832,128]{1,0:T(8,128)(2,1)S(1)} %get-tuple-element.48), channel_id=1, source_target_pairs={{0,2},{1,3},{2,0},{3,1},{4,6},{5,7},{6,4},{7,5},{8,10},{9,11},{10,... | collective-permute-start | bytes 638984 | tf_op jit(solution)/shard_map/ppermute | solution.py:27
  39.9 0.2 collective-permute-start.7
  40.1 2.5 %collective-permute-done.9.got_ref = bf16[1040,128]{1,0:T(8,128)(2,1)S(1)} collective-permute-done((bf16[1040,128]{1,0:T(8,128)(2,1)S(1)}, bf16[1040,128]{1,0:T(8,128)(2,1)S(1)}, u32[]{:S(2)}, u32[]{:S(2)}) %collective-permute-start.9) | collective-permute-done | bytes 266272 | tf_op jit(solution)/shard_map/ppermute | solution.py:27
  42.6 0.1 shard_map.126
  42.6 2.7 %collective-permute-start.10 = (bf16[528,128]{1,0:T(8,128)(2,1)S(1)}, bf16[528,128]{1,0:T(8,128)(2,1)S(1)}, u32[]{:S(2)}, u32[]{:S(2)}) collective-permute-start(bf16[528,128]{1,0:T(8,128)(2,1)S(1)} %get-tuple-element.59), channel_id=1, source_target_pairs={{0,16},{4,20},{8,24},{12,28},{16,0},{20,4},{24,8},{28,12},{1,17},{... | collective-permute-start | bytes 405512 | tf_op jit(solution)/shard_map/ppermute | solution.py:27
  45.3 5.3 %collective-permute-done.15.got_ref = bf16[1024,128]{1,0:T(8,128)(2,1)S(1)} collective-permute-done((bf16[1024,128]{1,0:T(8,128)(2,1)S(1)}, bf16[1024,128]{1,0:T(8,128)(2,1)S(1)}, u32[]{:S(2)}, u32[]{:S(2)}) %collective-permute-start.15) | collective-permute-done | bytes 262176 | tf_op jit(solution)/shard_map/ppermute | solution.py:27
  50.7 0.8 %collective-permute-start.16 = (bf16[512,128]{1,0:T(8,128)(2,1)S(1)}, bf16[512,128]{1,0:T(8,128)(2,1)S(1)}, u32[]{:S(2)}, u32[]{:S(2)}) collective-permute-start(bf16[512,128]{1,0:T(8,128)(2,1)S(1)} %get-tuple-element.64), channel_id=1, source_target_pairs={{0,16},{4,20},{8,24},{12,28},{16,0},{20,4},{24,8},{28,12},{1,17},{... | collective-permute-start | bytes 393224 | tf_op jit(solution)/shard_map/ppermute | solution.py:27
  51.5 0.0 collective-permute-done.5.refs_1_
  51.5 0.0 collective-permute-done.6.refs_2_
  51.5 0.0 collective-permute-done.7.refs_3_
  51.5 0.0 copy-done.1
  51.5 0.0 copy-done.2
  51.5 0.0 copy-done
  51.5 3.2 %shard_map.123 = (bf16[128,1024]{1,0:T(8,128)(2,1)}, f32[64,128]{1,0:T(8,128)}) custom-call(s32[12]{0:T(128)S(1)} %pad_add_fusion.ids_ref, f32[64,128]{1,0:T(8,128)S(1)} %get-tuple-element.45.eig_ref, bf16[832,128]{1,0:T(8,128)(2,1)S(1)} %get-tuple-element.46.refs_0_, bf16[832,128]{1,0:T(8,128)(2,1)S(1)} %collective-permute-done.5.refs_1_, ...), custom_call_target="tpu_custom_call" | custom-call | flops 1000000000 | bytes 7340032 | tf_op jit(solution)/shard_map/pallas_call | solution.py:460
  54.7 4.8 %collective-permute-done.16.refs_3_ = bf16[512,128]{1,0:T(8,128)(2,1)S(1)} collective-permute-done((bf16[512,128]{1,0:T(8,128)(2,1)S(1)}, bf16[512,128]{1,0:T(8,128)(2,1)S(1)}, u32[]{:S(2)}, u32[]{:S(2)}) %collective-permute-start.16) | collective-permute-done | bytes 131104 | tf_op jit(solution)/shard_map/ppermute | solution.py:27
  59.5 0.0 collective-permute-done.10.refs_1_
  59.5 1.0 %shard_map.131 = (f32[4,128,256]{2,1,0:T(8,128)}, f32[4,64]{1,0:T(4,128)}) custom-call(f32[512,128]{1,0:T(8,128)S(1)} %get-tuple-element.58.refs_0_, bf16[528,128]{1,0:T(8,128)(2,1)S(1)} %collective-permute-done.10.refs_1_, f32[512,128]{1,0:T(8,128)S(1)} %get-tuple-element.63.refs_2_, bf16[512,128]{1,0:T(8,128)(2,1)S(1)} %collective-permute-done.16.refs_3_, ...), custom_call_target="tpu_custom_call" | custom-call | flops 1000000 | bytes 2097152 | tf_op jit(solution)/shard_map/pallas_call | solution.py:460
  (10 shorter events, 0.1 us)
Async XLA Ops:
  0.6 9.6 %collective-permute-start = (bf16[128,1024]{1,0:T(8,128)(2,1)}, bf16[128,1024]{1,0:T(8,128)(2,1)S(1)}, u32[]{:S(2)}, u32[]{:S(2)}) collective-permute-start(bf16[128,1024]{1,0:T(8,128)(2,1)} %bitcast.13), channel_id=1, source_target_pairs={{0,1},{1,0},{2,3},{3,2},{4,5},{5,4},{6,7},{7,6},{8,9},{9,8},{10,11... | collective-permute-start | bytes 786440 | tf_op jit(solution)/shard_map/ppermute | solution.py:27
  3.7 8.0 %collective-permute-start.1 = (bf16[128,1024]{1,0:T(8,128)(2,1)}, bf16[128,1024]{1,0:T(8,128)(2,1)S(1)}, u32[]{:S(2)}, u32[]{:S(2)}) collective-permute-start(bf16[128,1024]{1,0:T(8,128)(2,1)} %bitcast.14), channel_id=1, source_target_pairs={{0,2},{1,3},{2,0},{3,1},{4,6},{5,7},{6,4},{7,5},{8,10},{9,11},{10,... | collective-permute-start | bytes 786440 | tf_op jit(solution)/shard_map/ppermute | solution.py:27
  5.3 10.0 %copy-start.3 = (bf16[1,128,1024]{2,1,0:T(8,128)(2,1)S(1)}, bf16[1,128,1024]{2,1,0:T(8,128)(2,1)}, u32[]{:S(2)}) copy-start(bf16[1,128,1024]{2,1,0:T(8,128)(2,1)} %param.10) | copy-start | bytes 786436
  5.3 12.0 %copy-start.5 = (f32[4,64]{1,0:T(4,128)S(1)}, f32[4,64]{1,0:T(4,128)}, u32[]{:S(2)}) copy-start(f32[4,64]{1,0:T(4,128)} %refs_11_.1) | copy-start | bytes 3076
  5.3 16.8 %copy-start.4 = (bf16[1,128,1024]{2,1,0:T(8,128)(2,1)S(1)}, bf16[1,128,1024]{2,1,0:T(8,128)(2,1)}, u32[]{:S(2)}) copy-start(bf16[1,128,1024]{2,1,0:T(8,128)(2,1)} %param.9) | copy-start | bytes 786436
  5.3 16.8 %copy-start.8 = (bf16[1,64,512]{2,1,0:T(8,128)(2,1)S(1)}, bf16[1,64,512]{2,1,0:T(8,128)(2,1)}, u32[]{:S(2)}) copy-start(bf16[1,64,512]{2,1,0:T(8,128)(2,1)} %param.15) | copy-start | bytes 196612
  5.3 16.8 %copy-start.11 = (s32[1,4,4,4]{3,2,1,0:T(4,128)S(1)}, s32[1,4,4,4]{3,2,1,0:T(4,128)}, u32[]{:S(2)}) copy-start(s32[1,4,4,4]{3,2,1,0:T(4,128)} %param.17) | copy-start | bytes 772
  8.8 5.0 %copy-start.6 = (bf16[1024,256]{1,0:T(8,128)(2,1)}, bf16[1024,256]{1,0:T(8,128)(2,1)S(1)}, u32[]{:S(2)}) copy-start(bf16[1024,256]{1,0:T(8,128)(2,1)S(1)} %get-tuple-element.44.refs_9_) | copy-start | bytes 1572868
  8.8 6.8 %copy-start.9 = (bf16[128,256]{1,0:T(8,128)(2,1)}, bf16[128,256]{1,0:T(8,128)(2,1)S(1)}, u32[]{:S(2)}) copy-start(bf16[128,256]{1,0:T(8,128)(2,1)S(1)} %get-tuple-element.40.refs_5_) | copy-start | bytes 196612
  11.7 10.4 %collective-permute-start.2 = (bf16[96,1024]{1,0:T(8,128)(2,1)S(1)}, bf16[96,1024]{1,0:T(8,128)(2,1)S(1)}, u32[]{:S(2)}, u32[]{:S(2)}) collective-permute-start(bf16[96,1024]{1,0:T(8,128)(2,1)S(1)} %get-tuple-element.38), channel_id=1, source_target_pairs={{0,1},{1,0},{2,3},{3,2},{4,5},{5,4},{6,7},{7,6},{8,9},{9,8},{10,11... | collective-permute-start | bytes 589832 | tf_op jit(solution)/shard_map/ppermute | solution.py:27
  12.1 9.9 %collective-permute-start.3 = (bf16[96,1024]{1,0:T(8,128)(2,1)S(1)}, bf16[96,1024]{1,0:T(8,128)(2,1)S(1)}, u32[]{:S(2)}, u32[]{:S(2)}) collective-permute-start(bf16[96,1024]{1,0:T(8,128)(2,1)S(1)} %get-tuple-element.39), channel_id=1, source_target_pairs={{0,2},{1,3},{2,0},{3,1},{4,6},{5,7},{6,4},{7,5},{8,10},{9,11},{10,... | collective-permute-start | bytes 589832 | tf_op jit(solution)/shard_map/ppermute | solution.py:27
  13.8 8.2 %collective-permute-start.4 = (bf16[128,256]{1,0:T(8,128)(2,1)}, bf16[128,256]{1,0:T(8,128)(2,1)}, u32[]{:S(2)}, u32[]{:S(2)}) collective-permute-start(bf16[128,256]{1,0:T(8,128)(2,1)} %get-tuple-element.41), channel_id=1, source_target_pairs={{0,3},{1,2},{2,1},{3,0},{4,7},{5,6},{6,5},{7,4},{8,11},{9,10},{10,... | collective-permute-start | bytes 196616 | tf_op jit(solution)/shard_map/ppermute | solution.py:27
  15.2 15.0 %collective-permute-start.11 = (bf16[128,1024]{1,0:T(8,128)(2,1)S(1)}, bf16[128,1024]{1,0:T(8,128)(2,1)S(1)}, u32[]{:S(2)}, u32[]{:S(2)}) collective-permute-start(bf16[128,1024]{1,0:T(8,128)(2,1)S(1)} %bitcast.8), channel_id=1, source_target_pairs={{0,1},{1,0},{2,3},{3,2},{4,5},{5,4},{6,7},{7,6},{8,9},{9,8},{10,11... | collective-permute-start | bytes 786440 | tf_op jit(solution)/shard_map/ppermute | solution.py:27
  15.6 14.6 %collective-permute-start.12 = (bf16[128,1024]{1,0:T(8,128)(2,1)S(1)}, bf16[128,1024]{1,0:T(8,128)(2,1)S(1)}, u32[]{:S(2)}, u32[]{:S(2)}) collective-permute-start(bf16[128,1024]{1,0:T(8,128)(2,1)S(1)} %bitcast.9), channel_id=1, source_target_pairs={{0,2},{1,3},{2,0},{3,1},{4,6},{5,7},{6,4},{7,5},{8,10},{9,11},{10,... | collective-permute-start | bytes 786440 | tf_op jit(solution)/shard_map/ppermute | solution.py:27
  22.0 8.9 %collective-permute-start.13 = (bf16[128,1024]{1,0:T(8,128)(2,1)S(1)}, bf16[128,1024]{1,0:T(8,128)(2,1)S(1)}, u32[]{:S(2)}, u32[]{:S(2)}) collective-permute-start(bf16[128,1024]{1,0:T(8,128)(2,1)S(1)} %bitcast.10), channel_id=1, source_target_pairs={{0,3},{1,2},{2,1},{3,0},{4,7},{5,6},{6,5},{7,4},{8,11},{9,10},{10,... | collective-permute-start | bytes 786440 | tf_op jit(solution)/shard_map/ppermute | solution.py:27
  22.1 1.0 %copy-start.7 = (bf16[1024,256]{1,0:T(8,128)(2,1)S(1)}, bf16[1024,256]{1,0:T(8,128)(2,1)}, u32[]{:S(2)}) copy-start(bf16[1024,256]{1,0:T(8,128)(2,1)} %copy-done.6) | copy-start | bytes 1572868
  23.1 0.8 %copy-start.10 = (bf16[128,256]{1,0:T(8,128)(2,1)S(1)}, bf16[128,256]{1,0:T(8,128)(2,1)}, u32[]{:S(2)}) copy-start(bf16[128,256]{1,0:T(8,128)(2,1)} %copy-done.9) | copy-start | bytes 196612
  30.2 2.9 %collective-permute-start.8 = (bf16[2064,128]{1,0:T(8,128)(2,1)S(1)}, bf16[2064,128]{1,0:T(8,128)(2,1)S(1)}, u32[]{:S(2)}, u32[]{:S(2)}) collective-permute-start(bf16[2064,128]{1,0:T(8,128)(2,1)S(1)} %get-tuple-element.53), channel_id=1, source_target_pairs={{0,4},{4,0},{8,12},{12,8},{16,20},{20,16},{24,28},{28,24},{1,5},{5... | collective-permute-start | bytes 1585160 | tf_op jit(solution)/shard_map/ppermute | solution.py:27
  31.9 4.0 %collective-permute-start.14 = (bf16[2048,128]{1,0:T(8,128)(2,1)S(1)}, bf16[2048,128]{1,0:T(8,128)(2,1)S(1)}, u32[]{:S(2)}, u32[]{:S(2)}) collective-permute-start(bf16[2048,128]{1,0:T(8,128)(2,1)S(1)} %shard_map.128), channel_id=1, source_target_pairs={{0,4},{4,0},{8,12},{12,8},{16,20},{20,16},{24,28},{28,24},{1,5},{5... | collective-permute-start | bytes 1572872 | tf_op jit(solution)/shard_map/ppermute | solution.py:27
  33.2 9.3 %collective-permute-start.9 = (bf16[1040,128]{1,0:T(8,128)(2,1)S(1)}, bf16[1040,128]{1,0:T(8,128)(2,1)S(1)}, u32[]{:S(2)}, u32[]{:S(2)}) collective-permute-start(bf16[1040,128]{1,0:T(8,128)(2,1)S(1)} %get-tuple-element.56), channel_id=1, source_target_pairs={{0,8},{4,12},{8,0},{12,4},{16,24},{20,28},{24,16},{28,20},{1,9},{5... | collective-permute-start | bytes 798728 | tf_op jit(solution)/shard_map/ppermute | solution.py:27
  34.9 16.6 %copy-start.1 = (bf16[1024,1024]{1,0:T(8,128)(2,1)S(1)}, bf16[1024,1024]{1,0:T(8,128)(2,1)}, u32[]{:S(2)}) copy-start(bf16[1024,1024]{1,0:T(8,128)(2,1)} %refs_5_.1) | copy-start | bytes 6291460
  34.9 16.6 %copy-start.2 = (bf16[1024,1024]{1,0:T(8,128)(2,1)S(1)}, bf16[1024,1024]{1,0:T(8,128)(2,1)}, u32[]{:S(2)}) copy-start(bf16[1024,1024]{1,0:T(8,128)(2,1)} %refs_6_.1) | copy-start | bytes 6291460
  36.0 15.5 %copy-start = (bf16[1024,1024]{1,0:T(8,128)(2,1)S(1)}, bf16[1024,1024]{1,0:T(8,128)(2,1)}, u32[]{:S(2)}) copy-start(bf16[1024,1024]{1,0:T(8,128)(2,1)} %refs_4_.1) | copy-start | bytes 6291460
  36.1 14.5 %collective-permute-start.15 = (bf16[1024,128]{1,0:T(8,128)(2,1)S(1)}, bf16[1024,128]{1,0:T(8,128)(2,1)S(1)}, u32[]{:S(2)}, u32[]{:S(2)}) collective-permute-start(bf16[1024,128]{1,0:T(8,128)(2,1)S(1)} %get-tuple-element.62), channel_id=1, source_target_pairs={{0,8},{4,12},{8,0},{12,4},{16,24},{20,28},{24,16},{28,20},{1,9},{5... | collective-permute-start | bytes 786440 | tf_op jit(solution)/shard_map/ppermute | solution.py:27
  36.6 14.8 %collective-permute-start.5 = (bf16[832,128]{1,0:T(8,128)(2,1)S(1)}, bf16[832,128]{1,0:T(8,128)(2,1)S(1)}, u32[]{:S(2)}, u32[]{:S(2)}) collective-permute-start(bf16[832,128]{1,0:T(8,128)(2,1)S(1)} %get-tuple-element.47), channel_id=1, source_target_pairs={{0,1},{1,0},{2,3},{3,2},{4,5},{5,4},{6,7},{7,6},{8,9},{9,8},{10,11... | collective-permute-start | bytes 638984 | tf_op jit(solution)/shard_map/ppermute | solution.py:27
  38.4 13.0 %collective-permute-start.6 = (bf16[832,128]{1,0:T(8,128)(2,1)S(1)}, bf16[832,128]{1,0:T(8,128)(2,1)S(1)}, u32[]{:S(2)}, u32[]{:S(2)}) collective-permute-start(bf16[832,128]{1,0:T(8,128)(2,1)S(1)} %get-tuple-element.48), channel_id=1, source_target_pairs={{0,2},{1,3},{2,0},{3,1},{4,6},{5,7},{6,4},{7,5},{8,10},{9,11},{10,... | collective-permute-start | bytes 638984 | tf_op jit(solution)/shard_map/ppermute | solution.py:27
  39.9 11.5 %collective-permute-start.7 = (bf16[832,128]{1,0:T(8,128)(2,1)S(1)}, bf16[832,128]{1,0:T(8,128)(2,1)S(1)}, u32[]{:S(2)}, u32[]{:S(2)}) collective-permute-start(bf16[832,128]{1,0:T(8,128)(2,1)S(1)} %get-tuple-element.49), channel_id=1, source_target_pairs={{0,3},{1,2},{2,1},{3,0},{4,7},{5,6},{6,5},{7,4},{8,11},{9,10},{10,... | collective-permute-start | bytes 638984 | tf_op jit(solution)/shard_map/ppermute | solution.py:27
  42.6 16.8 %collective-permute-start.10 = (bf16[528,128]{1,0:T(8,128)(2,1)S(1)}, bf16[528,128]{1,0:T(8,128)(2,1)S(1)}, u32[]{:S(2)}, u32[]{:S(2)}) collective-permute-start(bf16[528,128]{1,0:T(8,128)(2,1)S(1)} %get-tuple-element.59), channel_id=1, source_target_pairs={{0,16},{4,20},{8,24},{12,28},{16,0},{20,4},{24,8},{28,12},{1,17},{... | collective-permute-start | bytes 405512 | tf_op jit(solution)/shard_map/ppermute | solution.py:27
  50.7 8.8 %collective-permute-start.16 = (bf16[512,128]{1,0:T(8,128)(2,1)S(1)}, bf16[512,128]{1,0:T(8,128)(2,1)S(1)}, u32[]{:S(2)}, u32[]{:S(2)}) collective-permute-start(bf16[512,128]{1,0:T(8,128)(2,1)S(1)} %get-tuple-element.64), channel_id=1, source_target_pairs={{0,16},{4,20},{8,24},{12,28},{16,0},{20,4},{24,8},{28,12},{1,17},{... | collective-permute-start | bytes 393224 | tf_op jit(solution)/shard_map/ppermute | solution.py:27

commit v6 on v5

--- a/solution.py
+++ b/solution.py
@@ -11,6 +11,7 @@
 
 BF16 = jnp.bfloat16
 SPAN = 512
+FRACTION = 4
 F32 = jnp.float32
 LIMIT = pltpu.CompilerParams(vmem_limit_bytes=32 * 2**20)
 
@@ -69,24 +70,10 @@
         c.wait()
 
 
-def pack_kernel(first_ref, second_ref, first_d, second_d, first_out, second_out):
-    half = first_ref.shape[0] // 2
-    for rows, d_ref, out_ref in (
-        (second_ref[:half], first_d, first_out),
-        (first_ref[half:], second_d, second_out),
-    ):
-        out_ref[:half] = rows
-        count = rows.shape[1] // d_ref.shape[1]
-        high = d_ref.shape[0] // count
-        for c in range(count):
-            lanes = slice(c * d_ref.shape[1], (c + 1) * d_ref.shape[1])
-            out_ref[half:, lanes] = d_ref[c * high : (c + 1) * high]
-
-
-def unpack(ref, half, width):
-    return jnp.concatenate(
-        [ref[half:, at : at + width] for at in range(0, ref.shape[1], width)], axis=0
-    )
+def split_kernel(first_ref, second_ref, top_ref, bottom_ref):
+    half = top_ref.shape[0]
+    top_ref[...] = second_ref[:half]
+    bottom_ref[...] = first_ref[half:]
 
 
 def column_block(ref, rows, index, target):
@@ -123,12 +110,11 @@
 
 
 def attention_kernel(
-    scale, heads, head_size, blocks, sizes, packed, count, target, ids_ref, mask_ref, *refs
+    scale, heads, head_size, blocks, sizes, count, target, first_rows, ids_ref, mask_ref, *refs
 ):
     pieces = len(sizes)
     row_refs, refs = refs[:pieces], refs[pieces:]
-    d_count = blocks - 2 if packed else blocks
-    d_refs, refs = refs[:d_count], refs[d_count:]
+    d_refs, refs = refs[:blocks], refs[blocks:]
     wq_ref, wk_ref, wv_ref, eig_ref, lam_ref, lam_t_ref = refs[:6]
     grads_ref, out_ref, gw_ref, eig_out, give_ref = refs[6:11]
     ret_refs = refs[11:-5]
@@ -160,10 +146,7 @@
     query = fit(mm(rows, wq_ref[...]).astype(BF16))
     keys = fit(mm(rows, wk_ref[...]).astype(BF16))
     values = fit(mm(rows, wv_ref[...]).astype(BF16))
-    d_parts = [r[...] for r in d_refs]
-    if packed:
-        d_parts[1:1] = [unpack(r, n, width) for r, n in zip(row_refs[3:], sizes[3:])]
-    d_att = fit(jnp.concatenate(d_parts, axis=0))
+    d_att = fit(jnp.concatenate([r[...] for r in d_refs], axis=0))
     query_t = (query.astype(F32) * scale).astype(BF16).T
     keys_t = keys.T
     values_t = values.T
@@ -219,6 +202,7 @@
         value = mm(half, dn[head // 2, here, :])
         delta = jnp.sum(prob * dprob, axis=0, keepdims=True)
         dscore = (prob * (dprob - delta)).astype(BF16)
+        right = mm(dscore, qn[head, here, :])
         left = mm(kt, dscore)
         grads_ref[first : first + head_size, here] = (left[:head_size] * scale).astype(BF16)
         weighted = lam_t_ref[:, head : head + 1] * left[head_size:]
@@ -226,7 +210,6 @@
             left_acc[:, here] = weighted
         else:
             left_acc[:, here] += weighted
-        right = mm(dscore, qn[head, here, :])
         if totals is None:
             return right, value
         return totals[0] + right, totals[1] + value
@@ -304,7 +287,7 @@
         part = slice(b * size, (b + 1) * size)
         ret_refs[b][: 3 * width] = grads_ref[:, part]
         ret_refs[b][3 * width :] = eig_sum[:, part].astype(BF16)
-    left = grads_ref[: 2 * width]
+    left = grads_ref[:first_rows]
     span = left.shape[0]
 
     def put(block, row, value):
@@ -393,14 +376,15 @@
         total = own_ref[...]
         for r in piece_refs:
             total += r[:rows].astype(F32)
-        found += [total[at : at + width] for at in range(0, rows, width)]
+        found.append(total)
         if c == 0:
             sums = gw_ref[...]
             for r in piece_refs:
                 sums += get_sums(r, rows, sums.shape)
             gw_out[...] = sums
-    for a, total in enumerate(found):
-        out_ref[a] = total.T
+    total = jnp.concatenate(found, axis=0)
+    for a in range(out_ref.shape[0]):
+        out_ref[a] = total[a * width : (a + 1) * width].T
 
 
 def nodes_kernel(blocks, width, ids_ref, eig_ref, *refs):
@@ -496,23 +480,14 @@
     d_parts, weights = made[:node_size], made[node_size:]
     d_att = [d_parts[0]] + [None] * (node_size - 1)
     for s in far_first:
-        if s < 3 and crossed:
-            continue
         d_att[s] = give(d_parts[s], "node", s, node_size)
     sizes = [size] * node_size
     if crossed:
-        high = size // 2 + size * width // model
-        packed = call(
-            pack_kernel,
-            [vmem] * 4,
-            [((high, model), BF16)] * 2,
-            (rows[1], rows[2], d_parts[1], d_parts[2]),
-            0,
-            2**19,
+        halves = call(
+            split_kernel, [vmem] * 2, [((size // 2, model), BF16)] * 2, (rows[1], rows[2]), 0, 2**19
         )
-        rows[3:] = [give(packed[i], "node", i + 1, node_size) for i in range(2)]
+        rows[3:] = [give(halves[i], "node", i + 1, node_size) for i in range(2)]
         sizes[3:] = [size // 2] * 2
-        d_att = [d_att[0], d_att[3]]
     sizes = tuple(sizes)
     cots = [own_cot] + [None] * (node_size - 1)
     for s in far_first:
@@ -523,6 +498,7 @@
     groups = -(-heads // 2)
     target = model // clus_size
     pairs = rest // 2
+    first_rows = 2 * width + width // FRACTION
     grads_t, out_t, gw_own, eig_own, give_first, *parts = call(
         functools.partial(
             attention_kernel,
@@ -531,9 +507,9 @@
             head_size,
             node_size,
             sizes,
-            crossed,
             rest,
             target,
+            first_rows,
         ),
         [smem, smem] + [vmem] * (len(rows) + len(d_att) + 6),
         [
@@ -541,7 +517,7 @@
             ((width, nodes), BF16),
             ((heads, eig_count), F32),
             ((eig_count, size), F32),
-            ((rest * 2 * width + 16, target), BF16),
+            ((rest * first_rows + 16, target), BF16),
         ]
         + [((3 * width + eig_count, size), BF16)] * node_size,
         (ids, block_mask[0], *rows, *d_att, *weights, eigvec[0], eig_weight, eig_weight.T),
@@ -572,7 +548,7 @@
         )[0]
 
     near_keeps, near_gots = [], []
-    lanes = (0, 2 * width), (2 * width, 3 * width), (0, width)
+    lanes = (0, first_rows), (first_rows, 3 * width), (0, width)
     plan = (
         [(grads_t, lanes[0], rows, sizes)],
         [(grads_t, lanes[1], rows, sizes), (out_t, lanes[2], cots, (size,) * node_size)],

time: 60.7 us -> 64 us (1.054)
  waiting for transfers between devices: 20.5 us -> 23.7 us
  starting transfers between devices: 19.4 us -> 21.9 us
  local copies, waits for them, and re-layouts: 2.02 us -> 0.13 us
    ppermute x17 -> x19, waiting for transfers between devices: 20.5 us -> 23.7 us  [take(): return lax.ppermute(value, axis, pairs)]
    ppermute x17 -> x19, starting transfers between devices: 19.4 us -> 21.9 us  [take(): return lax.ppermute(value, axis, pairs)]
    unnamed x25 -> x17, local copies, waits for them, and re-layouts: 2.02 us -> 0.13 us
  transfers between devices with their start and end apart: 17 -> 19, of which waited for: 7 -> 9; matrix products, arithmetic and copies ran while one was open for 0% -> 0% of each run, Pallas kernels for 27% -> 25%
where the time goes in v6:
time: 64 us; the launch traced here: 63.8 us
  waiting for transfers between devices  23.7 us (37%)
  starting transfers between devices  21.9 us (34%)
  Pallas kernels  17.2 us (27%)
  between operations  0.85 us (1%)
    ppermute x19, waiting for transfers between devices, take(): return lax.ppermute(value, axis, pairs)  23.7 us
    ppermute x19, starting transfers between devices, take(): return lax.ppermute(value, axis, pairs)  21.9 us
    pallas_call x12, Pallas kernels, call_here(): pl.pallas_call(kernel, in_specs=in_specs, out_specs=[vmem] * len(out_shap...  17.2 us
  transfers between devices with their start and end apart: 19, of which 9 were waited for; matrix products, arithmetic and copies ran while one was open for 0% of the time, Pallas kernels for 25%

profile of v6, /device:TPU:0, one launch (start us, length us, event | category | flops | bytes accessed | tf_op | source)
XLA Modules:
  0.0 63.8 jit_solution(14739872547612802999)
XLA Ops:
  0.6 3.0 %collective-permute-start = (bf16[128,1024]{1,0:T(8,128)(2,1)}, bf16[128,1024]{1,0:T(8,128)(2,1)S(1)}, u32[]{:S(2)}, u32[]{:S(2)}) collective-permute-start(bf16[128,1024]{1,0:T(8,128)(2,1)} %bitcast.14), channel_id=1, source_target_pairs={{0,1},{1,0},{2,3},{3,2},{4,5},{5,4},{6,7},{7,6},{8,9},{9,8},{10,11... | collective-permute-start | bytes 786440 | tf_op jit(solution)/shard_map/ppermute | solution.py:28
  3.7 1.5 %collective-permute-start.1 = (bf16[128,1024]{1,0:T(8,128)(2,1)}, bf16[128,1024]{1,0:T(8,128)(2,1)S(1)}, u32[]{:S(2)}, u32[]{:S(2)}) collective-permute-start(bf16[128,1024]{1,0:T(8,128)(2,1)} %bitcast.15), channel_id=1, source_target_pairs={{0,2},{1,3},{2,0},{3,1},{4,6},{5,7},{6,4},{7,5},{8,10},{9,11},{10,... | collective-permute-start | bytes 786440 | tf_op jit(solution)/shard_map/ppermute | solution.py:28
  5.2 5.0 %collective-permute-done.first_ref.refs_1_.refs_2_ = bf16[128,1024]{1,0:T(8,128)(2,1)S(1)} collective-permute-done((bf16[128,1024]{1,0:T(8,128)(2,1)}, bf16[128,1024]{1,0:T(8,128)(2,1)S(1)}, u32[]{:S(2)}, u32[]{:S(2)}) %collective-permute-start) | collective-permute-done | bytes 262176 | tf_op jit(solution)/shard_map/ppermute | solution.py:28
  10.2 1.5 %collective-permute-done.1.second_ref.refs_2_.refs_3_ = bf16[128,1024]{1,0:T(8,128)(2,1)S(1)} collective-permute-done((bf16[128,1024]{1,0:T(8,128)(2,1)}, bf16[128,1024]{1,0:T(8,128)(2,1)S(1)}, u32[]{:S(2)}, u32[]{:S(2)}) %collective-permute-start.1) | collective-permute-done | bytes 262176 | tf_op jit(solution)/shard_map/ppermute | solution.py:28
  11.7 0.4 collective-permute-start.2
  12.1 1.7 %collective-permute-start.3 = (bf16[64,1024]{1,0:T(8,128)(2,1)S(1)}, bf16[64,1024]{1,0:T(8,128)(2,1)S(1)}, u32[]{:S(2)}, u32[]{:S(2)}) collective-permute-start(bf16[64,1024]{1,0:T(8,128)(2,1)S(1)} %get-tuple-element.37), channel_id=1, source_target_pairs={{0,2},{1,3},{2,0},{3,1},{4,6},{5,7},{6,4},{7,5},{8,10},{9,11},{10,... | collective-permute-start | bytes 393224 | tf_op jit(solution)/shard_map/ppermute | solution.py:28
  13.8 0.1 pad_add_fusion.ids_ref
  13.9 0.0 copy-start.4
  13.9 0.0 copy-start.3
  13.9 0.0 copy-start.5
  13.9 0.0 copy-start.7
  13.9 3.5 %shard_map.121 = (bf16[128,256]{1,0:T(8,128)(2,1)S(1)}, bf16[128,256]{1,0:T(8,128)(2,1)}, bf16[128,256]{1,0:T(8,128)(2,1)}, bf16[128,256]{1,0:T(8,128)(2,1)}, bf...) custom-call(s32[12]{0:T(128)S(1)} %pad_add_fusion.ids_ref, ...), custom_call_target="tpu_custom_call" | custom-call | flops 300000000 | bytes 3145728 | tf_op jit(solution)/shard_map/pallas_call | solution.py:444
  17.4 1.6 %collective-permute-start.4 = (bf16[128,256]{1,0:T(8,128)(2,1)}, bf16[128,256]{1,0:T(8,128)(2,1)S(1)}, u32[]{:S(2)}, u32[]{:S(2)}) collective-permute-start(bf16[128,256]{1,0:T(8,128)(2,1)} %get-tuple-element.39), channel_id=1, source_target_pairs={{0,1},{1,0},{2,3},{3,2},{4,5},{5,4},{6,7},{7,6},{8,9},{9,8},{10,11... | collective-permute-start | bytes 196616 | tf_op jit(solution)/shard_map/ppermute | solution.py:28
  19.0 0.5 collective-permute-start.5
  19.5 1.5 %collective-permute-start.6 = (bf16[128,256]{1,0:T(8,128)(2,1)}, bf16[128,256]{1,0:T(8,128)(2,1)S(1)}, u32[]{:S(2)}, u32[]{:S(2)}) collective-permute-start(bf16[128,256]{1,0:T(8,128)(2,1)} %get-tuple-element.41), channel_id=1, source_target_pairs={{0,3},{1,2},{2,1},{3,0},{4,7},{5,6},{6,5},{7,4},{8,11},{9,10},{10,... | collective-permute-start | bytes 196616 | tf_op jit(solution)/shard_map/ppermute | solution.py:28
  21.0 0.0 copy-done.4
  21.0 0.1 copy.13
  21.1 1.6 %collective-permute-done.4.refs_6_ = bf16[128,256]{1,0:T(8,128)(2,1)S(1)} collective-permute-done((bf16[128,256]{1,0:T(8,128)(2,1)}, bf16[128,256]{1,0:T(8,128)(2,1)S(1)}, u32[]{:S(2)}, u32[]{:S(2)}) %collective-permute-start.4) | collective-permute-done | bytes 65568 | tf_op jit(solution)/shard_map/ppermute | solution.py:28
  22.7 0.0 copy-done.3
  22.7 1.2 %collective-permute-start.13 = (bf16[128,1024]{1,0:T(8,128)(2,1)S(1)}, bf16[128,1024]{1,0:T(8,128)(2,1)S(1)}, u32[]{:S(2)}, u32[]{:S(2)}) collective-permute-start(bf16[128,1024]{1,0:T(8,128)(2,1)S(1)} %bitcast.8), channel_id=1, source_target_pairs={{0,1},{1,0},{2,3},{3,2},{4,5},{5,4},{6,7},{7,6},{8,9},{9,8},{10,11... | collective-permute-start | bytes 786440 | tf_op jit(solution)/shard_map/ppermute | solution.py:28
  23.9 0.3 collective-permute-done.5.refs_7_
  24.1 0.5 collective-permute-start.14
  24.7 0.9 %collective-permute-done.6.refs_8_ = bf16[128,256]{1,0:T(8,128)(2,1)S(1)} collective-permute-done((bf16[128,256]{1,0:T(8,128)(2,1)}, bf16[128,256]{1,0:T(8,128)(2,1)S(1)}, u32[]{:S(2)}, u32[]{:S(2)}) %collective-permute-start.6) | collective-permute-done | bytes 65568 | tf_op jit(solution)/shard_map/ppermute | solution.py:28
  25.6 1.5 %collective-permute-start.15 = (bf16[128,1024]{1,0:T(8,128)(2,1)S(1)}, bf16[128,1024]{1,0:T(8,128)(2,1)S(1)}, u32[]{:S(2)}, u32[]{:S(2)}) collective-permute-start(bf16[128,1024]{1,0:T(8,128)(2,1)S(1)} %bitcast.10), channel_id=1, source_target_pairs={{0,3},{1,2},{2,1},{3,0},{4,7},{5,6},{6,5},{7,4},{8,11},{9,10},{10,... | collective-permute-start | bytes 786440 | tf_op jit(solution)/shard_map/ppermute | solution.py:28
  27.1 0.0 collective-permute-done.2.refs_3_.refs_4_
  27.1 0.0 collective-permute-done.3.refs_4_.refs_5_
  27.1 0.0 copy-done.5
  27.1 0.0 copy-done.6
  27.1 0.0 copy-done.7
  27.1 5.9 %shard_map.122 = (bf16[768,512]{1,0:T(8,128)(2,1)S(1)}, bf16[256,512]{1,0:T(8,128)(2,1)S(1)}, f32[4,64]{1,0:T(4,128)S(1)}, f32[64,128]{1,0:T(8,128)S(1)}, bf16[2...) custom-call(s32[12]{0:T(128)S(1)} %pad_add_fusion.ids_ref, ...), custom_call_target="tpu_custom_call" | custom-call | flops 8000000000 | bytes 8388608 | tf_op jit(solution)/shard_map/pallas_call | solution.py:444
  33.0 0.1 collective-permute-start.10
  33.0 0.0 collective-permute-done.13.refs_8_
  33.1 2.4 %collective-permute-done.14.refs_9_ = bf16[128,1024]{1,0:T(8,128)(2,1)S(1)} collective-permute-done((bf16[128,1024]{1,0:T(8,128)(2,1)S(1)}, bf16[128,1024]{1,0:T(8,128)(2,1)S(1)}, u32[]{:S(2)}, u32[]{:S(2)}) %collective-permute-start.14) | collective-permute-done | bytes 262176 | tf_op jit(solution)/shard_map/ppermute | solution.py:28
  35.4 0.0 collective-permute-done.15.refs_10_
  35.4 1.1 %shard_map.128 = bf16[1792,128]{1,0:T(8,128)(2,1)S(1)} custom-call(s32[12]{0:T(128)S(1)} %pad_add_fusion.ids_ref, bf16[768,512]{1,0:T(8,128)(2,1)S(1)} %get-tuple-element.52.refs_0_, bf16[128,1024]{1,0:T(8,128)(2,1)S(1)} %bitcast.17, bf16[128,1024]{1,0:T(8,128)(2,1)S(1)} %collective-permute-done.first_ref.refs_1_.refs_2_, ...), custom_call_target="tpu_custom_call" | custom-call | flops 1000000000 | bytes 1048576 | tf_op jit(solution)/shard_map/pallas_call | solution.py:444
  36.5 0.1 collective-permute-start.16
  36.5 1.1 %shard_map.124.keep_ref = bf16[4,576,128]{2,1,0:T(8,128)(2,1)S(1)} custom-call(s32[12]{0:T(128)S(1)} %pad_add_fusion.ids_ref, bf16[768,512]{1,0:T(8,128)(2,1)S(1)} %get-tuple-element.52.refs_0_, bf16[128,1024]{1,0:T(8,128)(2,1)S(1)} %bitcast.18, bf16[128,1024]{1,0:T(8,128)(2,1)S(1)} %collective-permute-done.first_ref.refs_1_.refs_2_, ...), custom_call_target="tpu_custom_call" | custom-call | flops 1000000000 | bytes 1048576 | tf_op jit(solution)/shard_map/pallas_call | solution.py:444
  37.6 0.0 collective-permute-done.10.got_ref
  37.6 0.0 copy-start.2
  37.6 0.2 shard_map.125
  37.8 1.6 %collective-permute-start.11 = (bf16[1168,128]{1,0:T(8,128)(2,1)S(1)}, bf16[1168,128]{1,0:T(8,128)(2,1)S(1)}, u32[]{:S(2)}, u32[]{:S(2)}) collective-permute-start(bf16[1168,128]{1,0:T(8,128)(2,1)S(1)} %get-tuple-element.56), channel_id=1, source_target_pairs={{0,8},{4,12},{8,0},{12,4},{16,24},{20,28},{24,16},{28,20},{1,9},{5... | collective-permute-start | bytes 897032 | tf_op jit(solution)/shard_map/ppermute | solution.py:28
  39.4 1.0 %shard_map.127.keep_ref = bf16[4,448,128]{2,1,0:T(8,128)(2,1)S(1)} custom-call(s32[12]{0:T(128)S(1)} %pad_add_fusion.ids_ref, bf16[768,512]{1,0:T(8,128)(2,1)S(1)} %get-tuple-element.52.refs_0_, bf16[128,1024]{1,0:T(8,128)(2,1)S(1)} %bitcast.19, bf16[128,1024]{1,0:T(8,128)(2,1)S(1)} %collective-permute-done.first_ref.refs_1_.refs_2_, ...), custom_call_target="tpu_custom_call" | custom-call | flops 1000000000 | bytes 1048576 | tf_op jit(solution)/shard_map/pallas_call | solution.py:444
  40.5 0.0 copy-start
  40.5 0.0 collective-permute-done.16.got_ref
  40.5 0.1 shard_map.129
  40.6 0.5 collective-permute-start.17
  41.1 0.5 collective-permute-start.7
  41.7 0.9 %collective-permute-start.8 = (bf16[832,128]{1,0:T(8,128)(2,1)S(1)}, bf16[832,128]{1,0:T(8,128)(2,1)S(1)}, u32[]{:S(2)}, u32[]{:S(2)}) collective-permute-start(bf16[832,128]{1,0:T(8,128)(2,1)S(1)} %get-tuple-element.48), channel_id=1, source_target_pairs={{0,2},{1,3},{2,0},{3,1},{4,6},{5,7},{6,4},{7,5},{8,10},{9,11},{10,... | collective-permute-start | bytes 638984 | tf_op jit(solution)/shard_map/ppermute | solution.py:28
  42.6 2.0 %collective-permute-start.9 = (bf16[832,128]{1,0:T(8,128)(2,1)S(1)}, bf16[832,128]{1,0:T(8,128)(2,1)S(1)}, u32[]{:S(2)}, u32[]{:S(2)}) collective-permute-start(bf16[832,128]{1,0:T(8,128)(2,1)S(1)} %get-tuple-element.49), channel_id=1, source_target_pairs={{0,3},{1,2},{2,1},{3,0},{4,7},{5,6},{6,5},{7,4},{8,11},{9,10},{10,... | collective-permute-start | bytes 638984 | tf_op jit(solution)/shard_map/ppermute | solution.py:28
  44.6 3.2 %collective-permute-done.11.got_ref = bf16[1168,128]{1,0:T(8,128)(2,1)S(1)} collective-permute-done((bf16[1168,128]{1,0:T(8,128)(2,1)S(1)}, bf16[1168,128]{1,0:T(8,128)(2,1)S(1)}, u32[]{:S(2)}, u32[]{:S(2)}) %collective-permute-start.11) | collective-permute-done | bytes 299040 | tf_op jit(solution)/shard_map/ppermute | solution.py:28
  47.8 0.1 shard_map.126
  47.9 2.7 %collective-permute-start.12 = (bf16[592,128]{1,0:T(8,128)(2,1)S(1)}, bf16[592,128]{1,0:T(8,128)(2,1)S(1)}, u32[]{:S(2)}, u32[]{:S(2)}) collective-permute-start(bf16[592,128]{1,0:T(8,128)(2,1)S(1)} %get-tuple-element.59), channel_id=1, source_target_pairs={{0,16},{4,20},{8,24},{12,28},{16,0},{20,4},{24,8},{28,12},{1,17},{... | collective-permute-start | bytes 454664 | tf_op jit(solution)/shard_map/ppermute | solution.py:28
  50.6 5.0 %collective-permute-done.17.got_ref = bf16[896,128]{1,0:T(8,128)(2,1)S(1)} collective-permute-done((bf16[896,128]{1,0:T(8,128)(2,1)S(1)}, bf16[896,128]{1,0:T(8,128)(2,1)S(1)}, u32[]{:S(2)}, u32[]{:S(2)}) %collective-permute-start.17) | collective-permute-done | bytes 229408 | tf_op jit(solution)/shard_map/ppermute | solution.py:28
  55.6 0.1 collective-permute-start.18
  55.7 0.0 collective-permute-done.7.refs_1_
  55.7 0.0 collective-permute-done.8.refs_2_
  55.7 0.0 collective-permute-done.9.refs_3_
  55.7 0.0 copy-done.2
  55.7 0.0 copy-done.1
  55.7 0.0 copy-done
  55.7 3.2 %shard_map.123 = (bf16[128,1024]{1,0:T(8,128)(2,1)}, f32[64,128]{1,0:T(8,128)}) custom-call(s32[12]{0:T(128)S(1)} %pad_add_fusion.ids_ref, f32[64,128]{1,0:T(8,128)S(1)} %get-tuple-element.45.eig_ref, bf16[832,128]{1,0:T(8,128)(2,1)S(1)} %get-tuple-element.46.refs_0_, bf16[832,128]{1,0:T(8,128)(2,1)S(1)} %collective-permute-done.7.refs_1_, ...), custom_call_target="tpu_custom_call" | custom-call | flops 1000000000 | bytes 7340032 | tf_op jit(solution)/shard_map/pallas_call | solution.py:444
  58.9 3.9 %collective-permute-done.18.refs_3_ = bf16[448,128]{1,0:T(8,128)(2,1)S(1)} collective-permute-done((bf16[448,128]{1,0:T(8,128)(2,1)S(1)}, bf16[448,128]{1,0:T(8,128)(2,1)S(1)}, u32[]{:S(2)}, u32[]{:S(2)}) %collective-permute-start.18) | collective-permute-done | bytes 114720 | tf_op jit(solution)/shard_map/ppermute | solution.py:28
  62.8 0.0 collective-permute-done.12.refs_1_
  62.8 1.0 %shard_map.131 = (f32[4,128,256]{2,1,0:T(8,128)}, f32[4,64]{1,0:T(4,128)}) custom-call(f32[576,128]{1,0:T(8,128)S(1)} %get-tuple-element.58.refs_0_, bf16[592,128]{1,0:T(8,128)(2,1)S(1)} %collective-permute-done.12.refs_1_, f32[448,128]{1,0:T(8,128)S(1)} %get-tuple-element.63.refs_2_, bf16[448,128]{1,0:T(8,128)(2,1)S(1)} %collective-permute-done.18.refs_3_, ...), custom_call_target="tpu_custom_call" | custom-call | flops 1000000 | bytes 2097152 | tf_op jit(solution)/shard_map/pallas_call | solution.py:444
  (6 shorter events, 0.1 us)
Async XLA Ops:
  0.6 9.6 %collective-permute-start = (bf16[128,1024]{1,0:T(8,128)(2,1)}, bf16[128,1024]{1,0:T(8,128)(2,1)S(1)}, u32[]{:S(2)}, u32[]{:S(2)}) collective-permute-start(bf16[128,1024]{1,0:T(8,128)(2,1)} %bitcast.14), channel_id=1, source_target_pairs={{0,1},{1,0},{2,3},{3,2},{4,5},{5,4},{6,7},{7,6},{8,9},{9,8},{10,11... | collective-permute-start | bytes 786440 | tf_op jit(solution)/shard_map/ppermute | solution.py:28
  3.7 8.0 %collective-permute-start.1 = (bf16[128,1024]{1,0:T(8,128)(2,1)}, bf16[128,1024]{1,0:T(8,128)(2,1)S(1)}, u32[]{:S(2)}, u32[]{:S(2)}) collective-permute-start(bf16[128,1024]{1,0:T(8,128)(2,1)} %bitcast.15), channel_id=1, source_target_pairs={{0,2},{1,3},{2,0},{3,1},{4,6},{5,7},{6,4},{7,5},{8,10},{9,11},{10,... | collective-permute-start | bytes 786440 | tf_op jit(solution)/shard_map/ppermute | solution.py:28
  11.7 15.4 %collective-permute-start.2 = (bf16[64,1024]{1,0:T(8,128)(2,1)S(1)}, bf16[64,1024]{1,0:T(8,128)(2,1)S(1)}, u32[]{:S(2)}, u32[]{:S(2)}) collective-permute-start(bf16[64,1024]{1,0:T(8,128)(2,1)S(1)} %get-tuple-element.36), channel_id=1, source_target_pairs={{0,1},{1,0},{2,3},{3,2},{4,5},{5,4},{6,7},{7,6},{8,9},{9,8},{10,11... | collective-permute-start | bytes 393224 | tf_op jit(solution)/shard_map/ppermute | solution.py:28
  12.1 15.0 %collective-permute-start.3 = (bf16[64,1024]{1,0:T(8,128)(2,1)S(1)}, bf16[64,1024]{1,0:T(8,128)(2,1)S(1)}, u32[]{:S(2)}, u32[]{:S(2)}) collective-permute-start(bf16[64,1024]{1,0:T(8,128)(2,1)S(1)} %get-tuple-element.37), channel_id=1, source_target_pairs={{0,2},{1,3},{2,0},{3,1},{4,6},{5,7},{6,4},{7,5},{8,10},{9,11},{10,... | collective-permute-start | bytes 393224 | tf_op jit(solution)/shard_map/ppermute | solution.py:28
  13.9 7.1 %copy-start.4 = (f32[4,64]{1,0:T(4,128)S(1)}, f32[4,64]{1,0:T(4,128)}, u32[]{:S(2)}) copy-start(f32[4,64]{1,0:T(4,128)} %refs_13_.1) | copy-start | bytes 3076
  13.9 8.8 %copy-start.3 = (bf16[1,128,1024]{2,1,0:T(8,128)(2,1)S(1)}, bf16[1,128,1024]{2,1,0:T(8,128)(2,1)}, u32[]{:S(2)}) copy-start(bf16[1,128,1024]{2,1,0:T(8,128)(2,1)} %param.10) | copy-start | bytes 786436
  13.9 13.2 %copy-start.5 = (bf16[1,128,1024]{2,1,0:T(8,128)(2,1)S(1)}, bf16[1,128,1024]{2,1,0:T(8,128)(2,1)}, u32[]{:S(2)}) copy-start(bf16[1,128,1024]{2,1,0:T(8,128)(2,1)} %param.9) | copy-start | bytes 786436
  13.9 13.2 %copy-start.6 = (bf16[1,64,512]{2,1,0:T(8,128)(2,1)S(1)}, bf16[1,64,512]{2,1,0:T(8,128)(2,1)}, u32[]{:S(2)}) copy-start(bf16[1,64,512]{2,1,0:T(8,128)(2,1)} %param.15) | copy-start | bytes 196612
  13.9 13.2 %copy-start.7 = (s32[1,4,4,4]{3,2,1,0:T(4,128)S(1)}, s32[1,4,4,4]{3,2,1,0:T(4,128)}, u32[]{:S(2)}) copy-start(s32[1,4,4,4]{3,2,1,0:T(4,128)} %param.17) | copy-start | bytes 772
  17.4 5.2 %collective-permute-start.4 = (bf16[128,256]{1,0:T(8,128)(2,1)}, bf16[128,256]{1,0:T(8,128)(2,1)S(1)}, u32[]{:S(2)}, u32[]{:S(2)}) collective-permute-start(bf16[128,256]{1,0:T(8,128)(2,1)} %get-tuple-element.39), channel_id=1, source_target_pairs={{0,1},{1,0},{2,3},{3,2},{4,5},{5,4},{6,7},{7,6},{8,9},{9,8},{10,11... | collective-permute-start | bytes 196616 | tf_op jit(solution)/shard_map/ppermute | solution.py:28
  19.0 5.2 %collective-permute-start.5 = (bf16[128,256]{1,0:T(8,128)(2,1)}, bf16[128,256]{1,0:T(8,128)(2,1)S(1)}, u32[]{:S(2)}, u32[]{:S(2)}) collective-permute-start(bf16[128,256]{1,0:T(8,128)(2,1)} %get-tuple-element.40), channel_id=1, source_target_pairs={{0,2},{1,3},{2,0},{3,1},{4,6},{5,7},{6,4},{7,5},{8,10},{9,11},{10,... | collective-permute-start | bytes 196616 | tf_op jit(solution)/shard_map/ppermute | solution.py:28
  19.5 6.1 %collective-permute-start.6 = (bf16[128,256]{1,0:T(8,128)(2,1)}, bf16[128,256]{1,0:T(8,128)(2,1)S(1)}, u32[]{:S(2)}, u32[]{:S(2)}) collective-permute-start(bf16[128,256]{1,0:T(8,128)(2,1)} %get-tuple-element.41), channel_id=1, source_target_pairs={{0,3},{1,2},{2,1},{3,0},{4,7},{5,6},{6,5},{7,4},{8,11},{9,10},{10,... | collective-permute-start | bytes 196616 | tf_op jit(solution)/shard_map/ppermute | solution.py:28
  22.7 10.4 %collective-permute-start.13 = (bf16[128,1024]{1,0:T(8,128)(2,1)S(1)}, bf16[128,1024]{1,0:T(8,128)(2,1)S(1)}, u32[]{:S(2)}, u32[]{:S(2)}) collective-permute-start(bf16[128,1024]{1,0:T(8,128)(2,1)S(1)} %bitcast.8), channel_id=1, source_target_pairs={{0,1},{1,0},{2,3},{3,2},{4,5},{5,4},{6,7},{7,6},{8,9},{9,8},{10,11... | collective-permute-start | bytes 786440 | tf_op jit(solution)/shard_map/ppermute | solution.py:28
  24.1 11.3 %collective-permute-start.14 = (bf16[128,1024]{1,0:T(8,128)(2,1)S(1)}, bf16[128,1024]{1,0:T(8,128)(2,1)S(1)}, u32[]{:S(2)}, u32[]{:S(2)}) collective-permute-start(bf16[128,1024]{1,0:T(8,128)(2,1)S(1)} %bitcast.9), channel_id=1, source_target_pairs={{0,2},{1,3},{2,0},{3,1},{4,6},{5,7},{6,4},{7,5},{8,10},{9,11},{10,... | collective-permute-start | bytes 786440 | tf_op jit(solution)/shard_map/ppermute | solution.py:28
  25.6 9.8 %collective-permute-start.15 = (bf16[128,1024]{1,0:T(8,128)(2,1)S(1)}, bf16[128,1024]{1,0:T(8,128)(2,1)S(1)}, u32[]{:S(2)}, u32[]{:S(2)}) collective-permute-start(bf16[128,1024]{1,0:T(8,128)(2,1)S(1)} %bitcast.10), channel_id=1, source_target_pairs={{0,3},{1,2},{2,1},{3,0},{4,7},{5,6},{6,5},{7,4},{8,11},{9,10},{10,... | collective-permute-start | bytes 786440 | tf_op jit(solution)/shard_map/ppermute | solution.py:28
  33.0 4.7 %collective-permute-start.10 = (bf16[2320,128]{1,0:T(8,128)(2,1)S(1)}, bf16[2320,128]{1,0:T(8,128)(2,1)S(1)}, u32[]{:S(2)}, u32[]{:S(2)}) collective-permute-start(bf16[2320,128]{1,0:T(8,128)(2,1)S(1)} %get-tuple-element.53), channel_id=1, source_target_pairs={{0,4},{4,0},{8,12},{12,8},{16,20},{20,16},{24,28},{28,24},{1,5},{5... | collective-permute-start | bytes 1781768 | tf_op jit(solution)/shard_map/ppermute | solution.py:28
  36.5 4.0 %collective-permute-start.16 = (bf16[1792,128]{1,0:T(8,128)(2,1)S(1)}, bf16[1792,128]{1,0:T(8,128)(2,1)S(1)}, u32[]{:S(2)}, u32[]{:S(2)}) collective-permute-start(bf16[1792,128]{1,0:T(8,128)(2,1)S(1)} %shard_map.128), channel_id=1, source_target_pairs={{0,4},{4,0},{8,12},{12,8},{16,20},{20,16},{24,28},{28,24},{1,5},{5... | collective-permute-start | bytes 1376264 | tf_op jit(solution)/shard_map/ppermute | solution.py:28
  37.6 18.1 %copy-start.2 = (bf16[1024,1024]{1,0:T(8,128)(2,1)S(1)}, bf16[1024,1024]{1,0:T(8,128)(2,1)}, u32[]{:S(2)}) copy-start(bf16[1024,1024]{1,0:T(8,128)(2,1)} %refs_6_.1) | copy-start | bytes 6291460
  37.8 10.0 %collective-permute-start.11 = (bf16[1168,128]{1,0:T(8,128)(2,1)S(1)}, bf16[1168,128]{1,0:T(8,128)(2,1)S(1)}, u32[]{:S(2)}, u32[]{:S(2)}) collective-permute-start(bf16[1168,128]{1,0:T(8,128)(2,1)S(1)} %get-tuple-element.56), channel_id=1, source_target_pairs={{0,8},{4,12},{8,0},{12,4},{16,24},{20,28},{24,16},{28,20},{1,9},{5... | collective-permute-start | bytes 897032 | tf_op jit(solution)/shard_map/ppermute | solution.py:28
  39.4 16.3 %copy-start.1 = (bf16[1024,1024]{1,0:T(8,128)(2,1)S(1)}, bf16[1024,1024]{1,0:T(8,128)(2,1)}, u32[]{:S(2)}) copy-start(bf16[1024,1024]{1,0:T(8,128)(2,1)} %refs_5_.1) | copy-start | bytes 6291460
  40.5 15.2 %copy-start = (bf16[1024,1024]{1,0:T(8,128)(2,1)S(1)}, bf16[1024,1024]{1,0:T(8,128)(2,1)}, u32[]{:S(2)}) copy-start(bf16[1024,1024]{1,0:T(8,128)(2,1)} %refs_4_.1) | copy-start | bytes 6291460
  40.6 14.9 %collective-permute-start.17 = (bf16[896,128]{1,0:T(8,128)(2,1)S(1)}, bf16[896,128]{1,0:T(8,128)(2,1)S(1)}, u32[]{:S(2)}, u32[]{:S(2)}) collective-permute-start(bf16[896,128]{1,0:T(8,128)(2,1)S(1)} %get-tuple-element.62), channel_id=1, source_target_pairs={{0,8},{4,12},{8,0},{12,4},{16,24},{20,28},{24,16},{28,20},{1,9},{5... | collective-permute-start | bytes 688136 | tf_op jit(solution)/shard_map/ppermute | solution.py:28
  41.1 14.5 %collective-permute-start.7 = (bf16[832,128]{1,0:T(8,128)(2,1)S(1)}, bf16[832,128]{1,0:T(8,128)(2,1)S(1)}, u32[]{:S(2)}, u32[]{:S(2)}) collective-permute-start(bf16[832,128]{1,0:T(8,128)(2,1)S(1)} %get-tuple-element.47), channel_id=1, source_target_pairs={{0,1},{1,0},{2,3},{3,2},{4,5},{5,4},{6,7},{7,6},{8,9},{9,8},{10,11... | collective-permute-start | bytes 638984 | tf_op jit(solution)/shard_map/ppermute | solution.py:28
  41.7 14.0 %collective-permute-start.8 = (bf16[832,128]{1,0:T(8,128)(2,1)S(1)}, bf16[832,128]{1,0:T(8,128)(2,1)S(1)}, u32[]{:S(2)}, u32[]{:S(2)}) collective-permute-start(bf16[832,128]{1,0:T(8,128)(2,1)S(1)} %get-tuple-element.48), channel_id=1, source_target_pairs={{0,2},{1,3},{2,0},{3,1},{4,6},{5,7},{6,4},{7,5},{8,10},{9,11},{10,... | collective-permute-start | bytes 638984 | tf_op jit(solution)/shard_map/ppermute | solution.py:28
  42.6 13.1 %collective-permute-start.9 = (bf16[832,128]{1,0:T(8,128)(2,1)S(1)}, bf16[832,128]{1,0:T(8,128)(2,1)S(1)}, u32[]{:S(2)}, u32[]{:S(2)}) collective-permute-start(bf16[832,128]{1,0:T(8,128)(2,1)S(1)} %get-tuple-element.49), channel_id=1, source_target_pairs={{0,3},{1,2},{2,1},{3,0},{4,7},{5,6},{6,5},{7,4},{8,11},{9,10},{10,... | collective-permute-start | bytes 638984 | tf_op jit(solution)/shard_map/ppermute | solution.py:28
  47.9 14.9 %collective-permute-start.12 = (bf16[592,128]{1,0:T(8,128)(2,1)S(1)}, bf16[592,128]{1,0:T(8,128)(2,1)S(1)}, u32[]{:S(2)}, u32[]{:S(2)}) collective-permute-start(bf16[592,128]{1,0:T(8,128)(2,1)S(1)} %get-tuple-element.59), channel_id=1, source_target_pairs={{0,16},{4,20},{8,24},{12,28},{16,0},{20,4},{24,8},{28,12},{1,17},{... | collective-permute-start | bytes 454664 | tf_op jit(solution)/shard_map/ppermute | solution.py:28
  55.6 7.2 %collective-permute-start.18 = (bf16[448,128]{1,0:T(8,128)(2,1)S(1)}, bf16[448,128]{1,0:T(8,128)(2,1)S(1)}, u32[]{:S(2)}, u32[]{:S(2)}) collective-permute-start(bf16[448,128]{1,0:T(8,128)(2,1)S(1)} %get-tuple-element.64), channel_id=1, source_target_pairs={{0,16},{4,20},{8,24},{12,28},{16,0},{20,4},{24,8},{28,12},{1,17},{... | collective-permute-start | bytes 344072 | tf_op jit(solution)/shard_map/ppermute | solution.py:28
